TPU v7x, 512 devices: a whole 4x4x16 slice. The times are simulated.
512 devices in a mesh: pix: 32 (over z, core), tm: 16 (over y, x).
Axes of the slice: x: 4, y: 4, z: 16, core: 2. Of those that a mesh axis runs over, the one named last changes fastest.
Arguments:
- raw_frames: bfloat16 [1024, 262144], P('tm', 'pix'), may hold values from 0.099609375 to 4
- eigen_flats: bfloat16 [16, 262144], P(None, 'pix'), may hold values from 0 to 1
- weights: float32 [1024, 16], P('tm'), may hold values from 0.02 to 1
- flat_count: int32 [1024], P('tm'), may hold values from 1 to 16
- bin_map: int32 [262144], P('pix'), may hold values from 0 to 64, as said below
Outputs:
- two_time: float32 [64, 1024, 1024], P('pix', 'tm')
Inputs may be any that keep to these rules, and one draw needn't show every extreme that they name: `bin_map`: each block of 8192 pixels (one device's tile) holds 60 to 96 pixels of every bin 1 to 64; in every draw one bin holds exactly 96 pixels in every tile.
All inputs are finite; a program needn't handle non-finite values.
Results may differ from a plain program's by a relative error of at most 0.0003.
Values may be sent and summed in bfloat16 or wider, within the bound.
No kernel may reach another device: no remote copies, remote signals or barrier semaphores. Data moves between devices by JAX's collectives and lax.ppermute only.
A program may use at most 64 MiB of HBM per device.

v0:
```python
import jax
import jax.numpy as jnp
from jax import lax
from jax.sharding import PartitionSpec as P

CAP = 96
BIN_DEV = 2


def bin_block(own_frames, local_sums, pixel_counts, portion):
    products = jnp.einsum("tsbc,usbc->btu", own_frames, portion, preferred_element_type=jnp.float32)
    other_sums = jnp.transpose(jnp.sum(portion, axis=(1, 3), dtype=jnp.float32))
    scaled = pixel_counts[:, None, None] * products
    return scaled / (local_sums[:, :, None] * other_sums[:, None, :])


def shards(raw_frames, eigen_flats, weights, flat_count, bin_map):
    frames, pixels = raw_frames.shape
    eigen_count = eigen_flats.shape[0]
    in_use = lax.broadcasted_iota(jnp.int32, (frames, eigen_count), 1) < flat_count[:, None]
    coefficients = jnp.where(in_use, weights, 0.0)
    flat_field = 0.5 + jnp.dot(
        coefficients, eigen_flats.astype(jnp.float32), precision=lax.Precision.HIGHEST
    )
    corrected = (raw_frames.astype(jnp.float32) / flat_field).astype(jnp.bfloat16)
    owners = lax.axis_size("pix")
    bin_total = BIN_DEV * owners
    labels = jnp.where(bin_map > 0, bin_map - 1, bin_total)
    ordering = jnp.argsort(labels * pixels + jnp.arange(pixels, dtype=jnp.int32))
    member = labels[:, None] == jnp.arange(bin_total, dtype=jnp.int32)[None, :]
    counts = jnp.sum(member, axis=0, dtype=jnp.int32)
    starts = jnp.cumsum(counts) - counts
    slot_index = jnp.arange(CAP, dtype=jnp.int32)
    filled = slot_index[None, :] < counts[:, None]
    source = ordering[jnp.minimum(starts[:, None] + slot_index[None, :], pixels - 1)]
    packed = jnp.where(
        filled.reshape(-1)[None, :], corrected[:, source.reshape(-1)], jnp.zeros((), jnp.bfloat16)
    )
    tallies = counts.astype(jnp.bfloat16)[None, :]
    received, tally_in = (
        lax.all_to_all(packed, "pix", split_axis=1, concat_axis=1, tiled=True),
        lax.all_to_all(tallies, "pix", split_axis=1, concat_axis=1, tiled=True),
    )
    own_frames = received.reshape(frames, owners, BIN_DEV, CAP)
    pixel_counts = jnp.sum(tally_in.astype(jnp.float32).reshape(owners, BIN_DEV), axis=0)
    local_sums = jnp.transpose(jnp.sum(own_frames, axis=(1, 3), dtype=jnp.float32))
    return bin_block(
        own_frames, local_sums, pixel_counts, lax.all_gather(own_frames, "tm", axis=0, tiled=True)
    )


def solution(mesh):
    return jax.shard_map(
        shards,
        mesh=mesh,
        in_specs=(P("tm", "pix"), P(None, "pix"), P("tm", None), P("tm"), P("pix")),
        out_specs=P("pix", "tm", None),
        check_vma=False,
    )
```

profile of v0, /device:TPU:1, one launch (start us, length us, event | category | flops | bytes accessed | tf_op | source)
XLA Modules:
  0.0 294.0 jit_solution(1987480666871033830)
XLA Ops:
  6.6 0.8 add_select_fusion
  7.4 0.3 convert_reduce_fusion.2
  7.7 0.1 lt.61
  7.8 0.1 lt.62
  8.0 0.1 copy.28
  8.1 0.1 reduce-window.8
  8.2 0.1 reduce.3
  8.5 6.8 %sort.17 = (s32[8192]{0:T(1024)}, s32[8192]{0:T(1024)S(1)}) sort(s32[8192]{0:T(1024)S(1)} %get-tuple-element.8, s32[8192]{0:T(1024)S(1)} %iota.25), dimensions={0}, to_apply=%region_2.3 | sort | flops 106496 | bytes 131072 | tf_op jit(solution)/shard_map/jit(argsort)/sort | solution.py:29
  15.3 34.3 %gather_fusion = s32[6144]{0:T(1024)S(1)} fusion(s32[8192]{0:T(1024)S(1)} %get-tuple-element.6, s32[6144]{0:T(1024)S(1)} %broadcast_clamp_fusion), kind=kCustom, calls=%fused_computation | custom fusion | bytes 73728 | tf_op jit(solution)/shard_map/gather | solution.py:35
  49.7 1.2 fusion.1
  50.9 1.1 copy.29
  52.0 22.1 %gather_fusion.1 = bf16[6144,64]{1,0:T(8,128)(2,1)} fusion(bf16[64,8192]{0,1:T(8,128)(2,1)S(1)} %copy.29, s32[6144]{0:T(1024)S(1)} %broadcast_clamp_fusion.1), kind=kCustom, calls=%fused_computation.1 | custom fusion | bytes 1597440 | tf_op jit(solution)/shard_map/gather | solution.py:37
  74.0 1.8 copy.30
  75.9 72.2 %all_to_all.12 = bf16[64,32,192]{2,0,1:T(8,128)(2,1)S(1)} all-to-all(bf16[64,32,192]{2,0,1:T(8,128)(2,1)S(1)} %broadcast_select_fusion), channel_id=1, replica_groups=mesh['pix'=32,'tm'=16] {'pix'}, dimensions={1} | all-to-all | bytes 1572864 | tf_op jit(solution)/shard_map/all_to_all | solution.py:41
  148.2 0.6 reshape.176
  148.8 1.3 copy.33
  150.1 0.1 convert_element_type.46
  150.2 15.1 %all_to_all.13 = bf16[1,32,2]{2,0,1:T(2,128)(2,1)S(1)} all-to-all(bf16[1,32,2]{2,0,1:T(2,128)(2,1)S(1)} %convert_element_type.46), channel_id=1, replica_groups=mesh['pix'=32,'tm'=16] {'pix'}, dimensions={1} | all-to-all | bytes 256 | tf_op jit(solution)/shard_map/all_to_all | solution.py:42
  165.3 0.2 convert_reduce_fusion.1
  165.5 0.1 reduce_sum.46
  165.6 0.1 reduce_sum.47
  165.8 102.4 %all-gather.2.cloned.1.call-done = bf16[1024,32,2,96]{3,0,1,2:T(8,128)(2,1)} async-done(((bf16[64,32,2,96]{3,0,1,2:T(8,128)(2,1)}), bf16[1024,32,2,96]{3,0,1,2:T(8,128)(2,1)}) %all-gather.2.cloned.1.call-update) | async-done | bytes 12582928 | tf_op jit(solution)/shard_map/all_gather | solution.py:48
  268.2 7.2 %convert_reduce_fusion = f32[1024,2]{0,1:T(2,128)S(1)} fusion(bf16[1024,32,2,96]{3,0,1,2:T(8,128)(2,1)} %all-gather.2.cloned.1.call-done), kind=kLoop, calls=%fused_computation.2 | loop fusion | flops 12580864 | bytes 12591104 | tf_op jit(solution)/shard_map/reduce_sum | solution.py:12
  275.5 11.7 %fusion.3 = f32[2,64,1024]{2,1,0:T(8,128)} fusion(bf16[1024,32,2,96]{3,0,1,2:T(8,128)(2,1)} %all-gather.2.cloned.1.call-done, f32[2,1024]{1,0:T(2,128)S(1)} %bitcast.24, f32[2,64]{1,0:T(2,128)S(1)} %bitcast.25, f32[2]{0:T(128)S(1)} %convert_reduce_fusion.3, bf16[64,32,2,96]{3,2,0,1:T(2,128)(2,1)S(1)} %reshape.176), kind=kOutput, calls=%fused_computation.11 | convolution fusion | flops 805699584 | bytes 13902344 | tf_op jit(solution)/shard_map/tsbc,usbc->btu/dot_general | solution.py:11
  (24 shorter events, 0.6 us)
Async XLA Ops:
  6.5 43.1 %copy-start = (bf16[16,8192]{1,0:T(8,128)(2,1)S(1)}, bf16[16,8192]{1,0:T(8,128)(2,1)}, u32[]{:S(2)}) copy-start(bf16[16,8192]{1,0:T(8,128)(2,1)} %param.6) | copy-start | bytes 786436
  6.5 261.7 %all-gather.2.cloned.1.call-start = ((), (), s32[]{:S(2)}) async-start(), calls=%async_computation.2 | async-start | bytes 17825792 | tf_op jit(solution)/shard_map/all_gather | solution.py:48
  15.3 34.4 %copy-start.1 = (bf16[64,8192]{1,0:T(8,128)(2,1)S(1)}, bf16[64,8192]{1,0:T(8,128)(2,1)}, u32[]{:S(2)}) copy-start(bf16[64,8192]{1,0:T(8,128)(2,1)} %param.5) | copy-start | bytes 3145732
  15.3 34.4 %copy-start.2 = (f32[64,16]{0,1:T(8,128)S(1)}, f32[64,16]{0,1:T(8,128)}, u32[]{:S(2)}) copy-start(f32[64,16]{0,1:T(8,128)} %param.7) | copy-start | bytes 12292
  15.3 34.4 %copy-start.3 = (s32[64]{0:T(128)S(1)}, s32[64]{0:T(128)}, u32[]{:S(2)}) copy-start(s32[64]{0:T(128)} %param.8) | copy-start | bytes 772
Sparse Core Ops, SparseCore 0:
  150.2 118.0 all-gather.1
where the time goes:
time: 294 us
  waiting for transfers between devices  102 us (35%)
  blocking collectives  87.3 us (30%)
  local copies, waits for them, and re-layouts  61.9 us (21%)
  other arithmetic  15.9 us (5%)
  between operations  13.6 us (5%)
  matrix products  12.9 us (4%)
    all_gather x1, waiting for transfers between devices, shards(): lax.all_gather(own_frames, 'tm', axis=0, tiled=True)  102 us
    all_to_all x1, blocking collectives, shards(): lax.all_to_all(packed, 'pix', split_axis=1, concat_axis=1, tiled=True)  72.2 us
    gather x1, local copies, waits for them, and re-layouts, shards(): ordering[jnp.minimum(starts[:, None] + slot_index[None, :], pixels - 1)]  34.3 us
    gather x2, local copies, waits for them, and re-layouts, shards(): corrected[:, source.reshape(-1)]  23.9 us
    all_to_all x1, blocking collectives, shards(): lax.all_to_all(tallies, 'pix', split_axis=1, concat_axis=1, tiled=True)  15.1 us
    dot_general x1, matrix products, bin_block(): jnp.einsum('tsbc,usbc->btu', own_frames, portion, preferred_element_type=...  11.7 us
    reduce_sum x1, other arithmetic, bin_block(): other_sums = jnp.transpose(jnp.sum(portion, axis=(1, 3), dtype=jnp.float32))  7.24 us
    sort x1, other arithmetic, shards(): jnp.argsort(labels * pixels + jnp.arange(pixels, dtype=jnp.int32))  6.77 us
  transfers between devices with their start and end apart: 1, of which 1 were waited for; matrix products, arithmetic and copies ran while one was open for 0% of the time, Pallas kernels for 0%

commit v1 on v0

v1 whole, which is shorter than its diff:
```python
import jax, jax.numpy as jnp
from jax import lax
from jax.experimental import pallas as pl
from jax.experimental.pallas import tpu as pltpu
from jax.sharding import Mesh, PartitionSpec as P

CAP = 96
FRAMES = 64
PIXELS = 8192
EIGEN = 16
BINS = 64
CHUNK = 256
CHUNKS = PIXELS // CHUNK
SLOTS = BINS * CAP
PART = 24
DESTS = 128
DEPTH = 32 * PART


def pack_kernel(coef_ref, bins_ref, eigen_ref, raw_ref, out_ref,
                hot_ref, cum_ref, row_ref, place_ref, even_ref, odd_ref, slot_ref, sem):
    f32, bf16 = jnp.float32, jnp.bfloat16
    label = lax.broadcasted_iota(jnp.int32, (BINS, CHUNK), 0) + 1
    for j in range(CHUNKS):
        hot_ref[j * BINS:(j + 1) * BINS, :] = jnp.where(
            bins_ref[j:j + 1, :] == label, 1.0, 0.0).astype(bf16)
    before = lax.broadcasted_iota(jnp.int32, (CHUNK, CHUNK + 128), 0)
    after = lax.broadcasted_iota(jnp.int32, (CHUNK, CHUNK + 128), 1)
    prefix = jnp.where((before < after) | (after >= CHUNK), 1.0, 0.0).astype(bf16)
    cum_ref[...] = jnp.dot(hot_ref[...], prefix, preferred_element_type=f32)
    carry = jnp.zeros((BINS, 128), f32)
    for j in range(CHUNKS):
        rows = slice(j * BINS, (j + 1) * BINS)
        for h in range(2):
            lanes = slice(h * 128, (h + 1) * 128)
            rank = jnp.sum(hot_ref[rows, lanes].astype(f32) * (cum_ref[rows, lanes] + carry), axis=0, keepdims=True)
            own = bins_ref[j:j + 1, lanes]
            row_ref[2 * j + h:2 * j + h + 1, :] = jnp.where(
                own > 0, (own - 1) * CAP + rank.astype(jnp.int32), SLOTS)
        carry = carry + cum_ref[rows, CHUNK:]
    copy = pltpu.make_async_copy(row_ref, place_ref, sem)
    copy.start()

    zero = jnp.zeros((128, 128), f32)

    @pl.loop(0, SLOTS // 128)
    def _(i):
        slot_ref[pl.ds(pl.multiple_of(i * 128, 128), 128), :] = zero
    slot_ref[SLOTS:, :] = jnp.zeros((8, 128), f32)

    coef = coef_ref[...]
    high = coef.astype(bf16)
    rest = coef - high.astype(f32)
    mid = rest.astype(bf16)
    low = (rest - mid.astype(f32)).astype(bf16)
    weights = jnp.concatenate([high, mid, low], axis=1)

    def correct(j, target):
        at = pl.ds(pl.multiple_of(j * CHUNK, CHUNK), CHUNK)
        flats = eigen_ref[:, at]
        field = 0.5 + jnp.dot(weights, jnp.concatenate([flats] * 3, axis=0), preferred_element_type=f32)
        value = (raw_ref[:, at].astype(f32) / field).astype(bf16).astype(f32)
        for h in range(2):
            half = value[:, h * 128:(h + 1) * 128]
            target[h * 128:(h + 1) * 128, :] = jnp.concatenate([half, half], axis=0).T

    def scatter(j, source):
        for h in range(2):
            for i in range(128):
                place = place_ref[2 * j + h, i]
                slot_ref[pl.ds(place, 1), :] = source[h * 128 + i:h * 128 + i + 1, :]

    correct(0, even_ref)
    copy.wait()

    @pl.loop(0, CHUNKS // 2 - 1)
    def _(i):
        scatter(2 * i, even_ref)
        correct(2 * i + 1, odd_ref)
        scatter(2 * i + 1, odd_ref)
        correct(2 * i + 2, even_ref)
    scatter(CHUNKS - 2, even_ref)
    correct(CHUNKS - 1, odd_ref)
    scatter(CHUNKS - 1, odd_ref)

    left = lax.broadcasted_iota(jnp.int32, (PART, 128), 1) < FRAMES

    @pl.loop(0, BINS // 4)
    def _(z):
        for x in range(4):
            for c in range(2):
                base = (4 * z + x) * CAP + c * 2 * PART
                lo = slot_ref[pl.ds(pl.multiple_of(base, 8), PART), :]
                hi = slot_ref[pl.ds(pl.multiple_of(base + PART, 8), PART), :]
                out_ref[x * 32 + 2 * z + c] = jnp.where(left, lo, hi).astype(bf16)


def pack(coef, bins, eigen, raw):
    f32 = jnp.float32
    return pl.pallas_call(
        pack_kernel,
        out_shape=jax.ShapeDtypeStruct((DESTS, PART, 128), jnp.bfloat16),
        in_specs=[pl.BlockSpec(memory_space=pltpu.VMEM)] * 4,
        out_specs=pl.BlockSpec(memory_space=pltpu.VMEM),
        scratch_shapes=[
            pltpu.VMEM((CHUNKS * BINS, CHUNK), jnp.bfloat16),
            pltpu.VMEM((CHUNKS * BINS, CHUNK + 128), f32),
            pltpu.VMEM((PIXELS // 128, 128), jnp.int32),
            pltpu.SMEM((PIXELS // 128, 128), jnp.int32),
            pltpu.VMEM((CHUNK, 128), f32),
            pltpu.VMEM((CHUNK, 128), f32),
            pltpu.VMEM((SLOTS + 8, 128), f32),
            pltpu.SemaphoreType.DMA,
        ],
        compiler_params=pltpu.CompilerParams(vmem_limit_bytes=40 << 20),
        name="pack",
    )(coef, bins, eigen, raw)


def gram_kernel(core_ref, mine_ref, next_ref, last_ref, keep_ref, send_ref, own_ref):
    f32, bf16 = jnp.float32, jnp.bfloat16
    first = core_ref[0] == 0
    left = lax.broadcasted_iota(jnp.int32, (1, 128), 1) < FRAMES
    ones = jnp.ones((8, DEPTH), bf16)

    def matrix(ref):
        return jnp.concatenate([ref[x * DEPTH:(x + 1) * DEPTH, :] for x in range(4)], axis=1)

    def fold(even_top, even_low, odd_top, odd_low):
        return jnp.where(left, even_top, odd_low) + pltpu.roll(
            jnp.where(left, odd_top, even_low), FRAMES, 1)

    def product(a, b, group):
        full = lax.dot_general(a, b, (((0,), (0,)), ((), ())), preferred_element_type=f32)
        for x in range(4):
            top, low = slice(x * 128, x * 128 + 64), slice(x * 128 + 64, x * 128 + 128)
            for e in range(2):
                even, odd = slice(e * 256, e * 256 + 128), slice(e * 256 + 128, e * 256 + 256)
                part = fold(full[top, even], full[low, even], full[top, odd], full[low, odd])
                lanes = slice(group * 256 + e * 128, group * 256 + e * 128 + 128)
                keep_ref[x, :, lanes] = jnp.where(first, part[:32], part[32:])
                send_ref[x * 32:(x + 1) * 32, lanes] = jnp.where(first, part[32:], part[:32])

    def total(b, group):
        full = jnp.dot(ones, b, preferred_element_type=f32)
        for e in range(2):
            even, odd = full[:, e * 256:e * 256 + 128], full[:, e * 256 + 128:e * 256 + 256]
            lanes = slice(group * 256 + e * 128, group * 256 + e * 128 + 128)
            part = fold(even, even, odd, odd)
            own_ref[:, lanes] = part
            send_ref[128:, lanes] = part

    mine, after, prior = matrix(mine_ref), matrix(next_ref), matrix(last_ref)
    product(mine, mine, 1)
    product(mine, prior, 0)
    product(mine, after, 2)
    product(prior, after, 3)
    total(prior, 0)
    total(mine, 1)
    total(after, 2)
    hits = jnp.where(mine_ref[:DEPTH, :].astype(f32) != 0.0, 1.0, 0.0).astype(bf16)
    hits = jnp.dot(ones, hits, preferred_element_type=f32)
    hits = hits + pltpu.roll(hits, FRAMES, 1)
    for e in range(2):
        own_ref[:, 768 + e * 128:896 + e * 128] = hits
        send_ref[128:, 768 + e * 128:896 + e * 128] = hits


def gram(core, mine, after, prior):
    f32 = jnp.float32
    return pl.pallas_call(
        gram_kernel,
        out_shape=(jax.ShapeDtypeStruct((4, 32, 1024), f32),
                   jax.ShapeDtypeStruct((136, 1024), f32),
                   jax.ShapeDtypeStruct((8, 1024), f32)),
        in_specs=[pl.BlockSpec(memory_space=pltpu.SMEM)] + [pl.BlockSpec(memory_space=pltpu.VMEM)] * 3,
        out_specs=(pl.BlockSpec(memory_space=pltpu.VMEM),) * 3,
        compiler_params=pltpu.CompilerParams(vmem_limit_bytes=40 << 20),
        name="gram",
    )(core, mine, after, prior)


def scale_kernel(core_ref, keep_ref, got_ref, own_ref, rows_ref, far_ref):
    first = core_ref[0] == 0
    sums = own_ref[...] + got_ref[128:, :]
    count = sums[0:1, 768:896]
    count = jnp.concatenate([count, count], axis=1)

    def column(group):
        tall = [jnp.broadcast_to(sums[0:1, group * 256 + e * 128:group * 256 + e * 128 + 128], (128, 128)).T
                for e in range(2)]
        tall = jnp.concatenate(tall, axis=0)
        parts = []
        for x in range(4):
            part = jnp.where(first, tall[x * 64:x * 64 + 32], tall[x * 64 + 32:x * 64 + 64])
            parts.append(jnp.concatenate([part, part], axis=1))
        return parts

    mine, prior = column(1), column(0)
    for x in range(4):
        for group in range(4):
            lanes = slice(group * 256, group * 256 + 256)
            value = keep_ref[x, :, lanes] + got_ref[x * 32:(x + 1) * 32, lanes]
            if group < 3:
                rows_ref[x, :, lanes] = count * value / (mine[x] * sums[0:1, lanes])
            else:
                far_ref[x] = count * value / (prior[x] * sums[0:1, 512:768])


def scale(core, keep, got, own):
    f32 = jnp.float32
    return pl.pallas_call(
        scale_kernel,
        out_shape=(jax.ShapeDtypeStruct((4, 32, 768), f32),
                   jax.ShapeDtypeStruct((4, 32, 256), f32)),
        in_specs=[pl.BlockSpec(memory_space=pltpu.SMEM)] + [pl.BlockSpec(memory_space=pltpu.VMEM)] * 3,
        out_specs=(pl.BlockSpec(memory_space=pltpu.VMEM),) * 2,
        name="scale",
    )(core, keep, got, own)


def place_kernel(at_ref, rows_ref, got_ref, out_ref):
    core, row = at_ref[0], at_ref[1]
    for b in range(2):
        for group in range(4):
            lanes = pl.ds(pl.multiple_of(lax.rem(row + 3 + group, 4) * 256, 256), 256)
            out_ref[b, pl.ds(pl.multiple_of(core * 32, 32), 32), lanes] = (
                rows_ref[2 * core + b, :, group * 256:(group + 1) * 256])
            out_ref[b, pl.ds(pl.multiple_of((1 - core) * 32, 32), 32), lanes] = (
                got_ref[b, :, group * 256:(group + 1) * 256])


def place(at, rows, got):
    return pl.pallas_call(
        place_kernel,
        out_shape=jax.ShapeDtypeStruct((2, 64, 1024), jnp.float32),
        in_specs=[pl.BlockSpec(memory_space=pltpu.SMEM)] + [pl.BlockSpec(memory_space=pltpu.VMEM)] * 2,
        out_specs=pl.BlockSpec(memory_space=pltpu.VMEM),
        name="place",
    )(at, rows, got)


def shift(size, step):
    return [(i, (i + step) % size) for i in range(size)]


def shards(raw_frames, eigen_flats, weights, flat_count, bin_map):
    core = lax.axis_index("c").astype(jnp.int32)
    row = lax.axis_index("y").astype(jnp.int32)
    in_use = lax.broadcasted_iota(jnp.int32, (FRAMES, EIGEN), 1) < flat_count[:, None]
    coefficients = jnp.where(in_use, weights, 0.0)
    packed = pack(coefficients, bin_map.reshape(CHUNKS, CHUNK), eigen_flats, raw_frames)
    mine = lax.all_to_all(packed, ("x", "z", "c"), 0, 0, tiled=True).reshape(4 * DEPTH, 128)
    prior = lax.ppermute(mine, "y", shift(4, 1))
    after = lax.ppermute(mine, "y", shift(4, -1))
    keep, send, own = gram(core[None], mine, after, prior)
    got = lax.ppermute(send, "c", shift(2, 1))
    rows, far = scale(core[None], keep, got, own)
    far = lax.ppermute(far, "y", shift(4, -1))
    rows = lax.all_to_all(jnp.concatenate([rows, far], axis=2), "x", 0, 0, tiled=True)
    other = lax.ppermute(lax.dynamic_slice_in_dim(rows, 2 * (1 - core), 2, 0), "c", shift(2, 1))
    return place(jnp.stack([core, row]), rows, other)


def solution(mesh):
    split = Mesh(mesh.devices.reshape(16, 2, 4, 4), ("z", "c", "y", "x"))
    return jax.shard_map(
        shards,
        mesh=split,
        in_specs=(P(("y", "x"), ("z", "c")), P(None, ("z", "c")), P(("y", "x"), None), P(("y", "x")), P(("z", "c"))),
        out_specs=P(("z", "c"), ("y", "x"), None),
        check_vma=False,
    )
```

time: 294 us -> 145 us (0.49)
  waiting for transfers between devices: 102 us -> 32.9 us
  local copies, waits for them, and re-layouts: 61.9 us -> 6.54 us
  blocking collectives: 87.3 us -> 63.7 us
  starting transfers between devices: 0.01 us -> 22 us
  Pallas kernels: 0 us -> 16.5 us
  between operations: 13.6 us -> 0.1 us
  other arithmetic: 15.9 us -> 2.53 us
  matrix products: 12.9 us -> 0 us
    all_gather x1 -> x0, waiting for transfers between devices: 102 us -> none  [shards(): lax.all_gather(own_frames, 'tm', axis=0, tiled=True)]
    gather x3 -> x0, local copies, waits for them, and re-layouts: 58.1 us -> none  [the longest x1 34.3 us: shards(): ordering[jnp.minimum(starts[:, None] + slot_index[None, :], pixels - 1)]]
    ppermute x0 -> x5, waiting for transfers between devices: none -> 25.1 us  [the longest x1 13.1 us: shards(): after = lax.ppermute(mine, 'y', shift(4, -1))]
    all_to_all x2 -> x1, blocking collectives: 87.3 us -> 63.7 us  [shards(): lax.all_to_all(packed, ('x', 'z', 'c'), 0, 0, tiled=True)]
    ppermute x0 -> x5, starting transfers between devices: none -> 17.9 us  [the longest x1 4.83 us: shards(): got = lax.ppermute(send, 'c', shift(2, 1))]
    pallas_call x0 -> x4, Pallas kernels: none -> 16.5 us  [the longest x1 10.2 us: pack(): pl.pallas_call(pack_kernel, out_shape=jax.ShapeDtypeStruct((DESTS, PART,...]
    dot_general x2 -> x0, matrix products: 12.9 us -> none  [the longest x1 11.7 us: bin_block(): jnp.einsum('tsbc,usbc->btu', own_frames, portion, preferred_element_type=...]
    reduce_sum x5 -> x0, other arithmetic: 7.92 us -> none  [the longest x1 7.24 us: bin_block(): other_sums = jnp.transpose(jnp.sum(portion, axis=(1, 3), dtype=jnp.float32))]
  transfers between devices with their start and end apart: 1 -> 6, of which waited for: 1 -> 6; matrix products, arithmetic and copies ran while one was open for 0% -> 0% of each run, Pallas kernels for 0% -> 0%
where the time goes in v1:
time: 145 us; the launch traced here: 144 us
  blocking collectives  63.7 us (44%)
  waiting for transfers between devices  32.9 us (23%)
  starting transfers between devices  22 us (15%)
  Pallas kernels  16.5 us (11%)
  local copies, waits for them, and re-layouts  6.54 us (5%)
  other arithmetic  2.53 us (2%)
    all_to_all x1, blocking collectives, shards(): lax.all_to_all(packed, ('x', 'z', 'c'), 0, 0, tiled=True)  63.7 us
    ppermute x1, waiting for transfers between devices, shards(): after = lax.ppermute(mine, 'y', shift(4, -1))  13.1 us
    pallas_call x1, Pallas kernels, pack(): pl.pallas_call(pack_kernel, out_shape=jax.ShapeDtypeStruct((DESTS, PART,...  10.2 us
    all_to_all x1, waiting for transfers between devices, shards(): lax.all_to_all(jnp.concatenate([rows, far], axis=2), 'x', 0, 0, tiled=True)  7.77 us
    unnamed x19, local copies, waits for them, and re-layouts  6.51 us
    ppermute x1, waiting for transfers between devices, shards(): prior = lax.ppermute(mine, 'y', shift(4, 1))  5.05 us
    ppermute x1, waiting for transfers between devices, shards(): far = lax.ppermute(far, 'y', shift(4, -1))  4.86 us
    ppermute x1, starting transfers between devices, shards(): got = lax.ppermute(send, 'c', shift(2, 1))  4.83 us
  transfers between devices with their start and end apart: 6, of which 6 were waited for; matrix products, arithmetic and copies ran while one was open for 0% of the time, Pallas kernels for 0%

profile of v1, /device:TPU:1, one launch (start us, length us, event | category | flops | bytes accessed | tf_op | source)
XLA Modules:
  0.0 144.2 jit_solution(12196728244914445405)
XLA Ops:
  0.0 0.8 copy.6
  0.8 0.6 copy-done.8
  1.5 1.2 copy-done
  2.8 0.9 copy-done.2
  3.7 10.2 %pack.1 = bf16[128,24,128]{2,1,0:T(8,128)(2,1)S(1)} custom-call(f32[64,16]{1,0:T(8,128)S(1)} %fusion.coef_ref, s32[32,256]{1,0:T(8,128)S(1)} %reshape.7.bins_ref, bf16[16,8192]{1,0:T(8,128)(2,1)S(1)} %copy-done.2, bf16[64,8192]{1,0:T(8,128)(2,1)S(1)} %copy-done), custom_call_target="tpu_custom_call" | custom-call | tf_op jit(solution)/shard_map/pack/pallas_call | solution.py:100
  13.9 63.7 %all_to_all.10 = bf16[128,24,128]{2,1,0:T(8,128)(2,1)S(1)} all-to-all(bf16[128,24,128]{2,1,0:T(8,128)(2,1)S(1)} %pack.1), channel_id=1, replica_groups=mesh['z'=16,'c'=2,'y'=4,'x'=4] {'x','z','c'}, dimensions={0} | all-to-all | bytes 1572864 | tf_op jit(solution)/shard_map/all_to_all | solution.py:253
  77.5 4.6 %collective-permute-start = (bf16[3072,128]{1,0:T(8,128)(2,1)S(1)}, bf16[3072,128]{1,0:T(8,128)(2,1)S(1)}, u32[]{:S(2)}, u32[]{:S(2)}) collective-permute-start(bf16[3072,128]{1,0:T(8,128)(2,1)S(1)} %bitcast.3), channel_id=1, source_target_pairs={{0,12},{4,0},{8,4},{12,8},{1,13},{5,1},{9,5},{13,9},{2,14},{6,2},{... | collective-permute-start | bytes 2359304 | tf_op jit(solution)/shard_map/ppermute | solution.py:255
  82.2 1.9 %collective-permute-start.1 = (bf16[3072,128]{1,0:T(8,128)(2,1)S(1)}, bf16[3072,128]{1,0:T(8,128)(2,1)S(1)}, u32[]{:S(2)}, u32[]{:S(2)}) collective-permute-start(bf16[3072,128]{1,0:T(8,128)(2,1)S(1)} %bitcast.4), channel_id=1, source_target_pairs={{0,4},{4,8},{8,12},{12,0},{1,5},{5,9},{9,13},{13,1},{2,6},{6,10},{... | collective-permute-start | bytes 2359304 | tf_op jit(solution)/shard_map/ppermute | solution.py:254
  84.1 13.1 %collective-permute-done.next_ref = bf16[3072,128]{1,0:T(8,128)(2,1)S(1)} collective-permute-done((bf16[3072,128]{1,0:T(8,128)(2,1)S(1)}, bf16[3072,128]{1,0:T(8,128)(2,1)S(1)}, u32[]{:S(2)}, u32[]{:S(2)}) %collective-permute-start) | collective-permute-done | bytes 786464 | tf_op jit(solution)/shard_map/ppermute | solution.py:255
  97.2 5.0 %collective-permute-done.1.last_ref = bf16[3072,128]{1,0:T(8,128)(2,1)S(1)} collective-permute-done((bf16[3072,128]{1,0:T(8,128)(2,1)S(1)}, bf16[3072,128]{1,0:T(8,128)(2,1)S(1)}, u32[]{:S(2)}, u32[]{:S(2)}) %collective-permute-start.1) | collective-permute-done | bytes 786464 | tf_op jit(solution)/shard_map/ppermute | solution.py:254
  102.3 2.2 %gram.1 = (f32[4,32,1024]{2,1,0:T(8,128)S(1)}, f32[136,1024]{1,0:T(8,128)S(1)}, f32[8,1024]{1,0:T(8,128)S(1)}) custom-call(s32[1]{0:T(128)} %bitcast.core_ref, bf16[3072,128]{1,0:T(8,128)(2,1)S(1)} %bitcast.5, bf16[3072,128]{1,0:T(8,128)(2,1)S(1)} %collective-permute-done.next_ref, bf16[3072,128]{1,0:T(8,128)(2,1)S(1)} %collective-permute-done.1.last_ref), custom_call_target="tpu_custom_call" | custom-call | tf_op jit(solution)/shard_map/gram/pallas_call | solution.py:171
  104.5 0.8 copy-done.1
  105.9 4.8 %collective-permute-start.2 = (f32[136,1024]{1,0:T(8,128)S(1)}, f32[136,1024]{1,0:T(8,128)S(1)}, u32[]{:S(2)}, u32[]{:S(2)}) collective-permute-start(f32[136,1024]{1,0:T(8,128)S(1)} %get-tuple-element.11), channel_id=1, source_target_pairs={{0,16},{16,0},{1,17},{17,1},{2,18},{18,2},{3,19},{19,3},{4,20},{20... | collective-permute-start | bytes 1671176 | tf_op jit(solution)/shard_map/ppermute | solution.py:257
  110.7 1.6 %collective-permute-done.2.got_ref = f32[136,1024]{1,0:T(8,128)S(1)} collective-permute-done((f32[136,1024]{1,0:T(8,128)S(1)}, f32[136,1024]{1,0:T(8,128)S(1)}, u32[]{:S(2)}, u32[]{:S(2)}) %collective-permute-start.2) | collective-permute-done | bytes 557088 | tf_op jit(solution)/shard_map/ppermute | solution.py:257
  112.3 0.8 copy-done.5
  113.1 2.1 %scale.1 = (f32[4,32,768]{2,1,0:T(8,128)}, f32[4,32,256]{2,1,0:T(8,128)}) custom-call(s32[1]{0:T(128)} %bitcast.core_ref, f32[4,32,1024]{2,1,0:T(8,128)} %copy-done.1, f32[136,1024]{1,0:T(8,128)} %copy-done.5, f32[8,1024]{1,0:T(8,128)} %copy-done.3), custom_call_target="tpu_custom_call" | custom-call | tf_op jit(solution)/shard_map/scale/pallas_call | solution.py:212
  115.3 1.9 %collective-permute-start.3 = (f32[4,32,256]{2,1,0:T(8,128)}, f32[4,32,256]{2,1,0:T(8,128)S(1)}, u32[]{:S(2)}, u32[]{:S(2)}) collective-permute-start(f32[4,32,256]{2,1,0:T(8,128)} %get-tuple-element.14), channel_id=1, source_target_pairs={{0,12},{4,0},{8,4},{12,8},{1,13},{5,1},{9,5},{13,9},{2,14},{6,2},{... | collective-permute-start | bytes 393224 | tf_op jit(solution)/shard_map/ppermute | solution.py:259
  117.2 4.9 %collective-permute-done.3 = f32[4,32,256]{2,1,0:T(8,128)S(1)} collective-permute-done((f32[4,32,256]{2,1,0:T(8,128)}, f32[4,32,256]{2,1,0:T(8,128)S(1)}, u32[]{:S(2)}, u32[]{:S(2)}) %collective-permute-start.3) | collective-permute-done | bytes 131104 | tf_op jit(solution)/shard_map/ppermute | solution.py:259
  122.0 1.8 %pad_maximum_fusion = f32[4,32,1024]{2,1,0:T(8,128)} fusion(f32[4,32,256]{2,1,0:T(8,128)S(1)} %collective-permute-done.3, f32[4,32,768]{2,1,0:T(8,128)} %get-tuple-element.13), kind=kLoop, calls=%fused_computation | loop fusion | flops 131072 | bytes 1048576 | tf_op jit(solution)/shard_map/concatenate | solution.py:260
  123.9 4.1 %all-to-all-start.1 = ((f32[4,32,1024]{2,1,0:T(8,128)}), f32[4,32,1024]{2,1,0:T(8,128)S(1)}, u32[]{:S(2)}, u32[]{:S(2)}) async-start(f32[4,32,1024]{2,1,0:T(8,128)} %pad_maximum_fusion), calls=%async_computation.1 | async-start | bytes 1048576 | tf_op jit(solution)/shard_map/all_to_all | solution.py:260
  128.0 7.8 %all-to-all-done.1.rows_ref = f32[4,32,1024]{2,1,0:T(8,128)S(1)} async-done(((f32[4,32,1024]{2,1,0:T(8,128)}), f32[4,32,1024]{2,1,0:T(8,128)S(1)}, u32[]{:S(2)}, u32[]{:S(2)}) %all-to-all-start.1) | async-done | bytes 524320 | tf_op jit(solution)/shard_map/all_to_all | solution.py:260
  135.8 4.6 %collective-permute-start.4 = (f32[2,32,1024]{2,1,0:T(8,128)S(1)}, f32[2,32,1024]{2,1,0:T(8,128)S(1)}, u32[]{:S(2)}, u32[]{:S(2)}) collective-permute-start(f32[2,32,1024]{2,1,0:T(8,128)S(1)} %constant_dynamic-slice_fusion), channel_id=1, source_target_pairs={{0,16},{16,0},{1,17},{17,1},{2,18},{18,2},{3,19},{19,3},{4,20},{20... | collective-permute-start | bytes 786440 | tf_op jit(solution)/shard_map/ppermute | solution.py:261
  141.5 0.7 copy-done.6
  142.2 2.0 %place.1 = f32[2,64,1024]{2,1,0:T(8,128)} custom-call(s32[2]{0:T(128)} %pad_add_fusion.at_ref, f32[4,32,1024]{2,1,0:T(8,128)} %copy-done.4, f32[2,32,1024]{2,1,0:T(8,128)} %copy-done.6), custom_call_target="tpu_custom_call" | custom-call | tf_op jit(solution)/shard_map/place/pallas_call | solution.py:234
  (17 shorter events, 1.9 us)
Async XLA Ops:
  0.0 0.8 copy-start.7
  0.8 0.7 copy-start.8
  1.5 1.2 copy-start
  2.8 0.9 copy-start.2
  77.5 19.7 %collective-permute-start = (bf16[3072,128]{1,0:T(8,128)(2,1)S(1)}, bf16[3072,128]{1,0:T(8,128)(2,1)S(1)}, u32[]{:S(2)}, u32[]{:S(2)}) collective-permute-start(bf16[3072,128]{1,0:T(8,128)(2,1)S(1)} %bitcast.3), channel_id=1, source_target_pairs={{0,12},{4,0},{8,4},{12,8},{1,13},{5,1},{9,5},{13,9},{2,14},{6,2},{... | collective-permute-start | bytes 2359304 | tf_op jit(solution)/shard_map/ppermute | solution.py:255
  82.2 20.1 %collective-permute-start.1 = (bf16[3072,128]{1,0:T(8,128)(2,1)S(1)}, bf16[3072,128]{1,0:T(8,128)(2,1)S(1)}, u32[]{:S(2)}, u32[]{:S(2)}) collective-permute-start(bf16[3072,128]{1,0:T(8,128)(2,1)S(1)} %bitcast.4), channel_id=1, source_target_pairs={{0,4},{4,8},{8,12},{12,0},{1,5},{5,9},{9,13},{13,1},{2,6},{6,10},{... | collective-permute-start | bytes 2359304 | tf_op jit(solution)/shard_map/ppermute | solution.py:254
  104.5 0.8 copy-start.1
  105.3 0.6 copy-start.3
  105.9 6.4 %collective-permute-start.2 = (f32[136,1024]{1,0:T(8,128)S(1)}, f32[136,1024]{1,0:T(8,128)S(1)}, u32[]{:S(2)}, u32[]{:S(2)}) collective-permute-start(f32[136,1024]{1,0:T(8,128)S(1)} %get-tuple-element.11), channel_id=1, source_target_pairs={{0,16},{16,0},{1,17},{17,1},{2,18},{18,2},{3,19},{19,3},{4,20},{20... | collective-permute-start | bytes 1671176 | tf_op jit(solution)/shard_map/ppermute | solution.py:257
  112.3 0.8 copy-start.5
  115.3 6.8 %collective-permute-start.3 = (f32[4,32,256]{2,1,0:T(8,128)}, f32[4,32,256]{2,1,0:T(8,128)S(1)}, u32[]{:S(2)}, u32[]{:S(2)}) collective-permute-start(f32[4,32,256]{2,1,0:T(8,128)} %get-tuple-element.14), channel_id=1, source_target_pairs={{0,12},{4,0},{8,4},{12,8},{1,13},{5,1},{9,5},{13,9},{2,14},{6,2},{... | collective-permute-start | bytes 393224 | tf_op jit(solution)/shard_map/ppermute | solution.py:259
  123.9 11.9 %all-to-all-start.1 = ((f32[4,32,1024]{2,1,0:T(8,128)}), f32[4,32,1024]{2,1,0:T(8,128)S(1)}, u32[]{:S(2)}, u32[]{:S(2)}) async-start(f32[4,32,1024]{2,1,0:T(8,128)} %pad_maximum_fusion), calls=%async_computation.1 | async-start | bytes 1048576 | tf_op jit(solution)/shard_map/all_to_all | solution.py:260
  135.7 5.7 %copy-start.4 = (f32[4,32,1024]{2,1,0:T(8,128)}, f32[4,32,1024]{2,1,0:T(8,128)S(1)}, u32[]{:S(2)}) copy-start(f32[4,32,1024]{2,1,0:T(8,128)S(1)} %all-to-all-done.1.rows_ref) | copy-start | bytes 1572868
  135.8 5.7 %collective-permute-start.4 = (f32[2,32,1024]{2,1,0:T(8,128)S(1)}, f32[2,32,1024]{2,1,0:T(8,128)S(1)}, u32[]{:S(2)}, u32[]{:S(2)}) collective-permute-start(f32[2,32,1024]{2,1,0:T(8,128)S(1)} %constant_dynamic-slice_fusion), channel_id=1, source_target_pairs={{0,16},{16,0},{1,17},{17,1},{2,18},{18,2},{3,19},{19,3},{4,20},{20... | collective-permute-start | bytes 786440 | tf_op jit(solution)/shard_map/ppermute | solution.py:261
  141.5 0.7 copy-start.6

commit v2 on v1

--- a/solution.py
+++ b/solution.py
@@ -17,13 +17,28 @@
 DEPTH = 32 * PART
 
 
-def pack_kernel(coef_ref, bins_ref, eigen_ref, raw_ref, out_ref,
-                hot_ref, cum_ref, row_ref, place_ref, even_ref, odd_ref, slot_ref, sem):
+def pack_kernel(weights_hbm, used_hbm, bins_hbm, eigen_hbm, raw_hbm, out_ref,
+                weights_ref, used_ref, bins_ref, eigen_ref, raw_ref,
+                hot_ref, cum_ref, row_ref, place_ref, even_ref, odd_ref, slot_ref, sems):
     f32, bf16 = jnp.float32, jnp.bfloat16
-    label = lax.broadcasted_iota(jnp.int32, (BINS, CHUNK), 0) + 1
+    sources = (bins_hbm, eigen_hbm, weights_hbm, used_hbm, raw_hbm)
+    targets = (bins_ref, eigen_ref, weights_ref, used_ref, raw_ref)
+    loads = [pltpu.make_async_copy(a, b, sems.at[i]) for i, (a, b) in enumerate(zip(sources, targets))]
+    for load in loads:
+        load.start()
+    zero = jnp.zeros((128, 128), f32)
+
+    @pl.loop(0, SLOTS // 128)
+    def _(i):
+        slot_ref[pl.ds(pl.multiple_of(i * 128, 128), 128), :] = zero
+    slot_ref[SLOTS:, :] = jnp.zeros((8, 128), f32)
+    loads[0].wait()
+
+    label = lax.broadcasted_iota(jnp.int32, (BINS, 128), 0) + 1
     for j in range(CHUNKS):
-        hot_ref[j * BINS:(j + 1) * BINS, :] = jnp.where(
-            bins_ref[j:j + 1, :] == label, 1.0, 0.0).astype(bf16)
+        for h in range(2):
+            hot_ref[j * BINS:(j + 1) * BINS, h * 128:(h + 1) * 128] = jnp.where(
+                bins_ref[2 * j + h:2 * j + h + 1, :] == label, 1.0, 0.0).astype(bf16)
     before = lax.broadcasted_iota(jnp.int32, (CHUNK, CHUNK + 128), 0)
     after = lax.broadcasted_iota(jnp.int32, (CHUNK, CHUNK + 128), 1)
     prefix = jnp.where((before < after) | (after >= CHUNK), 1.0, 0.0).astype(bf16)
@@ -34,26 +49,22 @@
         for h in range(2):
             lanes = slice(h * 128, (h + 1) * 128)
             rank = jnp.sum(hot_ref[rows, lanes].astype(f32) * (cum_ref[rows, lanes] + carry), axis=0, keepdims=True)
-            own = bins_ref[j:j + 1, lanes]
+            own = bins_ref[2 * j + h:2 * j + h + 1, :]
             row_ref[2 * j + h:2 * j + h + 1, :] = jnp.where(
                 own > 0, (own - 1) * CAP + rank.astype(jnp.int32), SLOTS)
         carry = carry + cum_ref[rows, CHUNK:]
-    copy = pltpu.make_async_copy(row_ref, place_ref, sem)
+    copy = pltpu.make_async_copy(row_ref, place_ref, sems.at[5])
     copy.start()
-
-    zero = jnp.zeros((128, 128), f32)
-
-    @pl.loop(0, SLOTS // 128)
-    def _(i):
-        slot_ref[pl.ds(pl.multiple_of(i * 128, 128), 128), :] = zero
-    slot_ref[SLOTS:, :] = jnp.zeros((8, 128), f32)
-
-    coef = coef_ref[...]
+    for load in loads[1:]:
+        load.wait()
+
+    in_use = lax.broadcasted_iota(jnp.int32, (EIGEN, FRAMES), 0) < used_ref[...]
+    coef = jnp.where(in_use, weights_ref[...], 0.0)
     high = coef.astype(bf16)
     rest = coef - high.astype(f32)
     mid = rest.astype(bf16)
     low = (rest - mid.astype(f32)).astype(bf16)
-    weights = jnp.concatenate([high, mid, low], axis=1)
+    weights = jnp.concatenate([high.astype(f32), mid.astype(f32), low.astype(f32)], axis=0).T.astype(bf16)
 
     def correct(j, target):
         at = pl.ds(pl.multiple_of(j * CHUNK, CHUNK), CHUNK)
@@ -95,14 +106,19 @@
                 out_ref[x * 32 + 2 * z + c] = jnp.where(left, lo, hi).astype(bf16)
 
 
-def pack(coef, bins, eigen, raw):
+def pack(weights, used, bins, eigen, raw):
     f32 = jnp.float32
     return pl.pallas_call(
         pack_kernel,
         out_shape=jax.ShapeDtypeStruct((DESTS, PART, 128), jnp.bfloat16),
-        in_specs=[pl.BlockSpec(memory_space=pltpu.VMEM)] * 4,
+        in_specs=[pl.BlockSpec(memory_space=pltpu.HBM)] * 5,
         out_specs=pl.BlockSpec(memory_space=pltpu.VMEM),
         scratch_shapes=[
+            pltpu.VMEM((EIGEN, FRAMES), f32),
+            pltpu.VMEM((1, FRAMES), jnp.int32),
+            pltpu.VMEM((PIXELS // 128, 128), jnp.int32),
+            pltpu.VMEM((EIGEN, PIXELS), jnp.bfloat16),
+            pltpu.VMEM((FRAMES, PIXELS), jnp.bfloat16),
             pltpu.VMEM((CHUNKS * BINS, CHUNK), jnp.bfloat16),
             pltpu.VMEM((CHUNKS * BINS, CHUNK + 128), f32),
             pltpu.VMEM((PIXELS // 128, 128), jnp.int32),
@@ -110,11 +126,11 @@
             pltpu.VMEM((CHUNK, 128), f32),
             pltpu.VMEM((CHUNK, 128), f32),
             pltpu.VMEM((SLOTS + 8, 128), f32),
-            pltpu.SemaphoreType.DMA,
+            pltpu.SemaphoreType.DMA((6,)),
         ],
-        compiler_params=pltpu.CompilerParams(vmem_limit_bytes=40 << 20),
+        compiler_params=pltpu.CompilerParams(vmem_limit_bytes=24 << 20),
         name="pack",
-    )(coef, bins, eigen, raw)
+    )(*(pltpu.with_memory_space_constraint(a, pltpu.HBM) for a in (weights, used, bins, eigen, raw)))
 
 
 def gram_kernel(core_ref, mine_ref, next_ref, last_ref, keep_ref, send_ref, own_ref):
@@ -175,7 +191,7 @@
                    jax.ShapeDtypeStruct((8, 1024), f32)),
         in_specs=[pl.BlockSpec(memory_space=pltpu.SMEM)] + [pl.BlockSpec(memory_space=pltpu.VMEM)] * 3,
         out_specs=(pl.BlockSpec(memory_space=pltpu.VMEM),) * 3,
-        compiler_params=pltpu.CompilerParams(vmem_limit_bytes=40 << 20),
+        compiler_params=pltpu.CompilerParams(vmem_limit_bytes=24 << 20),
         name="gram",
     )(core, mine, after, prior)
 
@@ -204,17 +220,20 @@
             if group < 3:
                 rows_ref[x, :, lanes] = count * value / (mine[x] * sums[0:1, lanes])
             else:
-                far_ref[x] = count * value / (prior[x] * sums[0:1, 512:768])
+                value = count * value / (prior[x] * sums[0:1, 512:768])
+                rows_ref[x, :, lanes] = value
+                far_ref[x] = value
 
 
 def scale(core, keep, got, own):
     f32 = jnp.float32
     return pl.pallas_call(
         scale_kernel,
-        out_shape=(jax.ShapeDtypeStruct((4, 32, 768), f32),
+        out_shape=(jax.ShapeDtypeStruct((4, 32, 1024), f32),
                    jax.ShapeDtypeStruct((4, 32, 256), f32)),
         in_specs=[pl.BlockSpec(memory_space=pltpu.SMEM)] + [pl.BlockSpec(memory_space=pltpu.VMEM)] * 3,
         out_specs=(pl.BlockSpec(memory_space=pltpu.VMEM),) * 2,
+        compiler_params=pltpu.CompilerParams(vmem_limit_bytes=8 << 20),
         name="scale",
     )(core, keep, got, own)
 
@@ -236,6 +255,7 @@
         out_shape=jax.ShapeDtypeStruct((2, 64, 1024), jnp.float32),
         in_specs=[pl.BlockSpec(memory_space=pltpu.SMEM)] + [pl.BlockSpec(memory_space=pltpu.VMEM)] * 2,
         out_specs=pl.BlockSpec(memory_space=pltpu.VMEM),
+        compiler_params=pltpu.CompilerParams(vmem_limit_bytes=8 << 20),
         name="place",
     )(at, rows, got)
 
@@ -247,9 +267,7 @@
 def shards(raw_frames, eigen_flats, weights, flat_count, bin_map):
     core = lax.axis_index("c").astype(jnp.int32)
     row = lax.axis_index("y").astype(jnp.int32)
-    in_use = lax.broadcasted_iota(jnp.int32, (FRAMES, EIGEN), 1) < flat_count[:, None]
-    coefficients = jnp.where(in_use, weights, 0.0)
-    packed = pack(coefficients, bin_map.reshape(CHUNKS, CHUNK), eigen_flats, raw_frames)
+    packed = pack(weights.T, flat_count[None, :], bin_map.reshape(PIXELS // 128, 128), eigen_flats, raw_frames)
     mine = lax.all_to_all(packed, ("x", "z", "c"), 0, 0, tiled=True).reshape(4 * DEPTH, 128)
     prior = lax.ppermute(mine, "y", shift(4, 1))
     after = lax.ppermute(mine, "y", shift(4, -1))
@@ -257,7 +275,7 @@
     got = lax.ppermute(send, "c", shift(2, 1))
     rows, far = scale(core[None], keep, got, own)
     far = lax.ppermute(far, "y", shift(4, -1))
-    rows = lax.all_to_all(jnp.concatenate([rows, far], axis=2), "x", 0, 0, tiled=True)
+    rows = lax.all_to_all(rows.at[:, :, 768:].set(far), "x", 0, 0, tiled=True)
     other = lax.ppermute(lax.dynamic_slice_in_dim(rows, 2 * (1 - core), 2, 0), "c", shift(2, 1))
     return place(jnp.stack([core, row]), rows, other)
 

time: 145 us -> 136 us (0.938)
  local copies, waits for them, and re-layouts: 6.54 us -> 0.68 us
  other arithmetic: 2.53 us -> 0.08 us
    unnamed x19 -> x0, local copies, waits for them, and re-layouts: 6.51 us -> none
    concatenate x1 -> x0, other arithmetic: 1.85 us -> none  [shards(): jnp.concatenate([rows, far], axis=2)]
where the time goes in v2:
time: 136 us; the launch traced here: 135 us
  blocking collectives  63.7 us (47%)
  waiting for transfers between devices  33.2 us (24%)
  starting transfers between devices  22 us (16%)
  Pallas kernels  15.5 us (11%)
    all_to_all x1, blocking collectives, shards(): lax.all_to_all(packed, ('x', 'z', 'c'), 0, 0, tiled=True)  63.7 us
    ppermute x1, waiting for transfers between devices, shards(): after = lax.ppermute(mine, 'y', shift(4, -1))  13.1 us
    pallas_call x1, Pallas kernels, pack(): pl.pallas_call(pack_kernel, out_shape=jax.ShapeDtypeStruct((DESTS, PART,...  11 us
    all_to_all x1, waiting for transfers between devices, shards(): rows = lax.all_to_all(rows.at[:, :, 768:].set(far), 'x', 0, 0, tiled=True)  7.77 us
    ppermute x1, waiting for transfers between devices, shards(): prior = lax.ppermute(mine, 'y', shift(4, 1))  5.05 us
    ppermute x1, starting transfers between devices, shards(): got = lax.ppermute(send, 'c', shift(2, 1))  4.85 us
    ppermute x1, waiting for transfers between devices, shards(): far = lax.ppermute(far, 'y', shift(4, -1))  4.65 us
    ppermute x1, starting transfers between devices, shards(): after = lax.ppermute(mine, 'y', shift(4, -1))  4.63 us
  transfers between devices with their start and end apart: 6, of which 6 were waited for; matrix products, arithmetic and copies ran while one was open for 0% of the time, Pallas kernels for 0%

profile of v2, /device:TPU:1, one launch (start us, length us, event | category | flops | bytes accessed | tf_op | source)
XLA Modules:
  0.0 135.2 jit_solution(12781528192456245855)
XLA Ops:
  0.0 11.0 %pack.1 = bf16[128,24,128]{2,1,0:T(8,128)(2,1)S(1)} custom-call(f32[16,64]{1,0:T(8,128)} %bitcast.10, s32[1,64]{1,0:T(1,128)} %bitcast.11, s32[64,128]{1,0:T(8,128)} %bitcast.9, bf16[16,8192]{1,0:T(8,128)(2,1)} %eigen_hbm.1, bf16[64,8192]{1,0:T(8,128)(2,1)} %raw_hbm.1), custom_call_target="tpu_custom_call" | custom-call | tf_op jit(solution)/shard_map/pack/pallas_call | solution.py:111
  11.0 63.7 %all_to_all.10 = bf16[128,24,128]{2,1,0:T(8,128)(2,1)S(1)} all-to-all(bf16[128,24,128]{2,1,0:T(8,128)(2,1)S(1)} %pack.1), channel_id=1, replica_groups=mesh['z'=16,'c'=2,'y'=4,'x'=4] {'x','z','c'}, dimensions={0} | all-to-all | bytes 1572864 | tf_op jit(solution)/shard_map/all_to_all | solution.py:271
  74.7 4.6 %collective-permute-start = (bf16[3072,128]{1,0:T(8,128)(2,1)S(1)}, bf16[3072,128]{1,0:T(8,128)(2,1)S(1)}, u32[]{:S(2)}, u32[]{:S(2)}) collective-permute-start(bf16[3072,128]{1,0:T(8,128)(2,1)S(1)} %bitcast.6), channel_id=1, source_target_pairs={{0,12},{4,0},{8,4},{12,8},{1,13},{5,1},{9,5},{13,9},{2,14},{6,2},{... | collective-permute-start | bytes 2359304 | tf_op jit(solution)/shard_map/ppermute | solution.py:273
  79.3 1.9 %collective-permute-start.1 = (bf16[3072,128]{1,0:T(8,128)(2,1)S(1)}, bf16[3072,128]{1,0:T(8,128)(2,1)S(1)}, u32[]{:S(2)}, u32[]{:S(2)}) collective-permute-start(bf16[3072,128]{1,0:T(8,128)(2,1)S(1)} %bitcast.7), channel_id=1, source_target_pairs={{0,4},{4,8},{8,12},{12,0},{1,5},{5,9},{9,13},{13,1},{2,6},{6,10},{... | collective-permute-start | bytes 2359304 | tf_op jit(solution)/shard_map/ppermute | solution.py:272
  81.2 13.1 %collective-permute-done.next_ref = bf16[3072,128]{1,0:T(8,128)(2,1)S(1)} collective-permute-done((bf16[3072,128]{1,0:T(8,128)(2,1)S(1)}, bf16[3072,128]{1,0:T(8,128)(2,1)S(1)}, u32[]{:S(2)}, u32[]{:S(2)}) %collective-permute-start) | collective-permute-done | bytes 786464 | tf_op jit(solution)/shard_map/ppermute | solution.py:273
  94.4 5.0 %collective-permute-done.1.last_ref = bf16[3072,128]{1,0:T(8,128)(2,1)S(1)} collective-permute-done((bf16[3072,128]{1,0:T(8,128)(2,1)S(1)}, bf16[3072,128]{1,0:T(8,128)(2,1)S(1)}, u32[]{:S(2)}, u32[]{:S(2)}) %collective-permute-start.1) | collective-permute-done | bytes 786464 | tf_op jit(solution)/shard_map/ppermute | solution.py:272
  99.4 2.2 %gram.1 = (f32[4,32,1024]{2,1,0:T(8,128)S(1)}, f32[136,1024]{1,0:T(8,128)S(1)}, f32[8,1024]{1,0:T(8,128)S(1)}) custom-call(s32[1]{0:T(128)} %bitcast.core_ref, bf16[3072,128]{1,0:T(8,128)(2,1)S(1)} %bitcast.8, bf16[3072,128]{1,0:T(8,128)(2,1)S(1)} %collective-permute-done.next_ref, bf16[3072,128]{1,0:T(8,128)(2,1)S(1)} %collective-permute-done.1.last_ref), custom_call_target="tpu_custom_call" | custom-call | tf_op jit(solution)/shard_map/gram/pallas_call | solution.py:187
  101.6 4.9 %collective-permute-start.2 = (f32[136,1024]{1,0:T(8,128)S(1)}, f32[136,1024]{1,0:T(8,128)S(1)}, u32[]{:S(2)}, u32[]{:S(2)}) collective-permute-start(f32[136,1024]{1,0:T(8,128)S(1)} %get-tuple-element.23), channel_id=1, source_target_pairs={{0,16},{16,0},{1,17},{17,1},{2,18},{18,2},{3,19},{19,3},{4,20},{20... | collective-permute-start | bytes 1671176 | tf_op jit(solution)/shard_map/ppermute | solution.py:275
  106.5 1.6 %collective-permute-done.2.got_ref = f32[136,1024]{1,0:T(8,128)S(1)} collective-permute-done((f32[136,1024]{1,0:T(8,128)S(1)}, f32[136,1024]{1,0:T(8,128)S(1)}, u32[]{:S(2)}, u32[]{:S(2)}) %collective-permute-start.2) | collective-permute-done | bytes 557088 | tf_op jit(solution)/shard_map/ppermute | solution.py:275
  108.1 1.0 scale.1
  109.0 1.9 %collective-permute-start.3 = (f32[4,32,256]{2,1,0:T(8,128)S(1)}, f32[4,32,256]{2,1,0:T(8,128)S(1)}, u32[]{:S(2)}, u32[]{:S(2)}) collective-permute-start(f32[4,32,256]{2,1,0:T(8,128)S(1)} %get-tuple-element.26), channel_id=1, source_target_pairs={{0,12},{4,0},{8,4},{12,8},{1,13},{5,1},{9,5},{13,9},{2,14},{6,2},{... | collective-permute-start | bytes 393224 | tf_op jit(solution)/shard_map/ppermute | solution.py:277
  110.9 4.6 %collective-permute-done.3 = f32[4,32,256]{2,1,0:T(8,128)S(1)} collective-permute-done((f32[4,32,256]{2,1,0:T(8,128)S(1)}, f32[4,32,256]{2,1,0:T(8,128)S(1)}, u32[]{:S(2)}, u32[]{:S(2)}) %collective-permute-start.3) | collective-permute-done | bytes 131104 | tf_op jit(solution)/shard_map/ppermute | solution.py:277
  115.6 0.7 constant_dynamic-update-slice_fusion
  116.2 4.1 %all-to-all-start.1 = ((f32[4,32,1024]{2,1,0:T(8,128)}), f32[4,32,1024]{2,1,0:T(8,128)S(1)}, u32[]{:S(2)}, u32[]{:S(2)}) async-start(f32[4,32,1024]{2,1,0:T(8,128)} %constant_dynamic-update-slice_fusion), calls=%async_computation.1 | async-start | bytes 1048576 | tf_op jit(solution)/shard_map/all_to_all | solution.py:278
  120.3 7.8 %all-to-all-done.1.rows_ref = f32[4,32,1024]{2,1,0:T(8,128)S(1)} async-done(((f32[4,32,1024]{2,1,0:T(8,128)}), f32[4,32,1024]{2,1,0:T(8,128)S(1)}, u32[]{:S(2)}, u32[]{:S(2)}) %all-to-all-start.1) | async-done | bytes 524320 | tf_op jit(solution)/shard_map/all_to_all | solution.py:278
  128.1 4.6 %collective-permute-start.4 = (f32[2,32,1024]{2,1,0:T(8,128)S(1)}, f32[2,32,1024]{2,1,0:T(8,128)S(1)}, u32[]{:S(2)}, u32[]{:S(2)}) collective-permute-start(f32[2,32,1024]{2,1,0:T(8,128)S(1)} %constant_dynamic-slice_fusion), channel_id=1, source_target_pairs={{0,16},{16,0},{1,17},{17,1},{2,18},{18,2},{3,19},{19,3},{4,20},{20... | collective-permute-start | bytes 786440 | tf_op jit(solution)/shard_map/ppermute | solution.py:279
  132.7 0.1 pad_add_fusion.at_ref
  132.8 1.1 collective-permute-done.4.got_ref
  133.8 1.4 %place.1 = f32[2,64,1024]{2,1,0:T(8,128)} custom-call(s32[2]{0:T(128)S(1)} %pad_add_fusion.at_ref, f32[4,32,1024]{2,1,0:T(8,128)S(1)} %all-to-all-done.1.rows_ref, f32[2,32,1024]{2,1,0:T(8,128)S(1)} %collective-permute-done.4.got_ref), custom_call_target="tpu_custom_call" | custom-call | tf_op jit(solution)/shard_map/place/pallas_call | solution.py:253
  (1 shorter events, 0.0 us)
Async XLA Ops:
  74.7 19.7 %collective-permute-start = (bf16[3072,128]{1,0:T(8,128)(2,1)S(1)}, bf16[3072,128]{1,0:T(8,128)(2,1)S(1)}, u32[]{:S(2)}, u32[]{:S(2)}) collective-permute-start(bf16[3072,128]{1,0:T(8,128)(2,1)S(1)} %bitcast.6), channel_id=1, source_target_pairs={{0,12},{4,0},{8,4},{12,8},{1,13},{5,1},{9,5},{13,9},{2,14},{6,2},{... | collective-permute-start | bytes 2359304 | tf_op jit(solution)/shard_map/ppermute | solution.py:273
  79.3 20.1 %collective-permute-start.1 = (bf16[3072,128]{1,0:T(8,128)(2,1)S(1)}, bf16[3072,128]{1,0:T(8,128)(2,1)S(1)}, u32[]{:S(2)}, u32[]{:S(2)}) collective-permute-start(bf16[3072,128]{1,0:T(8,128)(2,1)S(1)} %bitcast.7), channel_id=1, source_target_pairs={{0,4},{4,8},{8,12},{12,0},{1,5},{5,9},{9,13},{13,1},{2,6},{6,10},{... | collective-permute-start | bytes 2359304 | tf_op jit(solution)/shard_map/ppermute | solution.py:272
  101.6 6.4 %collective-permute-start.2 = (f32[136,1024]{1,0:T(8,128)S(1)}, f32[136,1024]{1,0:T(8,128)S(1)}, u32[]{:S(2)}, u32[]{:S(2)}) collective-permute-start(f32[136,1024]{1,0:T(8,128)S(1)} %get-tuple-element.23), channel_id=1, source_target_pairs={{0,16},{16,0},{1,17},{17,1},{2,18},{18,2},{3,19},{19,3},{4,20},{20... | collective-permute-start | bytes 1671176 | tf_op jit(solution)/shard_map/ppermute | solution.py:275
  109.0 6.6 %collective-permute-start.3 = (f32[4,32,256]{2,1,0:T(8,128)S(1)}, f32[4,32,256]{2,1,0:T(8,128)S(1)}, u32[]{:S(2)}, u32[]{:S(2)}) collective-permute-start(f32[4,32,256]{2,1,0:T(8,128)S(1)} %get-tuple-element.26), channel_id=1, source_target_pairs={{0,12},{4,0},{8,4},{12,8},{1,13},{5,1},{9,5},{13,9},{2,14},{6,2},{... | collective-permute-start | bytes 393224 | tf_op jit(solution)/shard_map/ppermute | solution.py:277
  116.2 11.9 %all-to-all-start.1 = ((f32[4,32,1024]{2,1,0:T(8,128)}), f32[4,32,1024]{2,1,0:T(8,128)S(1)}, u32[]{:S(2)}, u32[]{:S(2)}) async-start(f32[4,32,1024]{2,1,0:T(8,128)} %constant_dynamic-update-slice_fusion), calls=%async_computation.1 | async-start | bytes 1048576 | tf_op jit(solution)/shard_map/all_to_all | solution.py:278
  128.1 5.7 %collective-permute-start.4 = (f32[2,32,1024]{2,1,0:T(8,128)S(1)}, f32[2,32,1024]{2,1,0:T(8,128)S(1)}, u32[]{:S(2)}, u32[]{:S(2)}) collective-permute-start(f32[2,32,1024]{2,1,0:T(8,128)S(1)} %constant_dynamic-slice_fusion), channel_id=1, source_target_pairs={{0,16},{16,0},{1,17},{17,1},{2,18},{18,2},{3,19},{19,3},{4,20},{20... | collective-permute-start | bytes 786440 | tf_op jit(solution)/shard_map/ppermute | solution.py:279

commit v3 on v2

--- a/solution.py
+++ b/solution.py
@@ -196,7 +196,7 @@
     )(core, mine, after, prior)
 
 
-def scale_kernel(core_ref, keep_ref, got_ref, own_ref, rows_ref, far_ref):
+def scale_kernel(core_ref, keep_ref, got_ref, own_ref, rows_ref):
     first = core_ref[0] == 0
     sums = own_ref[...] + got_ref[128:, :]
     count = sums[0:1, 768:896]
@@ -220,44 +220,45 @@
             if group < 3:
                 rows_ref[x, :, lanes] = count * value / (mine[x] * sums[0:1, lanes])
             else:
-                value = count * value / (prior[x] * sums[0:1, 512:768])
-                rows_ref[x, :, lanes] = value
-                far_ref[x] = value
+                rows_ref[x, :, lanes] = count * value / (prior[x] * sums[0:1, 512:768])
 
 
 def scale(core, keep, got, own):
     f32 = jnp.float32
     return pl.pallas_call(
         scale_kernel,
-        out_shape=(jax.ShapeDtypeStruct((4, 32, 1024), f32),
-                   jax.ShapeDtypeStruct((4, 32, 256), f32)),
+        out_shape=jax.ShapeDtypeStruct((4, 32, 1024), f32),
         in_specs=[pl.BlockSpec(memory_space=pltpu.SMEM)] + [pl.BlockSpec(memory_space=pltpu.VMEM)] * 3,
-        out_specs=(pl.BlockSpec(memory_space=pltpu.VMEM),) * 2,
+        out_specs=pl.BlockSpec(memory_space=pltpu.VMEM),
         compiler_params=pltpu.CompilerParams(vmem_limit_bytes=8 << 20),
         name="scale",
     )(core, keep, got, own)
 
 
-def place_kernel(at_ref, rows_ref, got_ref, out_ref):
+def place_kernel(at_ref, rows_ref, swap_ref, far_ref, cross_ref, out_ref):
     core, row = at_ref[0], at_ref[1]
-    for b in range(2):
-        for group in range(4):
-            lanes = pl.ds(pl.multiple_of(lax.rem(row + 3 + group, 4) * 256, 256), 256)
-            out_ref[b, pl.ds(pl.multiple_of(core * 32, 32), 32), lanes] = (
-                rows_ref[2 * core + b, :, group * 256:(group + 1) * 256])
-            out_ref[b, pl.ds(pl.multiple_of((1 - core) * 32, 32), 32), lanes] = (
-                got_ref[b, :, group * 256:(group + 1) * 256])
-
-
-def place(at, rows, got):
+    own, other = (pl.ds(pl.multiple_of(c * 32, 32), 32) for c in (core, 1 - core))
+    for group in range(4):
+        lanes = pl.ds(pl.multiple_of(lax.rem(row + 3 + group, 4) * 256, 256), 256)
+        source = slice(group * 256, (group + 1) * 256)
+        for b in range(2):
+            if group < 3:
+                out_ref[b, own, lanes] = rows_ref[2 * core + b, :, source]
+                out_ref[b, other, lanes] = swap_ref[b, :, source]
+            else:
+                out_ref[b, own, lanes] = far_ref[b]
+                out_ref[b, other, lanes] = cross_ref[b]
+
+
+def place(at, rows, swap, far, cross):
     return pl.pallas_call(
         place_kernel,
         out_shape=jax.ShapeDtypeStruct((2, 64, 1024), jnp.float32),
-        in_specs=[pl.BlockSpec(memory_space=pltpu.SMEM)] + [pl.BlockSpec(memory_space=pltpu.VMEM)] * 2,
+        in_specs=[pl.BlockSpec(memory_space=pltpu.SMEM)] + [pl.BlockSpec(memory_space=pltpu.VMEM)] * 4,
         out_specs=pl.BlockSpec(memory_space=pltpu.VMEM),
         compiler_params=pltpu.CompilerParams(vmem_limit_bytes=8 << 20),
         name="place",
-    )(at, rows, got)
+    )(at, rows, swap, far, cross)
 
 
 def shift(size, step):
@@ -273,11 +274,12 @@
     after = lax.ppermute(mine, "y", shift(4, -1))
     keep, send, own = gram(core[None], mine, after, prior)
     got = lax.ppermute(send, "c", shift(2, 1))
-    rows, far = scale(core[None], keep, got, own)
-    far = lax.ppermute(far, "y", shift(4, -1))
-    rows = lax.all_to_all(rows.at[:, :, 768:].set(far), "x", 0, 0, tiled=True)
-    other = lax.ppermute(lax.dynamic_slice_in_dim(rows, 2 * (1 - core), 2, 0), "c", shift(2, 1))
-    return place(jnp.stack([core, row]), rows, other)
+    rows = lax.all_to_all(scale(core[None], keep, got, own), "x", 0, 0, tiled=True)
+    diagonal = [(c * 4 + y, (1 - c) * 4 + (y + 3) % 4) for c in range(2) for y in range(4)]
+    cross = lax.ppermute(lax.dynamic_slice(rows, (2 * (1 - core), 0, 768), (2, 32, 256)), ("c", "y"), diagonal)
+    far = lax.ppermute(lax.dynamic_slice(rows, (2 * core, 0, 768), (2, 32, 256)), "y", shift(4, -1))
+    swap = lax.ppermute(lax.dynamic_slice(rows, (2 * (1 - core), 0, 0), (2, 32, 768)), "c", shift(2, 1))
+    return place(jnp.stack([core, row]), rows, swap, far, cross)
 
 
 def solution(mesh):

time: 136 us -> 135 us (level)
    ppermute x2 -> x3, waiting for transfers between devices: 5.71 us -> 3.71 us  [the longest x1 2.11 us: shards(): lax.ppermute(lax.dynamic_slice(rows, (2 * (1 - core), 0, 768), (2, 32, 25...]
    ppermute x2 -> x3, starting transfers between devices: 6.48 us -> 7.26 us  [the longest x1 3.42 us: shards(): lax.ppermute(lax.dynamic_slice(rows, (2 * (1 - core), 0, 0), (2, 32, 768)...]
  transfers between devices with their start and end apart: 6 -> 7, of which waited for: 6 -> 6; matrix products, arithmetic and copies ran while one was open for 0% -> 0% of each run, Pallas kernels for 0% -> 0%
where the time goes in v3:
time: 135 us
  blocking collectives  63.7 us (47%)
  waiting for transfers between devices  32.4 us (24%)
  starting transfers between devices  22.8 us (17%)
  Pallas kernels  15.5 us (11%)
    all_to_all x1, blocking collectives, shards(): lax.all_to_all(packed, ('x', 'z', 'c'), 0, 0, tiled=True)  63.7 us
    ppermute x1, waiting for transfers between devices, shards(): after = lax.ppermute(mine, 'y', shift(4, -1))  13.1 us
    pallas_call x1, Pallas kernels, pack(): pl.pallas_call(pack_kernel, out_shape=jax.ShapeDtypeStruct((DESTS, PART,...  11 us
    all_to_all x1, waiting for transfers between devices, shards(): lax.all_to_all(scale(core[None], keep, got, own), 'x', 0, 0, tiled=True)  8.92 us
    ppermute x1, waiting for transfers between devices, shards(): prior = lax.ppermute(mine, 'y', shift(4, 1))  5.05 us
    ppermute x1, starting transfers between devices, shards(): got = lax.ppermute(send, 'c', shift(2, 1))  4.85 us
    ppermute x1, starting transfers between devices, shards(): after = lax.ppermute(mine, 'y', shift(4, -1))  4.63 us
    all_to_all x1, starting transfers between devices, shards(): lax.all_to_all(scale(core[None], keep, got, own), 'x', 0, 0, tiled=True)  4.1 us
  transfers between devices with their start and end apart: 7, of which 6 were waited for; matrix products, arithmetic and copies ran while one was open for 0% of the time, Pallas kernels for 0%

profile of v3, /device:TPU:1, one launch (start us, length us, event | category | flops | bytes accessed | tf_op | source)
XLA Modules:
  0.0 134.5 jit_solution(491240250613947694)
XLA Ops:
  0.0 11.0 %pack.1 = bf16[128,24,128]{2,1,0:T(8,128)(2,1)S(1)} custom-call(f32[16,64]{1,0:T(8,128)} %bitcast.10, s32[1,64]{1,0:T(1,128)} %bitcast.11, s32[64,128]{1,0:T(8,128)} %bitcast.9, bf16[16,8192]{1,0:T(8,128)(2,1)} %eigen_hbm.1, bf16[64,8192]{1,0:T(8,128)(2,1)} %raw_hbm.1), custom_call_target="tpu_custom_call" | custom-call | tf_op jit(solution)/shard_map/pack/pallas_call | solution.py:111
  11.0 63.7 %all_to_all.10 = bf16[128,24,128]{2,1,0:T(8,128)(2,1)S(1)} all-to-all(bf16[128,24,128]{2,1,0:T(8,128)(2,1)S(1)} %pack.1), channel_id=1, replica_groups=mesh['z'=16,'c'=2,'y'=4,'x'=4] {'x','z','c'}, dimensions={0} | all-to-all | bytes 1572864 | tf_op jit(solution)/shard_map/all_to_all | solution.py:272
  74.7 4.6 %collective-permute-start = (bf16[3072,128]{1,0:T(8,128)(2,1)S(1)}, bf16[3072,128]{1,0:T(8,128)(2,1)S(1)}, u32[]{:S(2)}, u32[]{:S(2)}) collective-permute-start(bf16[3072,128]{1,0:T(8,128)(2,1)S(1)} %bitcast.6), channel_id=1, source_target_pairs={{0,12},{4,0},{8,4},{12,8},{1,13},{5,1},{9,5},{13,9},{2,14},{6,2},{... | collective-permute-start | bytes 2359304 | tf_op jit(solution)/shard_map/ppermute | solution.py:274
  79.3 1.9 %collective-permute-start.1 = (bf16[3072,128]{1,0:T(8,128)(2,1)S(1)}, bf16[3072,128]{1,0:T(8,128)(2,1)S(1)}, u32[]{:S(2)}, u32[]{:S(2)}) collective-permute-start(bf16[3072,128]{1,0:T(8,128)(2,1)S(1)} %bitcast.7), channel_id=1, source_target_pairs={{0,4},{4,8},{8,12},{12,0},{1,5},{5,9},{9,13},{13,1},{2,6},{6,10},{... | collective-permute-start | bytes 2359304 | tf_op jit(solution)/shard_map/ppermute | solution.py:273
  81.2 13.1 %collective-permute-done.next_ref = bf16[3072,128]{1,0:T(8,128)(2,1)S(1)} collective-permute-done((bf16[3072,128]{1,0:T(8,128)(2,1)S(1)}, bf16[3072,128]{1,0:T(8,128)(2,1)S(1)}, u32[]{:S(2)}, u32[]{:S(2)}) %collective-permute-start) | collective-permute-done | bytes 786464 | tf_op jit(solution)/shard_map/ppermute | solution.py:274
  94.4 5.0 %collective-permute-done.1.last_ref = bf16[3072,128]{1,0:T(8,128)(2,1)S(1)} collective-permute-done((bf16[3072,128]{1,0:T(8,128)(2,1)S(1)}, bf16[3072,128]{1,0:T(8,128)(2,1)S(1)}, u32[]{:S(2)}, u32[]{:S(2)}) %collective-permute-start.1) | collective-permute-done | bytes 786464 | tf_op jit(solution)/shard_map/ppermute | solution.py:273
  99.4 2.2 %gram.1 = (f32[4,32,1024]{2,1,0:T(8,128)S(1)}, f32[136,1024]{1,0:T(8,128)S(1)}, f32[8,1024]{1,0:T(8,128)S(1)}) custom-call(s32[1]{0:T(128)} %bitcast.core_ref, bf16[3072,128]{1,0:T(8,128)(2,1)S(1)} %bitcast.8, bf16[3072,128]{1,0:T(8,128)(2,1)S(1)} %collective-permute-done.next_ref, bf16[3072,128]{1,0:T(8,128)(2,1)S(1)} %collective-permute-done.1.last_ref), custom_call_target="tpu_custom_call" | custom-call | tf_op jit(solution)/shard_map/gram/pallas_call | solution.py:187
  101.6 4.9 %collective-permute-start.2 = (f32[136,1024]{1,0:T(8,128)S(1)}, f32[136,1024]{1,0:T(8,128)S(1)}, u32[]{:S(2)}, u32[]{:S(2)}) collective-permute-start(f32[136,1024]{1,0:T(8,128)S(1)} %get-tuple-element.9), channel_id=1, source_target_pairs={{0,16},{16,0},{1,17},{17,1},{2,18},{18,2},{3,19},{19,3},{4,20},{20... | collective-permute-start | bytes 1671176 | tf_op jit(solution)/shard_map/ppermute | solution.py:276
  106.5 1.6 %collective-permute-done.2.got_ref = f32[136,1024]{1,0:T(8,128)S(1)} collective-permute-done((f32[136,1024]{1,0:T(8,128)S(1)}, f32[136,1024]{1,0:T(8,128)S(1)}, u32[]{:S(2)}, u32[]{:S(2)}) %collective-permute-start.2) | collective-permute-done | bytes 557088 | tf_op jit(solution)/shard_map/ppermute | solution.py:276
  108.1 1.0 scale.1
  109.0 4.1 %all-to-all-start.1 = ((f32[4,32,1024]{2,1,0:T(8,128)}), f32[4,32,1024]{2,1,0:T(8,128)S(1)}, u32[]{:S(2)}, u32[]{:S(2)}) async-start(f32[4,32,1024]{2,1,0:T(8,128)} %scale.1), calls=%async_computation.1 | async-start | bytes 1048576 | tf_op jit(solution)/shard_map/all_to_all | solution.py:277
  113.1 8.9 %all-to-all-done.1.rows_ref = f32[4,32,1024]{2,1,0:T(8,128)S(1)} async-done(((f32[4,32,1024]{2,1,0:T(8,128)}), f32[4,32,1024]{2,1,0:T(8,128)S(1)}, u32[]{:S(2)}, u32[]{:S(2)}) %all-to-all-start.1) | async-done | bytes 524320 | tf_op jit(solution)/shard_map/all_to_all | solution.py:277
  122.0 3.4 %collective-permute-start.3 = (f32[2,32,768]{2,1,0:T(8,128)S(1)}, f32[2,32,768]{2,1,0:T(8,128)S(1)}, u32[]{:S(2)}, u32[]{:S(2)}) collective-permute-start(f32[2,32,768]{2,1,0:T(8,128)S(1)} %constant_dynamic-slice_fusion.2), channel_id=1, source_target_pairs={{0,16},{16,0},{1,17},{17,1},{2,18},{18,2},{3,19},{19,3},{4,20},{20... | collective-permute-start | bytes 589832 | tf_op jit(solution)/shard_map/ppermute | solution.py:281
  125.5 1.9 %collective-permute-start.4 = (f32[2,32,256]{2,1,0:T(8,128)S(1)}, f32[2,32,256]{2,1,0:T(8,128)S(1)}, u32[]{:S(2)}, u32[]{:S(2)}) collective-permute-start(f32[2,32,256]{2,1,0:T(8,128)S(1)} %get-tuple-element.12), channel_id=1, source_target_pairs={{0,12},{4,0},{8,4},{12,8},{1,13},{5,1},{9,5},{13,9},{2,14},{6,2},{... | collective-permute-start | bytes 196616 | tf_op jit(solution)/shard_map/ppermute | solution.py:280
  127.4 1.9 %collective-permute-start.5 = (f32[2,32,256]{2,1,0:T(8,128)S(1)}, f32[2,32,256]{2,1,0:T(8,128)S(1)}, u32[]{:S(2)}, u32[]{:S(2)}) collective-permute-start(f32[2,32,256]{2,1,0:T(8,128)S(1)} %get-tuple-element.11), channel_id=1, source_target_pairs={{0,28},{4,16},{8,20},{12,24},{16,12},{20,0},{24,4},{28,8},{1,29},{... | collective-permute-start | bytes 196616 | tf_op jit(solution)/shard_map/ppermute | solution.py:279
  129.4 0.1 pad_add_fusion.at_ref
  129.4 1.6 %collective-permute-done.4.far_ref = f32[2,32,256]{2,1,0:T(8,128)S(1)} collective-permute-done((f32[2,32,256]{2,1,0:T(8,128)S(1)}, f32[2,32,256]{2,1,0:T(8,128)S(1)}, u32[]{:S(2)}, u32[]{:S(2)}) %collective-permute-start.4) | collective-permute-done | bytes 65568 | tf_op jit(solution)/shard_map/ppermute | solution.py:280
  131.0 2.1 %collective-permute-done.5.cross_ref = f32[2,32,256]{2,1,0:T(8,128)S(1)} collective-permute-done((f32[2,32,256]{2,1,0:T(8,128)S(1)}, f32[2,32,256]{2,1,0:T(8,128)S(1)}, u32[]{:S(2)}, u32[]{:S(2)}) %collective-permute-start.5) | collective-permute-done | bytes 65568 | tf_op jit(solution)/shard_map/ppermute | solution.py:279
  133.1 0.0 collective-permute-done.3.swap_ref
  133.1 1.4 %place.1 = f32[2,64,1024]{2,1,0:T(8,128)} custom-call(s32[2]{0:T(128)S(1)} %pad_add_fusion.at_ref, f32[4,32,1024]{2,1,0:T(8,128)S(1)} %all-to-all-done.1.rows_ref, f32[2,32,768]{2,1,0:T(8,128)S(1)} %collective-permute-done.3.swap_ref, f32[2,32,256]{2,1,0:T(8,128)S(1)} %collective-permute-done.4.far_ref, f32[2,32,256]{2,1,0:T(8,128)S(1)} %collective-permute-done.5.cross_ref), custom_call_target="tpu_custom_call" | custom-call | tf_op jit(solution)/shard_map/place/pallas_call | solution.py:254
  (2 shorter events, 0.0 us)
Async XLA Ops:
  74.7 19.7 %collective-permute-start = (bf16[3072,128]{1,0:T(8,128)(2,1)S(1)}, bf16[3072,128]{1,0:T(8,128)(2,1)S(1)}, u32[]{:S(2)}, u32[]{:S(2)}) collective-permute-start(bf16[3072,128]{1,0:T(8,128)(2,1)S(1)} %bitcast.6), channel_id=1, source_target_pairs={{0,12},{4,0},{8,4},{12,8},{1,13},{5,1},{9,5},{13,9},{2,14},{6,2},{... | collective-permute-start | bytes 2359304 | tf_op jit(solution)/shard_map/ppermute | solution.py:274
  79.3 20.1 %collective-permute-start.1 = (bf16[3072,128]{1,0:T(8,128)(2,1)S(1)}, bf16[3072,128]{1,0:T(8,128)(2,1)S(1)}, u32[]{:S(2)}, u32[]{:S(2)}) collective-permute-start(bf16[3072,128]{1,0:T(8,128)(2,1)S(1)} %bitcast.7), channel_id=1, source_target_pairs={{0,4},{4,8},{8,12},{12,0},{1,5},{5,9},{9,13},{13,1},{2,6},{6,10},{... | collective-permute-start | bytes 2359304 | tf_op jit(solution)/shard_map/ppermute | solution.py:273
  101.6 6.4 %collective-permute-start.2 = (f32[136,1024]{1,0:T(8,128)S(1)}, f32[136,1024]{1,0:T(8,128)S(1)}, u32[]{:S(2)}, u32[]{:S(2)}) collective-permute-start(f32[136,1024]{1,0:T(8,128)S(1)} %get-tuple-element.9), channel_id=1, source_target_pairs={{0,16},{16,0},{1,17},{17,1},{2,18},{18,2},{3,19},{19,3},{4,20},{20... | collective-permute-start | bytes 1671176 | tf_op jit(solution)/shard_map/ppermute | solution.py:276
  109.0 13.0 %all-to-all-start.1 = ((f32[4,32,1024]{2,1,0:T(8,128)}), f32[4,32,1024]{2,1,0:T(8,128)S(1)}, u32[]{:S(2)}, u32[]{:S(2)}) async-start(f32[4,32,1024]{2,1,0:T(8,128)} %scale.1), calls=%async_computation.1 | async-start | bytes 1048576 | tf_op jit(solution)/shard_map/all_to_all | solution.py:277
  122.0 11.1 %collective-permute-start.3 = (f32[2,32,768]{2,1,0:T(8,128)S(1)}, f32[2,32,768]{2,1,0:T(8,128)S(1)}, u32[]{:S(2)}, u32[]{:S(2)}) collective-permute-start(f32[2,32,768]{2,1,0:T(8,128)S(1)} %constant_dynamic-slice_fusion.2), channel_id=1, source_target_pairs={{0,16},{16,0},{1,17},{17,1},{2,18},{18,2},{3,19},{19,3},{4,20},{20... | collective-permute-start | bytes 589832 | tf_op jit(solution)/shard_map/ppermute | solution.py:281
  125.5 5.5 %collective-permute-start.4 = (f32[2,32,256]{2,1,0:T(8,128)S(1)}, f32[2,32,256]{2,1,0:T(8,128)S(1)}, u32[]{:S(2)}, u32[]{:S(2)}) collective-permute-start(f32[2,32,256]{2,1,0:T(8,128)S(1)} %get-tuple-element.12), channel_id=1, source_target_pairs={{0,12},{4,0},{8,4},{12,8},{1,13},{5,1},{9,5},{13,9},{2,14},{6,2},{... | collective-permute-start | bytes 196616 | tf_op jit(solution)/shard_map/ppermute | solution.py:280
  127.4 5.7 %collective-permute-start.5 = (f32[2,32,256]{2,1,0:T(8,128)S(1)}, f32[2,32,256]{2,1,0:T(8,128)S(1)}, u32[]{:S(2)}, u32[]{:S(2)}) collective-permute-start(f32[2,32,256]{2,1,0:T(8,128)S(1)} %get-tuple-element.11), channel_id=1, source_target_pairs={{0,28},{4,16},{8,20},{12,24},{16,12},{20,0},{24,4},{28,8},{1,29},{... | collective-permute-start | bytes 196616 | tf_op jit(solution)/shard_map/ppermute | solution.py:279

commit v4 on v3

--- a/solution.py
+++ b/solution.py
@@ -11,6 +11,9 @@
 BINS = 64
 CHUNK = 256
 CHUNKS = PIXELS // CHUNK
+STEP = 512
+STEPS = PIXELS // STEP
+DEEP = 4
 SLOTS = BINS * CAP
 PART = 24
 DESTS = 128
@@ -19,7 +22,7 @@
 
 def pack_kernel(weights_hbm, used_hbm, bins_hbm, eigen_hbm, raw_hbm, out_ref,
                 weights_ref, used_ref, bins_ref, eigen_ref, raw_ref,
-                hot_ref, cum_ref, row_ref, place_ref, even_ref, odd_ref, slot_ref, sems):
+                hot_ref, cum_ref, row_ref, place0, place1, place2, place3, even_ref, odd_ref, slot_ref, sems):
     f32, bf16 = jnp.float32, jnp.bfloat16
     sources = (bins_hbm, eigen_hbm, weights_hbm, used_hbm, raw_hbm)
     targets = (bins_ref, eigen_ref, weights_ref, used_ref, raw_ref)
@@ -53,8 +56,14 @@
             row_ref[2 * j + h:2 * j + h + 1, :] = jnp.where(
                 own > 0, (own - 1) * CAP + rank.astype(jnp.int32), SLOTS)
         carry = carry + cum_ref[rows, CHUNK:]
-    copy = pltpu.make_async_copy(row_ref, place_ref, sems.at[5])
-    copy.start()
+    places, values = (place0, place1, place2, place3), (even_ref, odd_ref)
+
+    def fetch(j, k):
+        rows = pl.ds(pl.multiple_of(j * (STEP // 128), STEP // 128), STEP // 128)
+        return pltpu.make_async_copy(row_ref.at[rows, :], places[k], sems.at[5 + k])
+
+    for k in range(DEEP):
+        fetch(k, k).start()
     for load in loads[1:]:
         load.wait()
 
@@ -67,32 +76,30 @@
     weights = jnp.concatenate([high.astype(f32), mid.astype(f32), low.astype(f32)], axis=0).T.astype(bf16)
 
     def correct(j, target):
-        at = pl.ds(pl.multiple_of(j * CHUNK, CHUNK), CHUNK)
+        at = pl.ds(pl.multiple_of(j * STEP, STEP), STEP)
         flats = eigen_ref[:, at]
         field = 0.5 + jnp.dot(weights, jnp.concatenate([flats] * 3, axis=0), preferred_element_type=f32)
         value = (raw_ref[:, at].astype(f32) / field).astype(bf16).astype(f32)
-        for h in range(2):
-            half = value[:, h * 128:(h + 1) * 128]
-            target[h * 128:(h + 1) * 128, :] = jnp.concatenate([half, half], axis=0).T
-
-    def scatter(j, source):
-        for h in range(2):
-            for i in range(128):
-                place = place_ref[2 * j + h, i]
-                slot_ref[pl.ds(place, 1), :] = source[h * 128 + i:h * 128 + i + 1, :]
+        for h in range(STEP // 128):
+            part = value[:, h * 128:(h + 1) * 128]
+            target[h * 128:(h + 1) * 128, :] = jnp.concatenate([part, part], axis=0).T
+
+    def scatter(source, place_ref):
+        for i in range(STEP):
+            slot_ref[pl.ds(place_ref[i // 128, i % 128], 1), :] = source[i:i + 1, :]
 
     correct(0, even_ref)
-    copy.wait()
-
-    @pl.loop(0, CHUNKS // 2 - 1)
+
+    @pl.loop(0, STEPS // DEEP)
     def _(i):
-        scatter(2 * i, even_ref)
-        correct(2 * i + 1, odd_ref)
-        scatter(2 * i + 1, odd_ref)
-        correct(2 * i + 2, even_ref)
-    scatter(CHUNKS - 2, even_ref)
-    correct(CHUNKS - 1, odd_ref)
-    scatter(CHUNKS - 1, odd_ref)
+        for k in range(DEEP):
+            fetch(DEEP * i + k, k).wait()
+            scatter(values[k % 2], places[k])
+
+            @pl.when(i < STEPS // DEEP - 1)
+            def _():
+                fetch(DEEP * (i + 1) + k, k).start()
+            correct(jnp.minimum(DEEP * i + k + 1, STEPS - 1), values[(k + 1) % 2])
 
     left = lax.broadcasted_iota(jnp.int32, (PART, 128), 1) < FRAMES
 
@@ -122,11 +129,11 @@
             pltpu.VMEM((CHUNKS * BINS, CHUNK), jnp.bfloat16),
             pltpu.VMEM((CHUNKS * BINS, CHUNK + 128), f32),
             pltpu.VMEM((PIXELS // 128, 128), jnp.int32),
-            pltpu.SMEM((PIXELS // 128, 128), jnp.int32),
-            pltpu.VMEM((CHUNK, 128), f32),
-            pltpu.VMEM((CHUNK, 128), f32),
+            *[pltpu.SMEM((STEP // 128, 128), jnp.int32)] * DEEP,
+            pltpu.VMEM((STEP, 128), f32),
+            pltpu.VMEM((STEP, 128), f32),
             pltpu.VMEM((SLOTS + 8, 128), f32),
-            pltpu.SemaphoreType.DMA((6,)),
+            pltpu.SemaphoreType.DMA((5 + DEEP,)),
         ],
         compiler_params=pltpu.CompilerParams(vmem_limit_bytes=24 << 20),
         name="pack",

time: 135 us -> 131 us (0.970)
  Pallas kernels: 15.5 us -> 11.7 us
    pallas_call x1, Pallas kernels: 11 us -> 7.19 us  [pack(): pl.pallas_call(pack_kernel, out_shape=jax.ShapeDtypeStruct((DESTS, PART,...]
where the time goes in v4:
time: 131 us
  blocking collectives  63.7 us (49%)
  waiting for transfers between devices  32.4 us (25%)
  starting transfers between devices  22.8 us (17%)
  Pallas kernels  11.7 us (9%)
    all_to_all x1, blocking collectives, shards(): lax.all_to_all(packed, ('x', 'z', 'c'), 0, 0, tiled=True)  63.7 us
    ppermute x1, waiting for transfers between devices, shards(): after = lax.ppermute(mine, 'y', shift(4, -1))  13.1 us
    all_to_all x1, waiting for transfers between devices, shards(): lax.all_to_all(scale(core[None], keep, got, own), 'x', 0, 0, tiled=True)  8.92 us
    pallas_call x1, Pallas kernels, pack(): pl.pallas_call(pack_kernel, out_shape=jax.ShapeDtypeStruct((DESTS, PART,...  7.19 us
    ppermute x1, waiting for transfers between devices, shards(): prior = lax.ppermute(mine, 'y', shift(4, 1))  5.05 us
    ppermute x1, starting transfers between devices, shards(): got = lax.ppermute(send, 'c', shift(2, 1))  4.86 us
    ppermute x1, starting transfers between devices, shards(): after = lax.ppermute(mine, 'y', shift(4, -1))  4.63 us
    all_to_all x1, starting transfers between devices, shards(): lax.all_to_all(scale(core[None], keep, got, own), 'x', 0, 0, tiled=True)  4.1 us
  transfers between devices with their start and end apart: 7, of which 6 were waited for; matrix products, arithmetic and copies ran while one was open for 0% of the time, Pallas kernels for 0%

profile of v4, /device:TPU:1, one launch (start us, length us, event | category | flops | bytes accessed | tf_op | source)
XLA Modules:
  0.0 130.7 jit_solution(8053442428420018321)
XLA Ops:
  0.0 7.2 %pack.1 = bf16[128,24,128]{2,1,0:T(8,128)(2,1)S(1)} custom-call(f32[16,64]{1,0:T(8,128)} %bitcast.10, s32[1,64]{1,0:T(1,128)} %bitcast.11, s32[64,128]{1,0:T(8,128)} %bitcast.9, bf16[16,8192]{1,0:T(8,128)(2,1)} %eigen_hbm.1, bf16[64,8192]{1,0:T(8,128)(2,1)} %raw_hbm.1), custom_call_target="tpu_custom_call" | custom-call | tf_op jit(solution)/shard_map/pack/pallas_call | solution.py:118
  7.2 63.7 %all_to_all.10 = bf16[128,24,128]{2,1,0:T(8,128)(2,1)S(1)} all-to-all(bf16[128,24,128]{2,1,0:T(8,128)(2,1)S(1)} %pack.1), channel_id=1, replica_groups=mesh['z'=16,'c'=2,'y'=4,'x'=4] {'x','z','c'}, dimensions={0} | all-to-all | bytes 1572864 | tf_op jit(solution)/shard_map/all_to_all | solution.py:279
  70.9 4.6 %collective-permute-start = (bf16[3072,128]{1,0:T(8,128)(2,1)S(1)}, bf16[3072,128]{1,0:T(8,128)(2,1)S(1)}, u32[]{:S(2)}, u32[]{:S(2)}) collective-permute-start(bf16[3072,128]{1,0:T(8,128)(2,1)S(1)} %bitcast.6), channel_id=1, source_target_pairs={{0,12},{4,0},{8,4},{12,8},{1,13},{5,1},{9,5},{13,9},{2,14},{6,2},{... | collective-permute-start | bytes 2359304 | tf_op jit(solution)/shard_map/ppermute | solution.py:281
  75.5 1.9 %collective-permute-start.1 = (bf16[3072,128]{1,0:T(8,128)(2,1)S(1)}, bf16[3072,128]{1,0:T(8,128)(2,1)S(1)}, u32[]{:S(2)}, u32[]{:S(2)}) collective-permute-start(bf16[3072,128]{1,0:T(8,128)(2,1)S(1)} %bitcast.7), channel_id=1, source_target_pairs={{0,4},{4,8},{8,12},{12,0},{1,5},{5,9},{9,13},{13,1},{2,6},{6,10},{... | collective-permute-start | bytes 2359304 | tf_op jit(solution)/shard_map/ppermute | solution.py:280
  77.4 13.1 %collective-permute-done.next_ref = bf16[3072,128]{1,0:T(8,128)(2,1)S(1)} collective-permute-done((bf16[3072,128]{1,0:T(8,128)(2,1)S(1)}, bf16[3072,128]{1,0:T(8,128)(2,1)S(1)}, u32[]{:S(2)}, u32[]{:S(2)}) %collective-permute-start) | collective-permute-done | bytes 786464 | tf_op jit(solution)/shard_map/ppermute | solution.py:281
  90.6 5.0 %collective-permute-done.1.last_ref = bf16[3072,128]{1,0:T(8,128)(2,1)S(1)} collective-permute-done((bf16[3072,128]{1,0:T(8,128)(2,1)S(1)}, bf16[3072,128]{1,0:T(8,128)(2,1)S(1)}, u32[]{:S(2)}, u32[]{:S(2)}) %collective-permute-start.1) | collective-permute-done | bytes 786464 | tf_op jit(solution)/shard_map/ppermute | solution.py:280
  95.6 2.2 %gram.1 = (f32[4,32,1024]{2,1,0:T(8,128)S(1)}, f32[136,1024]{1,0:T(8,128)S(1)}, f32[8,1024]{1,0:T(8,128)S(1)}) custom-call(s32[1]{0:T(128)} %bitcast.core_ref, bf16[3072,128]{1,0:T(8,128)(2,1)S(1)} %bitcast.8, bf16[3072,128]{1,0:T(8,128)(2,1)S(1)} %collective-permute-done.next_ref, bf16[3072,128]{1,0:T(8,128)(2,1)S(1)} %collective-permute-done.1.last_ref), custom_call_target="tpu_custom_call" | custom-call | tf_op jit(solution)/shard_map/gram/pallas_call | solution.py:194
  97.8 4.9 %collective-permute-start.2 = (f32[136,1024]{1,0:T(8,128)S(1)}, f32[136,1024]{1,0:T(8,128)S(1)}, u32[]{:S(2)}, u32[]{:S(2)}) collective-permute-start(f32[136,1024]{1,0:T(8,128)S(1)} %get-tuple-element.9), channel_id=1, source_target_pairs={{0,16},{16,0},{1,17},{17,1},{2,18},{18,2},{3,19},{19,3},{4,20},{20... | collective-permute-start | bytes 1671176 | tf_op jit(solution)/shard_map/ppermute | solution.py:283
  102.7 1.6 %collective-permute-done.2.got_ref = f32[136,1024]{1,0:T(8,128)S(1)} collective-permute-done((f32[136,1024]{1,0:T(8,128)S(1)}, f32[136,1024]{1,0:T(8,128)S(1)}, u32[]{:S(2)}, u32[]{:S(2)}) %collective-permute-start.2) | collective-permute-done | bytes 557088 | tf_op jit(solution)/shard_map/ppermute | solution.py:283
  104.2 1.0 scale.1
  105.2 4.1 %all-to-all-start.1 = ((f32[4,32,1024]{2,1,0:T(8,128)}), f32[4,32,1024]{2,1,0:T(8,128)S(1)}, u32[]{:S(2)}, u32[]{:S(2)}) async-start(f32[4,32,1024]{2,1,0:T(8,128)} %scale.1), calls=%async_computation.1 | async-start | bytes 1048576 | tf_op jit(solution)/shard_map/all_to_all | solution.py:284
  109.3 8.9 %all-to-all-done.1.rows_ref = f32[4,32,1024]{2,1,0:T(8,128)S(1)} async-done(((f32[4,32,1024]{2,1,0:T(8,128)}), f32[4,32,1024]{2,1,0:T(8,128)S(1)}, u32[]{:S(2)}, u32[]{:S(2)}) %all-to-all-start.1) | async-done | bytes 524320 | tf_op jit(solution)/shard_map/all_to_all | solution.py:284
  118.2 3.4 %collective-permute-start.3 = (f32[2,32,768]{2,1,0:T(8,128)S(1)}, f32[2,32,768]{2,1,0:T(8,128)S(1)}, u32[]{:S(2)}, u32[]{:S(2)}) collective-permute-start(f32[2,32,768]{2,1,0:T(8,128)S(1)} %constant_dynamic-slice_fusion.2), channel_id=1, source_target_pairs={{0,16},{16,0},{1,17},{17,1},{2,18},{18,2},{3,19},{19,3},{4,20},{20... | collective-permute-start | bytes 589832 | tf_op jit(solution)/shard_map/ppermute | solution.py:288
  121.7 1.9 %collective-permute-start.4 = (f32[2,32,256]{2,1,0:T(8,128)S(1)}, f32[2,32,256]{2,1,0:T(8,128)S(1)}, u32[]{:S(2)}, u32[]{:S(2)}) collective-permute-start(f32[2,32,256]{2,1,0:T(8,128)S(1)} %get-tuple-element.12), channel_id=1, source_target_pairs={{0,12},{4,0},{8,4},{12,8},{1,13},{5,1},{9,5},{13,9},{2,14},{6,2},{... | collective-permute-start | bytes 196616 | tf_op jit(solution)/shard_map/ppermute | solution.py:287
  123.6 1.9 %collective-permute-start.5 = (f32[2,32,256]{2,1,0:T(8,128)S(1)}, f32[2,32,256]{2,1,0:T(8,128)S(1)}, u32[]{:S(2)}, u32[]{:S(2)}) collective-permute-start(f32[2,32,256]{2,1,0:T(8,128)S(1)} %get-tuple-element.11), channel_id=1, source_target_pairs={{0,28},{4,16},{8,20},{12,24},{16,12},{20,0},{24,4},{28,8},{1,29},{... | collective-permute-start | bytes 196616 | tf_op jit(solution)/shard_map/ppermute | solution.py:286
  125.5 0.1 pad_add_fusion.at_ref
  125.6 1.6 %collective-permute-done.4.far_ref = f32[2,32,256]{2,1,0:T(8,128)S(1)} collective-permute-done((f32[2,32,256]{2,1,0:T(8,128)S(1)}, f32[2,32,256]{2,1,0:T(8,128)S(1)}, u32[]{:S(2)}, u32[]{:S(2)}) %collective-permute-start.4) | collective-permute-done | bytes 65568 | tf_op jit(solution)/shard_map/ppermute | solution.py:287
  127.2 2.1 %collective-permute-done.5.cross_ref = f32[2,32,256]{2,1,0:T(8,128)S(1)} collective-permute-done((f32[2,32,256]{2,1,0:T(8,128)S(1)}, f32[2,32,256]{2,1,0:T(8,128)S(1)}, u32[]{:S(2)}, u32[]{:S(2)}) %collective-permute-start.5) | collective-permute-done | bytes 65568 | tf_op jit(solution)/shard_map/ppermute | solution.py:286
  129.3 0.0 collective-permute-done.3.swap_ref
  129.3 1.4 %place.1 = f32[2,64,1024]{2,1,0:T(8,128)} custom-call(s32[2]{0:T(128)S(1)} %pad_add_fusion.at_ref, f32[4,32,1024]{2,1,0:T(8,128)S(1)} %all-to-all-done.1.rows_ref, f32[2,32,768]{2,1,0:T(8,128)S(1)} %collective-permute-done.3.swap_ref, f32[2,32,256]{2,1,0:T(8,128)S(1)} %collective-permute-done.4.far_ref, f32[2,32,256]{2,1,0:T(8,128)S(1)} %collective-permute-done.5.cross_ref), custom_call_target="tpu_custom_call" | custom-call | tf_op jit(solution)/shard_map/place/pallas_call | solution.py:261
  (2 shorter events, 0.0 us)
Async XLA Ops:
  70.9 19.7 %collective-permute-start = (bf16[3072,128]{1,0:T(8,128)(2,1)S(1)}, bf16[3072,128]{1,0:T(8,128)(2,1)S(1)}, u32[]{:S(2)}, u32[]{:S(2)}) collective-permute-start(bf16[3072,128]{1,0:T(8,128)(2,1)S(1)} %bitcast.6), channel_id=1, source_target_pairs={{0,12},{4,0},{8,4},{12,8},{1,13},{5,1},{9,5},{13,9},{2,14},{6,2},{... | collective-permute-start | bytes 2359304 | tf_op jit(solution)/shard_map/ppermute | solution.py:281
  75.5 20.1 %collective-permute-start.1 = (bf16[3072,128]{1,0:T(8,128)(2,1)S(1)}, bf16[3072,128]{1,0:T(8,128)(2,1)S(1)}, u32[]{:S(2)}, u32[]{:S(2)}) collective-permute-start(bf16[3072,128]{1,0:T(8,128)(2,1)S(1)} %bitcast.7), channel_id=1, source_target_pairs={{0,4},{4,8},{8,12},{12,0},{1,5},{5,9},{9,13},{13,1},{2,6},{6,10},{... | collective-permute-start | bytes 2359304 | tf_op jit(solution)/shard_map/ppermute | solution.py:280
  97.8 6.4 %collective-permute-start.2 = (f32[136,1024]{1,0:T(8,128)S(1)}, f32[136,1024]{1,0:T(8,128)S(1)}, u32[]{:S(2)}, u32[]{:S(2)}) collective-permute-start(f32[136,1024]{1,0:T(8,128)S(1)} %get-tuple-element.9), channel_id=1, source_target_pairs={{0,16},{16,0},{1,17},{17,1},{2,18},{18,2},{3,19},{19,3},{4,20},{20... | collective-permute-start | bytes 1671176 | tf_op jit(solution)/shard_map/ppermute | solution.py:283
  105.2 13.0 %all-to-all-start.1 = ((f32[4,32,1024]{2,1,0:T(8,128)}), f32[4,32,1024]{2,1,0:T(8,128)S(1)}, u32[]{:S(2)}, u32[]{:S(2)}) async-start(f32[4,32,1024]{2,1,0:T(8,128)} %scale.1), calls=%async_computation.1 | async-start | bytes 1048576 | tf_op jit(solution)/shard_map/all_to_all | solution.py:284
  118.2 11.1 %collective-permute-start.3 = (f32[2,32,768]{2,1,0:T(8,128)S(1)}, f32[2,32,768]{2,1,0:T(8,128)S(1)}, u32[]{:S(2)}, u32[]{:S(2)}) collective-permute-start(f32[2,32,768]{2,1,0:T(8,128)S(1)} %constant_dynamic-slice_fusion.2), channel_id=1, source_target_pairs={{0,16},{16,0},{1,17},{17,1},{2,18},{18,2},{3,19},{19,3},{4,20},{20... | collective-permute-start | bytes 589832 | tf_op jit(solution)/shard_map/ppermute | solution.py:288
  121.7 5.5 %collective-permute-start.4 = (f32[2,32,256]{2,1,0:T(8,128)S(1)}, f32[2,32,256]{2,1,0:T(8,128)S(1)}, u32[]{:S(2)}, u32[]{:S(2)}) collective-permute-start(f32[2,32,256]{2,1,0:T(8,128)S(1)} %get-tuple-element.12), channel_id=1, source_target_pairs={{0,12},{4,0},{8,4},{12,8},{1,13},{5,1},{9,5},{13,9},{2,14},{6,2},{... | collective-permute-start | bytes 196616 | tf_op jit(solution)/shard_map/ppermute | solution.py:287
  123.6 5.7 %collective-permute-start.5 = (f32[2,32,256]{2,1,0:T(8,128)S(1)}, f32[2,32,256]{2,1,0:T(8,128)S(1)}, u32[]{:S(2)}, u32[]{:S(2)}) collective-permute-start(f32[2,32,256]{2,1,0:T(8,128)S(1)} %get-tuple-element.11), channel_id=1, source_target_pairs={{0,28},{4,16},{8,20},{12,24},{16,12},{20,0},{24,4},{28,8},{1,29},{... | collective-permute-start | bytes 196616 | tf_op jit(solution)/shard_map/ppermute | solution.py:286

commit v5 on v4

--- a/solution.py
+++ b/solution.py
@@ -15,9 +15,9 @@
 STEPS = PIXELS // STEP
 DEEP = 4
 SLOTS = BINS * CAP
-PART = 24
-DESTS = 128
-DEPTH = 32 * PART
+PART = CAP // 2
+DESTS = 64
+DEPTH = 16 * PART
 
 
 def pack_kernel(weights_hbm, used_hbm, bins_hbm, eigen_hbm, raw_hbm, out_ref,
@@ -106,11 +106,10 @@
     @pl.loop(0, BINS // 4)
     def _(z):
         for x in range(4):
-            for c in range(2):
-                base = (4 * z + x) * CAP + c * 2 * PART
-                lo = slot_ref[pl.ds(pl.multiple_of(base, 8), PART), :]
-                hi = slot_ref[pl.ds(pl.multiple_of(base + PART, 8), PART), :]
-                out_ref[x * 32 + 2 * z + c] = jnp.where(left, lo, hi).astype(bf16)
+            base = (4 * z + x) * CAP
+            lo = slot_ref[pl.ds(pl.multiple_of(base, 8), PART), :]
+            hi = slot_ref[pl.ds(pl.multiple_of(base + PART, 8), PART), :]
+            out_ref[x * 16 + z] = jnp.where(left, lo, hi).astype(bf16)
 
 
 def pack(weights, used, bins, eigen, raw):
@@ -242,7 +241,7 @@
     )(core, keep, got, own)
 
 
-def place_kernel(at_ref, rows_ref, swap_ref, far_ref, cross_ref, out_ref):
+def place_kernel(at_ref, rows_ref, swap_ref, far_ref, out_ref):
     core, row = at_ref[0], at_ref[1]
     own, other = (pl.ds(pl.multiple_of(c * 32, 32), 32) for c in (core, 1 - core))
     for group in range(4):
@@ -254,18 +253,18 @@
                 out_ref[b, other, lanes] = swap_ref[b, :, source]
             else:
                 out_ref[b, own, lanes] = far_ref[b]
-                out_ref[b, other, lanes] = cross_ref[b]
-
-
-def place(at, rows, swap, far, cross):
+                out_ref[b, other, lanes] = far_ref[2 + b]
+
+
+def place(at, rows, swap, far):
     return pl.pallas_call(
         place_kernel,
         out_shape=jax.ShapeDtypeStruct((2, 64, 1024), jnp.float32),
-        in_specs=[pl.BlockSpec(memory_space=pltpu.SMEM)] + [pl.BlockSpec(memory_space=pltpu.VMEM)] * 4,
+        in_specs=[pl.BlockSpec(memory_space=pltpu.SMEM)] + [pl.BlockSpec(memory_space=pltpu.VMEM)] * 3,
         out_specs=pl.BlockSpec(memory_space=pltpu.VMEM),
         compiler_params=pltpu.CompilerParams(vmem_limit_bytes=8 << 20),
         name="place",
-    )(at, rows, swap, far, cross)
+    )(at, rows, swap, far)
 
 
 def shift(size, step):
@@ -276,17 +275,16 @@
     core = lax.axis_index("c").astype(jnp.int32)
     row = lax.axis_index("y").astype(jnp.int32)
     packed = pack(weights.T, flat_count[None, :], bin_map.reshape(PIXELS // 128, 128), eigen_flats, raw_frames)
-    mine = lax.all_to_all(packed, ("x", "z", "c"), 0, 0, tiled=True).reshape(4 * DEPTH, 128)
+    mine = lax.all_to_all(packed, ("x", "z"), 0, 0, tiled=True).reshape(4 * DEPTH, 128)
     prior = lax.ppermute(mine, "y", shift(4, 1))
     after = lax.ppermute(mine, "y", shift(4, -1))
     keep, send, own = gram(core[None], mine, after, prior)
     got = lax.ppermute(send, "c", shift(2, 1))
     rows = lax.all_to_all(scale(core[None], keep, got, own), "x", 0, 0, tiled=True)
-    diagonal = [(c * 4 + y, (1 - c) * 4 + (y + 3) % 4) for c in range(2) for y in range(4)]
-    cross = lax.ppermute(lax.dynamic_slice(rows, (2 * (1 - core), 0, 768), (2, 32, 256)), ("c", "y"), diagonal)
-    far = lax.ppermute(lax.dynamic_slice(rows, (2 * core, 0, 768), (2, 32, 256)), "y", shift(4, -1))
-    swap = lax.ppermute(lax.dynamic_slice(rows, (2 * (1 - core), 0, 0), (2, 32, 768)), "c", shift(2, 1))
-    return place(jnp.stack([core, row]), rows, swap, far, cross)
+    swap = lax.ppermute(lax.dynamic_slice_in_dim(rows, 2 * (1 - core), 2, 0), "c", shift(2, 1))
+    far = jnp.concatenate([lax.dynamic_slice(rows, (2 * core, 0, 768), (2, 32, 256)), swap[:, :, 768:]], axis=0)
+    far = lax.ppermute(far, "y", shift(4, -1))
+    return place(jnp.stack([core, row]), rows, swap, far)
 
 
 def solution(mesh):

time: 131 us -> 127 us (0.969)
  blocking collectives: 63.7 us -> 58.8 us
    all_to_all x1, blocking collectives: 63.7 us -> 58.8 us  [shards(): lax.all_to_all(packed, ('x', 'z'), 0, 0, tiled=True).reshape(4 * DEPTH, 128)]
    ppermute x1, waiting for transfers between devices: 13.1 us -> 11 us  [shards(): after = lax.ppermute(mine, 'y', shift(4, -1))]
    ppermute x1, starting transfers between devices: 4.86 us -> 6.99 us  [shards(): got = lax.ppermute(send, 'c', shift(2, 1))]
    ppermute x3 -> x2, waiting for transfers between devices: 3.71 us -> 5.69 us  [the longest x1 4.57 us: shards(): far = lax.ppermute(far, 'y', shift(4, -1))]
    ppermute x3 -> x2, starting transfers between devices: 7.26 us -> 5.34 us  [the longest x1 3.42 us: shards(): lax.ppermute(lax.dynamic_slice_in_dim(rows, 2 * (1 - core), 2, 0), 'c', s...]
  transfers between devices with their start and end apart: 7 -> 6, of which waited for: 6 -> 6; matrix products, arithmetic and copies ran while one was open for 0% -> 0% of each run, Pallas kernels for 0% -> 0%
where the time goes in v5:
time: 127 us; the launch traced here: 126 us
  blocking collectives  58.8 us (46%)
  waiting for transfers between devices  32.2 us (25%)
  starting transfers between devices  23 us (18%)
  Pallas kernels  11.7 us (9%)
    all_to_all x1, blocking collectives, shards(): lax.all_to_all(packed, ('x', 'z'), 0, 0, tiled=True).reshape(4 * DEPTH, 128)  58.8 us
    ppermute x1, waiting for transfers between devices, shards(): after = lax.ppermute(mine, 'y', shift(4, -1))  11 us
    all_to_all x1, waiting for transfers between devices, shards(): lax.all_to_all(scale(core[None], keep, got, own), 'x', 0, 0, tiled=True)  8.92 us
    pallas_call x1, Pallas kernels, pack(): pl.pallas_call(pack_kernel, out_shape=jax.ShapeDtypeStruct((DESTS, PART,...  7.18 us
    ppermute x1, starting transfers between devices, shards(): got = lax.ppermute(send, 'c', shift(2, 1))  6.99 us
    ppermute x1, waiting for transfers between devices, shards(): prior = lax.ppermute(mine, 'y', shift(4, 1))  5.05 us
    ppermute x1, starting transfers between devices, shards(): after = lax.ppermute(mine, 'y', shift(4, -1))  4.62 us
    ppermute x1, waiting for transfers between devices, shards(): far = lax.ppermute(far, 'y', shift(4, -1))  4.57 us
  transfers between devices with their start and end apart: 6, of which 6 were waited for; matrix products, arithmetic and copies ran while one was open for 0% of the time, Pallas kernels for 0%

profile of v5, /device:TPU:1, one launch (start us, length us, event | category | flops | bytes accessed | tf_op | source)
XLA Modules:
  0.0 126.0 jit_solution(11661721341678562753)
XLA Ops:
  0.0 7.2 %pack.1 = bf16[64,48,128]{2,1,0:T(8,128)(2,1)S(1)} custom-call(f32[16,64]{1,0:T(8,128)} %bitcast.10, s32[1,64]{1,0:T(1,128)} %bitcast.11, s32[64,128]{1,0:T(8,128)} %bitcast.9, bf16[16,8192]{1,0:T(8,128)(2,1)} %eigen_hbm.1, bf16[64,8192]{1,0:T(8,128)(2,1)} %raw_hbm.1), custom_call_target="tpu_custom_call" | custom-call | tf_op jit(solution)/shard_map/pack/pallas_call | solution.py:117
  7.2 58.8 %all_to_all.10 = bf16[64,48,128]{2,1,0:T(8,128)(2,1)S(1)} all-to-all(bf16[64,48,128]{2,1,0:T(8,128)(2,1)S(1)} %pack.1), channel_id=1, replica_groups=mesh['z'=16,'c'=2,'y'=4,'x'=4] {'x','z'}, dimensions={0} | all-to-all | bytes 1572864 | tf_op jit(solution)/shard_map/all_to_all | solution.py:278
  66.0 4.6 %collective-permute-start = (bf16[3072,128]{1,0:T(8,128)(2,1)S(1)}, bf16[3072,128]{1,0:T(8,128)(2,1)S(1)}, u32[]{:S(2)}, u32[]{:S(2)}) collective-permute-start(bf16[3072,128]{1,0:T(8,128)(2,1)S(1)} %bitcast.6), channel_id=1, source_target_pairs={{0,12},{4,0},{8,4},{12,8},{1,13},{5,1},{9,5},{13,9},{2,14},{6,2},{... | collective-permute-start | bytes 2359304 | tf_op jit(solution)/shard_map/ppermute | solution.py:280
  70.6 1.9 %collective-permute-start.1 = (bf16[3072,128]{1,0:T(8,128)(2,1)S(1)}, bf16[3072,128]{1,0:T(8,128)(2,1)S(1)}, u32[]{:S(2)}, u32[]{:S(2)}) collective-permute-start(bf16[3072,128]{1,0:T(8,128)(2,1)S(1)} %bitcast.7), channel_id=1, source_target_pairs={{0,4},{4,8},{8,12},{12,0},{1,5},{5,9},{9,13},{13,1},{2,6},{6,10},{... | collective-permute-start | bytes 2359304 | tf_op jit(solution)/shard_map/ppermute | solution.py:279
  72.6 11.0 %collective-permute-done.next_ref = bf16[3072,128]{1,0:T(8,128)(2,1)S(1)} collective-permute-done((bf16[3072,128]{1,0:T(8,128)(2,1)S(1)}, bf16[3072,128]{1,0:T(8,128)(2,1)S(1)}, u32[]{:S(2)}, u32[]{:S(2)}) %collective-permute-start) | collective-permute-done | bytes 786464 | tf_op jit(solution)/shard_map/ppermute | solution.py:280
  83.6 5.0 %collective-permute-done.1.last_ref = bf16[3072,128]{1,0:T(8,128)(2,1)S(1)} collective-permute-done((bf16[3072,128]{1,0:T(8,128)(2,1)S(1)}, bf16[3072,128]{1,0:T(8,128)(2,1)S(1)}, u32[]{:S(2)}, u32[]{:S(2)}) %collective-permute-start.1) | collective-permute-done | bytes 786464 | tf_op jit(solution)/shard_map/ppermute | solution.py:279
  88.6 2.2 %gram.1 = (f32[4,32,1024]{2,1,0:T(8,128)S(1)}, f32[136,1024]{1,0:T(8,128)S(1)}, f32[8,1024]{1,0:T(8,128)S(1)}) custom-call(s32[1]{0:T(128)} %bitcast.core_ref, bf16[3072,128]{1,0:T(8,128)(2,1)S(1)} %bitcast.8, bf16[3072,128]{1,0:T(8,128)(2,1)S(1)} %collective-permute-done.next_ref, bf16[3072,128]{1,0:T(8,128)(2,1)S(1)} %collective-permute-done.1.last_ref), custom_call_target="tpu_custom_call" | custom-call | tf_op jit(solution)/shard_map/gram/pallas_call | solution.py:193
  90.8 7.0 %collective-permute-start.2 = (f32[136,1024]{1,0:T(8,128)S(1)}, f32[136,1024]{1,0:T(8,128)S(1)}, u32[]{:S(2)}, u32[]{:S(2)}) collective-permute-start(f32[136,1024]{1,0:T(8,128)S(1)} %get-tuple-element.9), channel_id=1, source_target_pairs={{0,16},{16,0},{1,17},{17,1},{2,18},{18,2},{3,19},{19,3},{4,20},{20... | collective-permute-start | bytes 1671176 | tf_op jit(solution)/shard_map/ppermute | solution.py:282
  97.8 1.6 %collective-permute-done.2.got_ref = f32[136,1024]{1,0:T(8,128)S(1)} collective-permute-done((f32[136,1024]{1,0:T(8,128)S(1)}, f32[136,1024]{1,0:T(8,128)S(1)}, u32[]{:S(2)}, u32[]{:S(2)}) %collective-permute-start.2) | collective-permute-done | bytes 557088 | tf_op jit(solution)/shard_map/ppermute | solution.py:282
  99.4 1.0 scale.1
  100.3 4.2 %all-to-all-start.1 = ((f32[4,32,1024]{2,1,0:T(8,128)}), f32[4,32,1024]{2,1,0:T(8,128)S(1)}, u32[]{:S(2)}, u32[]{:S(2)}) async-start(f32[4,32,1024]{2,1,0:T(8,128)} %scale.1), calls=%async_computation.1 | async-start | bytes 1048576 | tf_op jit(solution)/shard_map/all_to_all | solution.py:283
  104.5 8.9 %all-to-all-done.1.rows_ref = f32[4,32,1024]{2,1,0:T(8,128)S(1)} async-done(((f32[4,32,1024]{2,1,0:T(8,128)}), f32[4,32,1024]{2,1,0:T(8,128)S(1)}, u32[]{:S(2)}, u32[]{:S(2)}) %all-to-all-start.1) | async-done | bytes 524320 | tf_op jit(solution)/shard_map/all_to_all | solution.py:283
  113.4 3.4 %collective-permute-start.3 = (f32[2,32,1024]{2,1,0:T(8,128)S(1)}, f32[2,32,1024]{2,1,0:T(8,128)S(1)}, u32[]{:S(2)}, u32[]{:S(2)}) collective-permute-start(f32[2,32,1024]{2,1,0:T(8,128)S(1)} %constant_dynamic-slice_fusion.1), channel_id=1, source_target_pairs={{0,16},{16,0},{1,17},{17,1},{2,18},{18,2},{3,19},{19,3},{4,20},{20... | collective-permute-start | bytes 786440 | tf_op jit(solution)/shard_map/ppermute | solution.py:284
  116.9 1.1 collective-permute-done.3.swap_ref
  118.0 1.9 %collective-permute-start.4 = (f32[4,32,256]{2,1,0:T(8,128)S(1)}, f32[4,32,256]{2,1,0:T(8,128)S(1)}, u32[]{:S(2)}, u32[]{:S(2)}) collective-permute-start(f32[4,32,256]{2,1,0:T(8,128)S(1)} %pad_maximum_fusion), channel_id=1, source_target_pairs={{0,12},{4,0},{8,4},{12,8},{1,13},{5,1},{9,5},{13,9},{2,14},{6,2},{... | collective-permute-start | bytes 393224 | tf_op jit(solution)/shard_map/ppermute | solution.py:286
  120.0 0.1 pad_add_fusion.at_ref
  120.0 4.6 %collective-permute-done.4.far_ref = f32[4,32,256]{2,1,0:T(8,128)S(1)} collective-permute-done((f32[4,32,256]{2,1,0:T(8,128)S(1)}, f32[4,32,256]{2,1,0:T(8,128)S(1)}, u32[]{:S(2)}, u32[]{:S(2)}) %collective-permute-start.4) | collective-permute-done | bytes 131104 | tf_op jit(solution)/shard_map/ppermute | solution.py:286
  124.6 1.4 %place.1 = f32[2,64,1024]{2,1,0:T(8,128)} custom-call(s32[2]{0:T(128)S(1)} %pad_add_fusion.at_ref, f32[4,32,1024]{2,1,0:T(8,128)S(1)} %all-to-all-done.1.rows_ref, f32[2,32,1024]{2,1,0:T(8,128)S(1)} %collective-permute-done.3.swap_ref, f32[4,32,256]{2,1,0:T(8,128)S(1)} %collective-permute-done.4.far_ref), custom_call_target="tpu_custom_call" | custom-call | tf_op jit(solution)/shard_map/place/pallas_call | solution.py:260
  (4 shorter events, 0.0 us)
Async XLA Ops:
  66.0 17.5 %collective-permute-start = (bf16[3072,128]{1,0:T(8,128)(2,1)S(1)}, bf16[3072,128]{1,0:T(8,128)(2,1)S(1)}, u32[]{:S(2)}, u32[]{:S(2)}) collective-permute-start(bf16[3072,128]{1,0:T(8,128)(2,1)S(1)} %bitcast.6), channel_id=1, source_target_pairs={{0,12},{4,0},{8,4},{12,8},{1,13},{5,1},{9,5},{13,9},{2,14},{6,2},{... | collective-permute-start | bytes 2359304 | tf_op jit(solution)/shard_map/ppermute | solution.py:280
  70.6 18.0 %collective-permute-start.1 = (bf16[3072,128]{1,0:T(8,128)(2,1)S(1)}, bf16[3072,128]{1,0:T(8,128)(2,1)S(1)}, u32[]{:S(2)}, u32[]{:S(2)}) collective-permute-start(bf16[3072,128]{1,0:T(8,128)(2,1)S(1)} %bitcast.7), channel_id=1, source_target_pairs={{0,4},{4,8},{8,12},{12,0},{1,5},{5,9},{9,13},{13,1},{2,6},{6,10},{... | collective-permute-start | bytes 2359304 | tf_op jit(solution)/shard_map/ppermute | solution.py:279
  90.8 8.6 %collective-permute-start.2 = (f32[136,1024]{1,0:T(8,128)S(1)}, f32[136,1024]{1,0:T(8,128)S(1)}, u32[]{:S(2)}, u32[]{:S(2)}) collective-permute-start(f32[136,1024]{1,0:T(8,128)S(1)} %get-tuple-element.9), channel_id=1, source_target_pairs={{0,16},{16,0},{1,17},{17,1},{2,18},{18,2},{3,19},{19,3},{4,20},{20... | collective-permute-start | bytes 1671176 | tf_op jit(solution)/shard_map/ppermute | solution.py:282
  100.3 13.1 %all-to-all-start.1 = ((f32[4,32,1024]{2,1,0:T(8,128)}), f32[4,32,1024]{2,1,0:T(8,128)S(1)}, u32[]{:S(2)}, u32[]{:S(2)}) async-start(f32[4,32,1024]{2,1,0:T(8,128)} %scale.1), calls=%async_computation.1 | async-start | bytes 1048576 | tf_op jit(solution)/shard_map/all_to_all | solution.py:283
  113.4 4.6 %collective-permute-start.3 = (f32[2,32,1024]{2,1,0:T(8,128)S(1)}, f32[2,32,1024]{2,1,0:T(8,128)S(1)}, u32[]{:S(2)}, u32[]{:S(2)}) collective-permute-start(f32[2,32,1024]{2,1,0:T(8,128)S(1)} %constant_dynamic-slice_fusion.1), channel_id=1, source_target_pairs={{0,16},{16,0},{1,17},{17,1},{2,18},{18,2},{3,19},{19,3},{4,20},{20... | collective-permute-start | bytes 786440 | tf_op jit(solution)/shard_map/ppermute | solution.py:284
  118.0 6.6 %collective-permute-start.4 = (f32[4,32,256]{2,1,0:T(8,128)S(1)}, f32[4,32,256]{2,1,0:T(8,128)S(1)}, u32[]{:S(2)}, u32[]{:S(2)}) collective-permute-start(f32[4,32,256]{2,1,0:T(8,128)S(1)} %pad_maximum_fusion), channel_id=1, source_target_pairs={{0,12},{4,0},{8,4},{12,8},{1,13},{5,1},{9,5},{13,9},{2,14},{6,2},{... | collective-permute-start | bytes 393224 | tf_op jit(solution)/shard_map/ppermute | solution.py:286

commit v6 on v5

--- a/solution.py
+++ b/solution.py
@@ -280,11 +280,13 @@
     after = lax.ppermute(mine, "y", shift(4, -1))
     keep, send, own = gram(core[None], mine, after, prior)
     got = lax.ppermute(send, "c", shift(2, 1))
-    rows = lax.all_to_all(scale(core[None], keep, got, own), "x", 0, 0, tiled=True)
-    swap = lax.ppermute(lax.dynamic_slice_in_dim(rows, 2 * (1 - core), 2, 0), "c", shift(2, 1))
-    far = jnp.concatenate([lax.dynamic_slice(rows, (2 * core, 0, 768), (2, 32, 256)), swap[:, :, 768:]], axis=0)
+    first, second, at, rows = lax.optimization_barrier(
+        (2 * core, 2 - 2 * core, jnp.stack([core, row]), scale(core[None], keep, got, own)))
+    rows = lax.all_to_all(rows, "x", 0, 0, tiled=True)
+    swap = lax.ppermute(lax.dynamic_slice_in_dim(rows, second, 2, 0, allow_negative_indices=False), "c", shift(2, 1))
+    far = jnp.concatenate([lax.dynamic_slice(rows, (first, 0, 768), (2, 32, 256), allow_negative_indices=False), swap[:, :, 768:]], axis=0)
     far = lax.ppermute(far, "y", shift(4, -1))
-    return place(jnp.stack([core, row]), rows, swap, far)
+    return place(at, rows, swap, far)
 
 
 def solution(mesh):

time: 127 us -> 126 us (level)
  blocking collectives: 58.8 us -> 71.4 us
  waiting for transfers between devices: 32.2 us -> 23.3 us
  starting transfers between devices: 23 us -> 19.2 us
    all_to_all x0 -> x1, blocking collectives: none -> 12.6 us  [shards(): rows = lax.all_to_all(rows, 'x', 0, 0, tiled=True)]
    all_to_all x1 -> x0, waiting for transfers between devices: 8.92 us -> none  [shards(): lax.all_to_all(scale(core[None], keep, got, own), 'x', 0, 0, tiled=True)]
    all_to_all x1 -> x0, starting transfers between devices: 4.17 us -> none  [shards(): lax.all_to_all(scale(core[None], keep, got, own), 'x', 0, 0, tiled=True)]
  transfers between devices with their start and end apart: 6 -> 5, of which waited for: 6 -> 5; matrix products, arithmetic and copies ran while one was open for 0% -> 0% of each run, Pallas kernels for 0% -> 0%
where the time goes in v6:
time: 126 us; the launch traced here: 125 us
  blocking collectives  71.4 us (57%)
  waiting for transfers between devices  23.3 us (18%)
  starting transfers between devices  19.2 us (15%)
  Pallas kernels  10.9 us (9%)
    all_to_all x1, blocking collectives, shards(): lax.all_to_all(packed, ('x', 'z'), 0, 0, tiled=True).reshape(4 * DEPTH, 128)  58.8 us
    all_to_all x1, blocking collectives, shards(): rows = lax.all_to_all(rows, 'x', 0, 0, tiled=True)  12.6 us
    ppermute x1, waiting for transfers between devices, shards(): after = lax.ppermute(mine, 'y', shift(4, -1))  11 us
    pallas_call x1, Pallas kernels, pack(): pl.pallas_call(pack_kernel, out_shape=jax.ShapeDtypeStruct((DESTS, PART,...  7.18 us
    ppermute x1, starting transfers between devices, shards(): got = lax.ppermute(send, 'c', shift(2, 1))  6.98 us
    ppermute x1, waiting for transfers between devices, shards(): prior = lax.ppermute(mine, 'y', shift(4, 1))  5.04 us
    ppermute x1, waiting for transfers between devices, shards(): far = lax.ppermute(far, 'y', shift(4, -1))  4.65 us
    ppermute x1, starting transfers between devices, shards(): after = lax.ppermute(mine, 'y', shift(4, -1))  4.63 us
  transfers between devices with their start and end apart: 5, of which 5 were waited for; matrix products, arithmetic and copies ran while one was open for 0% of the time, Pallas kernels for 0%

profile of v6, /device:TPU:1, one launch (start us, length us, event | category | flops | bytes accessed | tf_op | source)
XLA Modules:
  0.0 125.0 jit_solution(8032292983920082500)
XLA Ops:
  0.0 7.2 %pack.1 = bf16[64,48,128]{2,1,0:T(8,128)(2,1)S(1)} custom-call(f32[16,64]{1,0:T(8,128)} %bitcast.10, s32[1,64]{1,0:T(1,128)} %bitcast.11, s32[64,128]{1,0:T(8,128)} %bitcast.9, bf16[16,8192]{1,0:T(8,128)(2,1)} %eigen_hbm.1, bf16[64,8192]{1,0:T(8,128)(2,1)} %raw_hbm.1), custom_call_target="tpu_custom_call" | custom-call | tf_op jit(solution)/shard_map/pack/pallas_call | solution.py:117
  7.2 58.8 %all_to_all.10 = bf16[64,48,128]{2,1,0:T(8,128)(2,1)S(1)} all-to-all(bf16[64,48,128]{2,1,0:T(8,128)(2,1)S(1)} %pack.1), channel_id=1, replica_groups=mesh['z'=16,'c'=2,'y'=4,'x'=4] {'x','z'}, dimensions={0} | all-to-all | bytes 1572864 | tf_op jit(solution)/shard_map/all_to_all | solution.py:278
  66.0 4.6 %collective-permute-start = (bf16[3072,128]{1,0:T(8,128)(2,1)S(1)}, bf16[3072,128]{1,0:T(8,128)(2,1)S(1)}, u32[]{:S(2)}, u32[]{:S(2)}) collective-permute-start(bf16[3072,128]{1,0:T(8,128)(2,1)S(1)} %bitcast.6), channel_id=1, source_target_pairs={{0,12},{4,0},{8,4},{12,8},{1,13},{5,1},{9,5},{13,9},{2,14},{6,2},{... | collective-permute-start | bytes 2359304 | tf_op jit(solution)/shard_map/ppermute | solution.py:280
  70.7 1.9 %collective-permute-start.1 = (bf16[3072,128]{1,0:T(8,128)(2,1)S(1)}, bf16[3072,128]{1,0:T(8,128)(2,1)S(1)}, u32[]{:S(2)}, u32[]{:S(2)}) collective-permute-start(bf16[3072,128]{1,0:T(8,128)(2,1)S(1)} %bitcast.7), channel_id=1, source_target_pairs={{0,4},{4,8},{8,12},{12,0},{1,5},{5,9},{9,13},{13,1},{2,6},{6,10},{... | collective-permute-start | bytes 2359304 | tf_op jit(solution)/shard_map/ppermute | solution.py:279
  72.6 11.0 %collective-permute-done.next_ref = bf16[3072,128]{1,0:T(8,128)(2,1)S(1)} collective-permute-done((bf16[3072,128]{1,0:T(8,128)(2,1)S(1)}, bf16[3072,128]{1,0:T(8,128)(2,1)S(1)}, u32[]{:S(2)}, u32[]{:S(2)}) %collective-permute-start) | collective-permute-done | bytes 786464 | tf_op jit(solution)/shard_map/ppermute | solution.py:280
  83.6 5.0 %collective-permute-done.1.last_ref = bf16[3072,128]{1,0:T(8,128)(2,1)S(1)} collective-permute-done((bf16[3072,128]{1,0:T(8,128)(2,1)S(1)}, bf16[3072,128]{1,0:T(8,128)(2,1)S(1)}, u32[]{:S(2)}, u32[]{:S(2)}) %collective-permute-start.1) | collective-permute-done | bytes 786464 | tf_op jit(solution)/shard_map/ppermute | solution.py:279
  88.7 2.2 %gram.1 = (f32[4,32,1024]{2,1,0:T(8,128)S(1)}, f32[136,1024]{1,0:T(8,128)S(1)}, f32[8,1024]{1,0:T(8,128)S(1)}) custom-call(s32[1]{0:T(128)} %bitcast.core_ref, bf16[3072,128]{1,0:T(8,128)(2,1)S(1)} %bitcast.8, bf16[3072,128]{1,0:T(8,128)(2,1)S(1)} %collective-permute-done.next_ref, bf16[3072,128]{1,0:T(8,128)(2,1)S(1)} %collective-permute-done.1.last_ref), custom_call_target="tpu_custom_call" | custom-call | tf_op jit(solution)/shard_map/gram/pallas_call | solution.py:193
  90.9 7.0 %collective-permute-start.2 = (f32[136,1024]{1,0:T(8,128)S(1)}, f32[136,1024]{1,0:T(8,128)S(1)}, u32[]{:S(2)}, u32[]{:S(2)}) collective-permute-start(f32[136,1024]{1,0:T(8,128)S(1)} %get-tuple-element.13), channel_id=1, source_target_pairs={{0,16},{16,0},{1,17},{17,1},{2,18},{18,2},{3,19},{19,3},{4,20},{20... | collective-permute-start | bytes 1671176 | tf_op jit(solution)/shard_map/ppermute | solution.py:282
  97.9 0.1 pad_add_fusion.at_ref
  97.9 1.5 %collective-permute-done.2.got_ref = f32[136,1024]{1,0:T(8,128)S(1)} collective-permute-done((f32[136,1024]{1,0:T(8,128)S(1)}, f32[136,1024]{1,0:T(8,128)S(1)}, u32[]{:S(2)}, u32[]{:S(2)}) %collective-permute-start.2) | collective-permute-done | bytes 557088 | tf_op jit(solution)/shard_map/ppermute | solution.py:282
  99.4 0.2 scale.1
  99.6 12.6 %all_to_all.11.rows_ref = f32[4,32,1024]{2,1,0:T(8,128)S(1)} all-to-all(f32[4,32,1024]{2,1,0:T(8,128)S(1)} %scale.1), channel_id=1, replica_groups=mesh['z'=16,'c'=2,'y'=4,'x'=4] {'x'}, dimensions={0} | all-to-all | bytes 1048576 | tf_op jit(solution)/shard_map/all_to_all | solution.py:285
  112.2 3.7 %collective-permute-start.3 = (f32[2,32,1024]{2,1,0:T(8,128)S(1)}, f32[2,32,1024]{2,1,0:T(8,128)S(1)}, u32[]{:S(2)}, u32[]{:S(2)}) collective-permute-start(f32[2,32,1024]{2,1,0:T(8,128)S(1)} %constant_dynamic-slice_fusion.1), channel_id=1, source_target_pairs={{0,16},{16,0},{1,17},{17,1},{2,18},{18,2},{3,19},{19,3},{4,20},{20... | collective-permute-start | bytes 786440 | tf_op jit(solution)/shard_map/ppermute | solution.py:286
  115.9 1.1 collective-permute-done.3.swap_ref
  117.0 1.9 %collective-permute-start.4 = (f32[4,32,256]{2,1,0:T(8,128)S(1)}, f32[4,32,256]{2,1,0:T(8,128)S(1)}, u32[]{:S(2)}, u32[]{:S(2)}) collective-permute-start(f32[4,32,256]{2,1,0:T(8,128)S(1)} %pad_maximum_fusion), channel_id=1, source_target_pairs={{0,12},{4,0},{8,4},{12,8},{1,13},{5,1},{9,5},{13,9},{2,14},{6,2},{... | collective-permute-start | bytes 393224 | tf_op jit(solution)/shard_map/ppermute | solution.py:288
  119.0 4.6 %collective-permute-done.4.far_ref = f32[4,32,256]{2,1,0:T(8,128)S(1)} collective-permute-done((f32[4,32,256]{2,1,0:T(8,128)S(1)}, f32[4,32,256]{2,1,0:T(8,128)S(1)}, u32[]{:S(2)}, u32[]{:S(2)}) %collective-permute-start.4) | collective-permute-done | bytes 131104 | tf_op jit(solution)/shard_map/ppermute | solution.py:288
  123.6 1.4 %place.1 = f32[2,64,1024]{2,1,0:T(8,128)} custom-call(s32[2]{0:T(128)S(1)} %pad_add_fusion.at_ref, f32[4,32,1024]{2,1,0:T(8,128)S(1)} %all_to_all.11.rows_ref, f32[2,32,1024]{2,1,0:T(8,128)S(1)} %collective-permute-done.3.swap_ref, f32[4,32,256]{2,1,0:T(8,128)S(1)} %collective-permute-done.4.far_ref), custom_call_target="tpu_custom_call" | custom-call | tf_op jit(solution)/shard_map/place/pallas_call | solution.py:260
  (4 shorter events, 0.0 us)
Async XLA Ops:
  66.0 17.6 %collective-permute-start = (bf16[3072,128]{1,0:T(8,128)(2,1)S(1)}, bf16[3072,128]{1,0:T(8,128)(2,1)S(1)}, u32[]{:S(2)}, u32[]{:S(2)}) collective-permute-start(bf16[3072,128]{1,0:T(8,128)(2,1)S(1)} %bitcast.6), channel_id=1, source_target_pairs={{0,12},{4,0},{8,4},{12,8},{1,13},{5,1},{9,5},{13,9},{2,14},{6,2},{... | collective-permute-start | bytes 2359304 | tf_op jit(solution)/shard_map/ppermute | solution.py:280
  70.7 18.0 %collective-permute-start.1 = (bf16[3072,128]{1,0:T(8,128)(2,1)S(1)}, bf16[3072,128]{1,0:T(8,128)(2,1)S(1)}, u32[]{:S(2)}, u32[]{:S(2)}) collective-permute-start(bf16[3072,128]{1,0:T(8,128)(2,1)S(1)} %bitcast.7), channel_id=1, source_target_pairs={{0,4},{4,8},{8,12},{12,0},{1,5},{5,9},{9,13},{13,1},{2,6},{6,10},{... | collective-permute-start | bytes 2359304 | tf_op jit(solution)/shard_map/ppermute | solution.py:279
  90.9 8.6 %collective-permute-start.2 = (f32[136,1024]{1,0:T(8,128)S(1)}, f32[136,1024]{1,0:T(8,128)S(1)}, u32[]{:S(2)}, u32[]{:S(2)}) collective-permute-start(f32[136,1024]{1,0:T(8,128)S(1)} %get-tuple-element.13), channel_id=1, source_target_pairs={{0,16},{16,0},{1,17},{17,1},{2,18},{18,2},{3,19},{19,3},{4,20},{20... | collective-permute-start | bytes 1671176 | tf_op jit(solution)/shard_map/ppermute | solution.py:282
  112.2 4.9 %collective-permute-start.3 = (f32[2,32,1024]{2,1,0:T(8,128)S(1)}, f32[2,32,1024]{2,1,0:T(8,128)S(1)}, u32[]{:S(2)}, u32[]{:S(2)}) collective-permute-start(f32[2,32,1024]{2,1,0:T(8,128)S(1)} %constant_dynamic-slice_fusion.1), channel_id=1, source_target_pairs={{0,16},{16,0},{1,17},{17,1},{2,18},{18,2},{3,19},{19,3},{4,20},{20... | collective-permute-start | bytes 786440 | tf_op jit(solution)/shard_map/ppermute | solution.py:286
  117.0 6.6 %collective-permute-start.4 = (f32[4,32,256]{2,1,0:T(8,128)S(1)}, f32[4,32,256]{2,1,0:T(8,128)S(1)}, u32[]{:S(2)}, u32[]{:S(2)}) collective-permute-start(f32[4,32,256]{2,1,0:T(8,128)S(1)} %pad_maximum_fusion), channel_id=1, source_target_pairs={{0,12},{4,0},{8,4},{12,8},{1,13},{5,1},{9,5},{13,9},{2,14},{6,2},{... | collective-permute-start | bytes 393224 | tf_op jit(solution)/shard_map/ppermute | solution.py:288

commit v7 on v6

--- a/solution.py
+++ b/solution.py
@@ -242,10 +242,10 @@
 
 
 def place_kernel(at_ref, rows_ref, swap_ref, far_ref, out_ref):
-    core, row = at_ref[0], at_ref[1]
+    core = at_ref[0]
     own, other = (pl.ds(pl.multiple_of(c * 32, 32), 32) for c in (core, 1 - core))
     for group in range(4):
-        lanes = pl.ds(pl.multiple_of(lax.rem(row + 3 + group, 4) * 256, 256), 256)
+        lanes = pl.ds(pl.multiple_of(at_ref[1 + group] * 256, 256), 256)
         source = slice(group * 256, (group + 1) * 256)
         for b in range(2):
             if group < 3:
@@ -267,8 +267,9 @@
     )(at, rows, swap, far)
 
 
-def shift(size, step):
-    return [(i, (i + step) % size) for i in range(size)]
+SWAP = [(0, 1), (1, 0)]
+NEAR = [(0, 1), (1, 0), (2, 3), (3, 2)]
+WRAP = [(0, 3), (1, 2), (2, 1), (3, 0)]
 
 
 def shards(raw_frames, eigen_flats, weights, flat_count, bin_map):
@@ -276,16 +277,16 @@
     row = lax.axis_index("y").astype(jnp.int32)
     packed = pack(weights.T, flat_count[None, :], bin_map.reshape(PIXELS // 128, 128), eigen_flats, raw_frames)
     mine = lax.all_to_all(packed, ("x", "z"), 0, 0, tiled=True).reshape(4 * DEPTH, 128)
-    prior = lax.ppermute(mine, "y", shift(4, 1))
-    after = lax.ppermute(mine, "y", shift(4, -1))
+    prior = lax.ppermute(mine, "y", NEAR)
+    after = lax.ppermute(mine, "y", WRAP)
     keep, send, own = gram(core[None], mine, after, prior)
-    got = lax.ppermute(send, "c", shift(2, 1))
+    got = lax.ppermute(send, "c", SWAP)
     first, second, at, rows = lax.optimization_barrier(
-        (2 * core, 2 - 2 * core, jnp.stack([core, row]), scale(core[None], keep, got, own)))
+        (2 * core, 2 - 2 * core, jnp.stack([core, row ^ 1, row, 3 - row, (row + 2) % 4]), scale(core[None], keep, got, own)))
     rows = lax.all_to_all(rows, "x", 0, 0, tiled=True)
-    swap = lax.ppermute(lax.dynamic_slice_in_dim(rows, second, 2, 0, allow_negative_indices=False), "c", shift(2, 1))
+    swap = lax.ppermute(lax.dynamic_slice_in_dim(rows, second, 2, 0, allow_negative_indices=False), "c", SWAP)
     far = jnp.concatenate([lax.dynamic_slice(rows, (first, 0, 768), (2, 32, 256), allow_negative_indices=False), swap[:, :, 768:]], axis=0)
-    far = lax.ppermute(far, "y", shift(4, -1))
+    far = lax.ppermute(far, "y", NEAR)
     return place(at, rows, swap, far)
 
 

time: 126 us -> 125 us (level)
  no operation moved by 1% of the time
where the time goes in v7:
time: 125 us; the launch traced here: 124 us
  blocking collectives  71.4 us (57%)
  waiting for transfers between devices  22.1 us (18%)
  starting transfers between devices  19.2 us (15%)
  Pallas kernels  10.9 us (9%)
    all_to_all x1, blocking collectives, shards(): lax.all_to_all(packed, ('x', 'z'), 0, 0, tiled=True).reshape(4 * DEPTH, 128)  58.8 us
    all_to_all x1, blocking collectives, shards(): rows = lax.all_to_all(rows, 'x', 0, 0, tiled=True)  12.6 us
    ppermute x1, waiting for transfers between devices, shards(): after = lax.ppermute(mine, 'y', WRAP)  11.8 us
    pallas_call x1, Pallas kernels, pack(): pl.pallas_call(pack_kernel, out_shape=jax.ShapeDtypeStruct((DESTS, PART,...  7.18 us
    ppermute x1, starting transfers between devices, shards(): got = lax.ppermute(send, 'c', SWAP)  6.99 us
    ppermute x1, waiting for transfers between devices, shards(): far = lax.ppermute(far, 'y', NEAR)  4.65 us
    ppermute x1, starting transfers between devices, shards(): after = lax.ppermute(mine, 'y', WRAP)  4.62 us
    ppermute x1, starting transfers between devices, shards(): lax.ppermute(lax.dynamic_slice_in_dim(rows, second, 2, 0, allow_negative_...  3.71 us
  transfers between devices with their start and end apart: 5, of which 5 were waited for; matrix products, arithmetic and copies ran while one was open for 0% of the time, Pallas kernels for 0%

profile of v7, /device:TPU:1, one launch (start us, length us, event | category | flops | bytes accessed | tf_op | source)
XLA Modules:
  0.0 123.8 jit_solution(13941355422662467381)
XLA Ops:
  0.0 7.2 %pack.1 = bf16[64,48,128]{2,1,0:T(8,128)(2,1)S(1)} custom-call(f32[16,64]{1,0:T(8,128)} %bitcast.13, s32[1,64]{1,0:T(1,128)} %bitcast.14, s32[64,128]{1,0:T(8,128)} %bitcast.12, bf16[16,8192]{1,0:T(8,128)(2,1)} %eigen_hbm.1, bf16[64,8192]{1,0:T(8,128)(2,1)} %raw_hbm.1), custom_call_target="tpu_custom_call" | custom-call | tf_op jit(solution)/shard_map/pack/pallas_call | solution.py:117
  7.2 58.8 %all_to_all.10 = bf16[64,48,128]{2,1,0:T(8,128)(2,1)S(1)} all-to-all(bf16[64,48,128]{2,1,0:T(8,128)(2,1)S(1)} %pack.1), channel_id=1, replica_groups=mesh['z'=16,'c'=2,'y'=4,'x'=4] {'x','z'}, dimensions={0} | all-to-all | bytes 1572864 | tf_op jit(solution)/shard_map/all_to_all | solution.py:279
  66.0 4.6 %collective-permute-start = (bf16[3072,128]{1,0:T(8,128)(2,1)S(1)}, bf16[3072,128]{1,0:T(8,128)(2,1)S(1)}, u32[]{:S(2)}, u32[]{:S(2)}) collective-permute-start(bf16[3072,128]{1,0:T(8,128)(2,1)S(1)} %bitcast.9), channel_id=1, source_target_pairs={{0,12},{4,8},{8,4},{12,0},{1,13},{5,9},{9,5},{13,1},{2,14},{6,10},... | collective-permute-start | bytes 2359304 | tf_op jit(solution)/shard_map/ppermute | solution.py:281
  70.7 1.9 %collective-permute-start.1 = (bf16[3072,128]{1,0:T(8,128)(2,1)S(1)}, bf16[3072,128]{1,0:T(8,128)(2,1)S(1)}, u32[]{:S(2)}, u32[]{:S(2)}) collective-permute-start(bf16[3072,128]{1,0:T(8,128)(2,1)S(1)} %bitcast.10), channel_id=1, source_target_pairs={{0,4},{4,0},{8,12},{12,8},{1,5},{5,1},{9,13},{13,9},{2,6},{6,2},{1... | collective-permute-start | bytes 2359304 | tf_op jit(solution)/shard_map/ppermute | solution.py:280
  72.6 11.8 %collective-permute-done.next_ref = bf16[3072,128]{1,0:T(8,128)(2,1)S(1)} collective-permute-done((bf16[3072,128]{1,0:T(8,128)(2,1)S(1)}, bf16[3072,128]{1,0:T(8,128)(2,1)S(1)}, u32[]{:S(2)}, u32[]{:S(2)}) %collective-permute-start) | collective-permute-done | bytes 786464 | tf_op jit(solution)/shard_map/ppermute | solution.py:281
  84.4 3.0 %collective-permute-done.1.last_ref = bf16[3072,128]{1,0:T(8,128)(2,1)S(1)} collective-permute-done((bf16[3072,128]{1,0:T(8,128)(2,1)S(1)}, bf16[3072,128]{1,0:T(8,128)(2,1)S(1)}, u32[]{:S(2)}, u32[]{:S(2)}) %collective-permute-start.1) | collective-permute-done | bytes 786464 | tf_op jit(solution)/shard_map/ppermute | solution.py:280
  87.4 2.2 %gram.1 = (f32[4,32,1024]{2,1,0:T(8,128)S(1)}, f32[136,1024]{1,0:T(8,128)S(1)}, f32[8,1024]{1,0:T(8,128)S(1)}) custom-call(s32[1]{0:T(128)} %bitcast.core_ref, bf16[3072,128]{1,0:T(8,128)(2,1)S(1)} %bitcast.11, bf16[3072,128]{1,0:T(8,128)(2,1)S(1)} %collective-permute-done.next_ref, bf16[3072,128]{1,0:T(8,128)(2,1)S(1)} %collective-permute-done.1.last_ref), custom_call_target="tpu_custom_call" | custom-call | tf_op jit(solution)/shard_map/gram/pallas_call | solution.py:193
  89.6 7.0 %collective-permute-start.2 = (f32[136,1024]{1,0:T(8,128)S(1)}, f32[136,1024]{1,0:T(8,128)S(1)}, u32[]{:S(2)}, u32[]{:S(2)}) collective-permute-start(f32[136,1024]{1,0:T(8,128)S(1)} %get-tuple-element.13), channel_id=1, source_target_pairs={{0,16},{16,0},{1,17},{17,1},{2,18},{18,2},{3,19},{19,3},{4,20},{20... | collective-permute-start | bytes 1671176 | tf_op jit(solution)/shard_map/ppermute | solution.py:283
  96.7 0.1 stack.23.at_ref
  96.7 1.5 %collective-permute-done.2.got_ref = f32[136,1024]{1,0:T(8,128)S(1)} collective-permute-done((f32[136,1024]{1,0:T(8,128)S(1)}, f32[136,1024]{1,0:T(8,128)S(1)}, u32[]{:S(2)}, u32[]{:S(2)}) %collective-permute-start.2) | collective-permute-done | bytes 557088 | tf_op jit(solution)/shard_map/ppermute | solution.py:283
  98.2 0.2 scale.1
  98.4 12.6 %all_to_all.11.rows_ref = f32[4,32,1024]{2,1,0:T(8,128)S(1)} all-to-all(f32[4,32,1024]{2,1,0:T(8,128)S(1)} %scale.1), channel_id=1, replica_groups=mesh['z'=16,'c'=2,'y'=4,'x'=4] {'x'}, dimensions={0} | all-to-all | bytes 1048576 | tf_op jit(solution)/shard_map/all_to_all | solution.py:286
  111.0 3.7 %collective-permute-start.3 = (f32[2,32,1024]{2,1,0:T(8,128)S(1)}, f32[2,32,1024]{2,1,0:T(8,128)S(1)}, u32[]{:S(2)}, u32[]{:S(2)}) collective-permute-start(f32[2,32,1024]{2,1,0:T(8,128)S(1)} %constant_dynamic-slice_fusion.1), channel_id=1, source_target_pairs={{0,16},{16,0},{1,17},{17,1},{2,18},{18,2},{3,19},{19,3},{4,20},{20... | collective-permute-start | bytes 786440 | tf_op jit(solution)/shard_map/ppermute | solution.py:287
  114.7 1.1 collective-permute-done.3.swap_ref
  115.8 1.9 %collective-permute-start.4 = (f32[4,32,256]{2,1,0:T(8,128)S(1)}, f32[4,32,256]{2,1,0:T(8,128)S(1)}, u32[]{:S(2)}, u32[]{:S(2)}) collective-permute-start(f32[4,32,256]{2,1,0:T(8,128)S(1)} %pad_maximum_fusion), channel_id=1, source_target_pairs={{0,4},{4,0},{8,12},{12,8},{1,5},{5,1},{9,13},{13,9},{2,6},{6,2},{1... | collective-permute-start | bytes 393224 | tf_op jit(solution)/shard_map/ppermute | solution.py:289
  117.8 4.6 %collective-permute-done.4.far_ref = f32[4,32,256]{2,1,0:T(8,128)S(1)} collective-permute-done((f32[4,32,256]{2,1,0:T(8,128)S(1)}, f32[4,32,256]{2,1,0:T(8,128)S(1)}, u32[]{:S(2)}, u32[]{:S(2)}) %collective-permute-start.4) | collective-permute-done | bytes 131104 | tf_op jit(solution)/shard_map/ppermute | solution.py:289
  122.4 1.4 %place.1 = f32[2,64,1024]{2,1,0:T(8,128)} custom-call(s32[5]{0:T(128)S(1)} %stack.23.at_ref, f32[4,32,1024]{2,1,0:T(8,128)S(1)} %all_to_all.11.rows_ref, f32[2,32,1024]{2,1,0:T(8,128)S(1)} %collective-permute-done.3.swap_ref, f32[4,32,256]{2,1,0:T(8,128)S(1)} %collective-permute-done.4.far_ref), custom_call_target="tpu_custom_call" | custom-call | tf_op jit(solution)/shard_map/place/pallas_call | solution.py:260
  (4 shorter events, 0.0 us)
Async XLA Ops:
  66.0 18.4 %collective-permute-start = (bf16[3072,128]{1,0:T(8,128)(2,1)S(1)}, bf16[3072,128]{1,0:T(8,128)(2,1)S(1)}, u32[]{:S(2)}, u32[]{:S(2)}) collective-permute-start(bf16[3072,128]{1,0:T(8,128)(2,1)S(1)} %bitcast.9), channel_id=1, source_target_pairs={{0,12},{4,8},{8,4},{12,0},{1,13},{5,9},{9,5},{13,1},{2,14},{6,10},... | collective-permute-start | bytes 2359304 | tf_op jit(solution)/shard_map/ppermute | solution.py:281
  70.7 16.8 %collective-permute-start.1 = (bf16[3072,128]{1,0:T(8,128)(2,1)S(1)}, bf16[3072,128]{1,0:T(8,128)(2,1)S(1)}, u32[]{:S(2)}, u32[]{:S(2)}) collective-permute-start(bf16[3072,128]{1,0:T(8,128)(2,1)S(1)} %bitcast.10), channel_id=1, source_target_pairs={{0,4},{4,0},{8,12},{12,8},{1,5},{5,1},{9,13},{13,9},{2,6},{6,2},{1... | collective-permute-start | bytes 2359304 | tf_op jit(solution)/shard_map/ppermute | solution.py:280
  89.6 8.6 %collective-permute-start.2 = (f32[136,1024]{1,0:T(8,128)S(1)}, f32[136,1024]{1,0:T(8,128)S(1)}, u32[]{:S(2)}, u32[]{:S(2)}) collective-permute-start(f32[136,1024]{1,0:T(8,128)S(1)} %get-tuple-element.13), channel_id=1, source_target_pairs={{0,16},{16,0},{1,17},{17,1},{2,18},{18,2},{3,19},{19,3},{4,20},{20... | collective-permute-start | bytes 1671176 | tf_op jit(solution)/shard_map/ppermute | solution.py:283
  111.0 4.9 %collective-permute-start.3 = (f32[2,32,1024]{2,1,0:T(8,128)S(1)}, f32[2,32,1024]{2,1,0:T(8,128)S(1)}, u32[]{:S(2)}, u32[]{:S(2)}) collective-permute-start(f32[2,32,1024]{2,1,0:T(8,128)S(1)} %constant_dynamic-slice_fusion.1), channel_id=1, source_target_pairs={{0,16},{16,0},{1,17},{17,1},{2,18},{18,2},{3,19},{19,3},{4,20},{20... | collective-permute-start | bytes 786440 | tf_op jit(solution)/shard_map/ppermute | solution.py:287
  115.8 6.6 %collective-permute-start.4 = (f32[4,32,256]{2,1,0:T(8,128)S(1)}, f32[4,32,256]{2,1,0:T(8,128)S(1)}, u32[]{:S(2)}, u32[]{:S(2)}) collective-permute-start(f32[4,32,256]{2,1,0:T(8,128)S(1)} %pad_maximum_fusion), channel_id=1, source_target_pairs={{0,4},{4,0},{8,12},{12,8},{1,5},{5,1},{9,13},{13,9},{2,6},{6,2},{1... | collective-permute-start | bytes 393224 | tf_op jit(solution)/shard_map/ppermute | solution.py:289

commit v8 on v7

--- a/solution.py
+++ b/solution.py
@@ -139,132 +139,141 @@
     )(*(pltpu.with_memory_space_constraint(a, pltpu.HBM) for a in (weights, used, bins, eigen, raw)))
 
 
-def gram_kernel(core_ref, mine_ref, next_ref, last_ref, keep_ref, send_ref, own_ref):
+def matrix(ref):
+    return jnp.concatenate([ref[x * DEPTH:(x + 1) * DEPTH, :] for x in range(4)], axis=1)
+
+
+def fold(even_top, even_low, odd_top, odd_low):
+    left = lax.broadcasted_iota(jnp.int32, (1, 128), 1) < FRAMES
+    return jnp.where(left, even_top, odd_low) + pltpu.roll(
+        jnp.where(left, odd_top, even_low), FRAMES, 1)
+
+
+def products(a, b):
+    full = lax.dot_general(a, b, (((0,), (0,)), ((), ())), preferred_element_type=jnp.float32)
+    for x in range(4):
+        top, low = slice(x * 128, x * 128 + 64), slice(x * 128 + 64, x * 128 + 128)
+        for e in range(2):
+            even, odd = slice(e * 256, e * 256 + 128), slice(e * 256 + 128, e * 256 + 256)
+            yield x, e, fold(full[top, even], full[low, even], full[top, odd], full[low, odd])
+
+
+def totals(b):
+    full = jnp.dot(jnp.ones((8, DEPTH), jnp.bfloat16), b, preferred_element_type=jnp.float32)
+    for e in range(2):
+        even, odd = full[:, e * 256:e * 256 + 128], full[:, e * 256 + 128:e * 256 + 256]
+        yield e, fold(even, even, odd, odd)
+
+
+def cross_kernel(core_ref, near_ref, wrap_ref, far_ref):
+    first = core_ref[0] == 0
+    near, wrap = matrix(near_ref), matrix(wrap_ref)
+    for x, e, part in products(near, wrap):
+        lanes = slice(e * 128, e * 128 + 128)
+        far_ref[0, x * 32:(x + 1) * 32, lanes] = jnp.where(first, part[:32], part[32:])
+        far_ref[1, x * 32:(x + 1) * 32, lanes] = jnp.where(first, part[32:], part[:32])
+    for e, part in totals(wrap):
+        for half in range(2):
+            far_ref[half, 128:, e * 128:e * 128 + 128] = part
+
+
+def cross(core, near, wrap):
+    return pl.pallas_call(
+        cross_kernel,
+        out_shape=jax.ShapeDtypeStruct((2, 136, 256), jnp.float32),
+        in_specs=[pl.BlockSpec(memory_space=pltpu.SMEM)] + [pl.BlockSpec(memory_space=pltpu.VMEM)] * 2,
+        out_specs=pl.BlockSpec(memory_space=pltpu.VMEM),
+        compiler_params=pltpu.CompilerParams(vmem_limit_bytes=16 << 20),
+        name="cross",
+    )(core, near, wrap)
+
+
+def gram_kernel(core_ref, mine_ref, near_ref, wrap_ref, keep_ref, send_ref, own_ref):
     f32, bf16 = jnp.float32, jnp.bfloat16
     first = core_ref[0] == 0
-    left = lax.broadcasted_iota(jnp.int32, (1, 128), 1) < FRAMES
-    ones = jnp.ones((8, DEPTH), bf16)
-
-    def matrix(ref):
-        return jnp.concatenate([ref[x * DEPTH:(x + 1) * DEPTH, :] for x in range(4)], axis=1)
-
-    def fold(even_top, even_low, odd_top, odd_low):
-        return jnp.where(left, even_top, odd_low) + pltpu.roll(
-            jnp.where(left, odd_top, even_low), FRAMES, 1)
-
-    def product(a, b, group):
-        full = lax.dot_general(a, b, (((0,), (0,)), ((), ())), preferred_element_type=f32)
-        for x in range(4):
-            top, low = slice(x * 128, x * 128 + 64), slice(x * 128 + 64, x * 128 + 128)
-            for e in range(2):
-                even, odd = slice(e * 256, e * 256 + 128), slice(e * 256 + 128, e * 256 + 256)
-                part = fold(full[top, even], full[low, even], full[top, odd], full[low, odd])
-                lanes = slice(group * 256 + e * 128, group * 256 + e * 128 + 128)
-                keep_ref[x, :, lanes] = jnp.where(first, part[:32], part[32:])
-                send_ref[x * 32:(x + 1) * 32, lanes] = jnp.where(first, part[32:], part[:32])
-
-    def total(b, group):
-        full = jnp.dot(ones, b, preferred_element_type=f32)
-        for e in range(2):
-            even, odd = full[:, e * 256:e * 256 + 128], full[:, e * 256 + 128:e * 256 + 256]
+    mine = matrix(mine_ref)
+    for group, ref in enumerate((near_ref, mine_ref, wrap_ref)):
+        other = matrix(ref)
+        for x, e, part in products(mine, other):
             lanes = slice(group * 256 + e * 128, group * 256 + e * 128 + 128)
-            part = fold(even, even, odd, odd)
-            own_ref[:, lanes] = part
-            send_ref[128:, lanes] = part
-
-    mine, after, prior = matrix(mine_ref), matrix(next_ref), matrix(last_ref)
-    product(mine, mine, 1)
-    product(mine, prior, 0)
-    product(mine, after, 2)
-    product(prior, after, 3)
-    total(prior, 0)
-    total(mine, 1)
-    total(after, 2)
+            keep_ref[x, :, lanes] = jnp.where(first, part[:32], part[32:])
+            send_ref[x * 32:(x + 1) * 32, lanes] = jnp.where(first, part[32:], part[:32])
+        for e, part in totals(other):
+            lanes = slice(group * 256 + e * 128, group * 256 + e * 128 + 128)
+            own_ref[:8, lanes] = part
+            send_ref[128:136, lanes] = part
     hits = jnp.where(mine_ref[:DEPTH, :].astype(f32) != 0.0, 1.0, 0.0).astype(bf16)
-    hits = jnp.dot(ones, hits, preferred_element_type=f32)
+    hits = jnp.dot(jnp.ones((8, DEPTH), bf16), hits, preferred_element_type=f32)
     hits = hits + pltpu.roll(hits, FRAMES, 1)
-    for e in range(2):
-        own_ref[:, 768 + e * 128:896 + e * 128] = hits
-        send_ref[128:, 768 + e * 128:896 + e * 128] = hits
-
-
-def gram(core, mine, after, prior):
+    hits = jnp.concatenate([hits] * 6, axis=1)
+    own_ref[8:, :] = hits
+    send_ref[136:, :] = hits
+
+
+def gram(core, mine, near, wrap):
     f32 = jnp.float32
     return pl.pallas_call(
         gram_kernel,
-        out_shape=(jax.ShapeDtypeStruct((4, 32, 1024), f32),
-                   jax.ShapeDtypeStruct((136, 1024), f32),
-                   jax.ShapeDtypeStruct((8, 1024), f32)),
+        out_shape=(jax.ShapeDtypeStruct((4, 32, 768), f32),
+                   jax.ShapeDtypeStruct((144, 768), f32),
+                   jax.ShapeDtypeStruct((16, 768), f32)),
         in_specs=[pl.BlockSpec(memory_space=pltpu.SMEM)] + [pl.BlockSpec(memory_space=pltpu.VMEM)] * 3,
         out_specs=(pl.BlockSpec(memory_space=pltpu.VMEM),) * 3,
         compiler_params=pltpu.CompilerParams(vmem_limit_bytes=24 << 20),
         name="gram",
-    )(core, mine, after, prior)
-
-
-def scale_kernel(core_ref, keep_ref, got_ref, own_ref, rows_ref):
+    )(core, mine, near, wrap)
+
+
+def scale_kernel(core_ref, keep_ref, got_ref, own_ref, far_ref, far_got_ref, rows_ref):
     first = core_ref[0] == 0
     sums = own_ref[...] + got_ref[128:, :]
-    count = sums[0:1, 768:896]
-    count = jnp.concatenate([count, count], axis=1)
-
-    def column(group):
-        tall = [jnp.broadcast_to(sums[0:1, group * 256 + e * 128:group * 256 + e * 128 + 128], (128, 128)).T
-                for e in range(2)]
-        tall = jnp.concatenate(tall, axis=0)
-        parts = []
-        for x in range(4):
-            part = jnp.where(first, tall[x * 64:x * 64 + 32], tall[x * 64 + 32:x * 64 + 64])
-            parts.append(jnp.concatenate([part, part], axis=1))
-        return parts
-
-    mine, prior = column(1), column(0)
+    far_sums = far_ref[0, 128:, :] + far_got_ref[128:, :]
+    count = sums[8:9, :256]
+    tall = [jnp.broadcast_to(sums[0:1, 256 + e * 128:384 + e * 128], (128, 128)).T for e in range(2)]
+    tall = jnp.concatenate(tall, axis=0)
     for x in range(4):
-        for group in range(4):
+        part = jnp.where(first, tall[x * 64:x * 64 + 32], tall[x * 64 + 32:x * 64 + 64])
+        mine = jnp.concatenate([part, part], axis=1)
+        rows = slice(x * 32, (x + 1) * 32)
+        for group in range(3):
             lanes = slice(group * 256, group * 256 + 256)
-            value = keep_ref[x, :, lanes] + got_ref[x * 32:(x + 1) * 32, lanes]
-            if group < 3:
-                rows_ref[x, :, lanes] = count * value / (mine[x] * sums[0:1, lanes])
-            else:
-                rows_ref[x, :, lanes] = count * value / (prior[x] * sums[0:1, 512:768])
-
-
-def scale(core, keep, got, own):
-    f32 = jnp.float32
+            value = keep_ref[x, :, lanes] + got_ref[rows, lanes]
+            rows_ref[x, :, lanes] = count * value / (mine * sums[0:1, lanes])
+        value = far_ref[0, rows, :] + far_got_ref[rows, :]
+        rows_ref[x, :, 768:] = count * value / (mine * far_sums[0:1, :])
+
+
+def scale(core, keep, got, own, far, far_got):
     return pl.pallas_call(
         scale_kernel,
-        out_shape=jax.ShapeDtypeStruct((4, 32, 1024), f32),
-        in_specs=[pl.BlockSpec(memory_space=pltpu.SMEM)] + [pl.BlockSpec(memory_space=pltpu.VMEM)] * 3,
+        out_shape=jax.ShapeDtypeStruct((4, 32, 1024), jnp.float32),
+        in_specs=[pl.BlockSpec(memory_space=pltpu.SMEM)] + [pl.BlockSpec(memory_space=pltpu.VMEM)] * 5,
         out_specs=pl.BlockSpec(memory_space=pltpu.VMEM),
         compiler_params=pltpu.CompilerParams(vmem_limit_bytes=8 << 20),
         name="scale",
-    )(core, keep, got, own)
-
-
-def place_kernel(at_ref, rows_ref, swap_ref, far_ref, out_ref):
+    )(core, keep, got, own, far, far_got)
+
+
+def place_kernel(at_ref, rows_ref, swap_ref, out_ref):
     core = at_ref[0]
     own, other = (pl.ds(pl.multiple_of(c * 32, 32), 32) for c in (core, 1 - core))
     for group in range(4):
         lanes = pl.ds(pl.multiple_of(at_ref[1 + group] * 256, 256), 256)
         source = slice(group * 256, (group + 1) * 256)
         for b in range(2):
-            if group < 3:
-                out_ref[b, own, lanes] = rows_ref[2 * core + b, :, source]
-                out_ref[b, other, lanes] = swap_ref[b, :, source]
-            else:
-                out_ref[b, own, lanes] = far_ref[b]
-                out_ref[b, other, lanes] = far_ref[2 + b]
-
-
-def place(at, rows, swap, far):
+            out_ref[b, own, lanes] = rows_ref[2 * core + b, :, source]
+            out_ref[b, other, lanes] = swap_ref[b, :, source]
+
+
+def place(at, rows, swap):
     return pl.pallas_call(
         place_kernel,
         out_shape=jax.ShapeDtypeStruct((2, 64, 1024), jnp.float32),
-        in_specs=[pl.BlockSpec(memory_space=pltpu.SMEM)] + [pl.BlockSpec(memory_space=pltpu.VMEM)] * 3,
+        in_specs=[pl.BlockSpec(memory_space=pltpu.SMEM)] + [pl.BlockSpec(memory_space=pltpu.VMEM)] * 2,
         out_specs=pl.BlockSpec(memory_space=pltpu.VMEM),
         compiler_params=pltpu.CompilerParams(vmem_limit_bytes=8 << 20),
         name="place",
-    )(at, rows, swap, far)
+    )(at, rows, swap)
 
 
 SWAP = [(0, 1), (1, 0)]
@@ -277,17 +286,18 @@
     row = lax.axis_index("y").astype(jnp.int32)
     packed = pack(weights.T, flat_count[None, :], bin_map.reshape(PIXELS // 128, 128), eigen_flats, raw_frames)
     mine = lax.all_to_all(packed, ("x", "z"), 0, 0, tiled=True).reshape(4 * DEPTH, 128)
-    prior = lax.ppermute(mine, "y", NEAR)
-    after = lax.ppermute(mine, "y", WRAP)
-    keep, send, own = gram(core[None], mine, after, prior)
+    near = lax.ppermute(mine, "y", NEAR)
+    wrap = lax.ppermute(mine, "y", WRAP)
+    far = lax.ppermute(cross(core[None], near, wrap), "y", NEAR)
+    keep, send, own = gram(core[None], mine, near, wrap)
     got = lax.ppermute(send, "c", SWAP)
-    first, second, at, rows = lax.optimization_barrier(
-        (2 * core, 2 - 2 * core, jnp.stack([core, row ^ 1, row, 3 - row, (row + 2) % 4]), scale(core[None], keep, got, own)))
+    far_got = lax.ppermute(far[1], "c", SWAP)
+    at, second, rows = lax.optimization_barrier(
+        (jnp.stack([core, row ^ 1, row, 3 - row, (row + 2) % 4]), 2 - 2 * core,
+         scale(core[None], keep, got, own, far, far_got)))
     rows = lax.all_to_all(rows, "x", 0, 0, tiled=True)
     swap = lax.ppermute(lax.dynamic_slice_in_dim(rows, second, 2, 0, allow_negative_indices=False), "c", SWAP)
-    far = jnp.concatenate([lax.dynamic_slice(rows, (first, 0, 768), (2, 32, 256), allow_negative_indices=False), swap[:, :, 768:]], axis=0)
-    far = lax.ppermute(far, "y", NEAR)
-    return place(at, rows, swap, far)
+    return place(at, rows, swap)
 
 
 def solution(mesh):

time: 125 us -> 124 us (level)
  waiting for transfers between devices: 22.1 us -> 16.2 us
  starting transfers between devices: 19.2 us -> 24.2 us
    ppermute x3 -> x4, starting transfers between devices: 8.46 us -> 13.5 us  [the longest x1 4.63 us: shards(): far_got = lax.ppermute(far[1], 'c', SWAP)]
    ppermute x3 -> x4, waiting for transfers between devices: 19.5 us -> 15 us  [the longest x1 10 us: shards(): near = lax.ppermute(mine, 'y', NEAR)]
    ppermute x1, waiting for transfers between devices: 1.46 us -> 0.01 us  [shards(): got = lax.ppermute(send, 'c', SWAP)]
    pallas_call x1 -> x2, Pallas kernels: 2.2 us -> 2.6 us  [the longest x1 1.86 us: gram(): pl.pallas_call(gram_kernel, out_shape=(jax.ShapeDtypeStruct((4, 32, 768),...]
  transfers between devices with their start and end apart: 5 -> 6, of which waited for: 5 -> 4; matrix products, arithmetic and copies ran while one was open for 0% -> 0% of each run, Pallas kernels for 0% -> 2%
where the time goes in v8:
time: 124 us; the launch traced here: 123 us
  blocking collectives  71.4 us (58%)
  starting transfers between devices  24.2 us (20%)
  waiting for transfers between devices  16.2 us (13%)
  Pallas kernels  11.3 us (9%)
    all_to_all x1, blocking collectives, shards(): lax.all_to_all(packed, ('x', 'z'), 0, 0, tiled=True).reshape(4 * DEPTH, 128)  58.8 us
    all_to_all x1, blocking collectives, shards(): rows = lax.all_to_all(rows, 'x', 0, 0, tiled=True)  12.6 us
    ppermute x1, waiting for transfers between devices, shards(): near = lax.ppermute(mine, 'y', NEAR)  10 us
    pallas_call x1, Pallas kernels, pack(): pl.pallas_call(pack_kernel, out_shape=jax.ShapeDtypeStruct((DESTS, PART,...  7.18 us
    ppermute x1, starting transfers between devices, shards(): got = lax.ppermute(send, 'c', SWAP)  6.98 us
    ppermute x1, starting transfers between devices, shards(): far_got = lax.ppermute(far[1], 'c', SWAP)  4.63 us
    ppermute x1, waiting for transfers between devices, shards(): wrap = lax.ppermute(mine, 'y', WRAP)  4.16 us
    ppermute x1, starting transfers between devices, shards(): wrap = lax.ppermute(mine, 'y', WRAP)  3.79 us
  transfers between devices with their start and end apart: 6, of which 4 were waited for; matrix products, arithmetic and copies ran while one was open for 0% of the time, Pallas kernels for 2%

profile of v8, /device:TPU:1, one launch (start us, length us, event | category | flops | bytes accessed | tf_op | source)
XLA Modules:
  0.0 123.4 jit_solution(12621878089092499365)
XLA Ops:
  0.0 7.2 %pack.1 = bf16[64,48,128]{2,1,0:T(8,128)(2,1)S(1)} custom-call(f32[16,64]{1,0:T(8,128)} %bitcast.15, s32[1,64]{1,0:T(1,128)} %bitcast.16, s32[64,128]{1,0:T(8,128)} %bitcast.14, bf16[16,8192]{1,0:T(8,128)(2,1)} %eigen_hbm.1, bf16[64,8192]{1,0:T(8,128)(2,1)} %raw_hbm.1), custom_call_target="tpu_custom_call" | custom-call | tf_op jit(solution)/shard_map/pack/pallas_call | solution.py:117
  7.2 58.8 %all_to_all.10 = bf16[64,48,128]{2,1,0:T(8,128)(2,1)S(1)} all-to-all(bf16[64,48,128]{2,1,0:T(8,128)(2,1)S(1)} %pack.1), channel_id=1, replica_groups=mesh['z'=16,'c'=2,'y'=4,'x'=4] {'x','z'}, dimensions={0} | all-to-all | bytes 1572864 | tf_op jit(solution)/shard_map/all_to_all | solution.py:288
  66.0 3.2 %collective-permute-start = (bf16[3072,128]{1,0:T(8,128)(2,1)S(1)}, bf16[3072,128]{1,0:T(8,128)(2,1)S(1)}, u32[]{:S(2)}, u32[]{:S(2)}) collective-permute-start(bf16[3072,128]{1,0:T(8,128)(2,1)S(1)} %bitcast.11), channel_id=1, source_target_pairs={{0,4},{4,0},{8,12},{12,8},{1,5},{5,1},{9,13},{13,9},{2,6},{6,2},{1... | collective-permute-start | bytes 2359304 | tf_op jit(solution)/shard_map/ppermute | solution.py:289
  69.2 3.8 %collective-permute-start.1 = (bf16[3072,128]{1,0:T(8,128)(2,1)S(1)}, bf16[3072,128]{1,0:T(8,128)(2,1)S(1)}, u32[]{:S(2)}, u32[]{:S(2)}) collective-permute-start(bf16[3072,128]{1,0:T(8,128)(2,1)S(1)} %bitcast.12), channel_id=1, source_target_pairs={{0,12},{4,8},{8,4},{12,0},{1,13},{5,9},{9,5},{13,1},{2,14},{6,10},... | collective-permute-start | bytes 2359304 | tf_op jit(solution)/shard_map/ppermute | solution.py:290
  73.0 10.0 %collective-permute-done.near_ref = bf16[3072,128]{1,0:T(8,128)(2,1)S(1)} collective-permute-done((bf16[3072,128]{1,0:T(8,128)(2,1)S(1)}, bf16[3072,128]{1,0:T(8,128)(2,1)S(1)}, u32[]{:S(2)}, u32[]{:S(2)}) %collective-permute-start) | collective-permute-done | bytes 786464 | tf_op jit(solution)/shard_map/ppermute | solution.py:289
  83.0 4.2 %collective-permute-done.1.wrap_ref = bf16[3072,128]{1,0:T(8,128)(2,1)S(1)} collective-permute-done((bf16[3072,128]{1,0:T(8,128)(2,1)S(1)}, bf16[3072,128]{1,0:T(8,128)(2,1)S(1)}, u32[]{:S(2)}, u32[]{:S(2)}) %collective-permute-start.1) | collective-permute-done | bytes 786464 | tf_op jit(solution)/shard_map/ppermute | solution.py:290
  87.2 0.7 cross.1
  87.9 1.9 %collective-permute-start.3 = (f32[2,136,256]{2,1,0:T(8,128)S(1)}, f32[2,136,256]{2,1,0:T(8,128)S(1)}, u32[]{:S(2)}, u32[]{:S(2)}) collective-permute-start(f32[2,136,256]{2,1,0:T(8,128)S(1)} %cross.1), channel_id=1, source_target_pairs={{0,4},{4,0},{8,12},{12,8},{1,5},{5,1},{9,13},{13,9},{2,6},{6,2},{1... | collective-permute-start | bytes 835592 | tf_op jit(solution)/shard_map/ppermute | solution.py:291
  89.9 1.9 %gram.1 = (f32[4,32,768]{2,1,0:T(8,128)S(1)}, f32[144,768]{1,0:T(8,128)S(1)}, f32[16,768]{1,0:T(8,128)S(1)}) custom-call(s32[1]{0:T(128)} %bitcast.core_ref, bf16[3072,128]{1,0:T(8,128)(2,1)S(1)} %bitcast.13, bf16[3072,128]{1,0:T(8,128)(2,1)S(1)} %collective-permute-done.near_ref, bf16[3072,128]{1,0:T(8,128)(2,1)S(1)} %collective-permute-done.1.wrap_ref), custom_call_target="tpu_custom_call" | custom-call | tf_op jit(solution)/shard_map/gram/pallas_call | solution.py:215
  91.7 7.0 %collective-permute-start.2 = (f32[144,768]{1,0:T(8,128)S(1)}, f32[144,768]{1,0:T(8,128)S(1)}, u32[]{:S(2)}, u32[]{:S(2)}) collective-permute-start(f32[144,768]{1,0:T(8,128)S(1)} %get-tuple-element.12), channel_id=1, source_target_pairs={{0,16},{16,0},{1,17},{17,1},{2,18},{18,2},{3,19},{19,3},{4,20},{20... | collective-permute-start | bytes 1327112 | tf_op jit(solution)/shard_map/ppermute | solution.py:293
  98.7 0.0 collective-permute-done.3.far_ref
  98.7 4.6 %collective-permute-start.4 = (f32[136,256]{1,0:T(8,128)S(1)}, f32[136,256]{1,0:T(8,128)S(1)}, u32[]{:S(2)}, u32[]{:S(2)}) collective-permute-start(f32[136,256]{1,0:T(8,128)S(1)} %slice_bitcast_fusion), channel_id=1, source_target_pairs={{0,16},{16,0},{1,17},{17,1},{2,18},{18,2},{3,19},{19,3},{4,20},{20... | collective-permute-start | bytes 417800 | tf_op jit(solution)/shard_map/ppermute | solution.py:294
  103.4 0.1 stack.23.at_ref
  103.5 0.9 collective-permute-done.4.far_got_ref
  104.4 0.0 collective-permute-done.2.got_ref
  104.4 0.2 scale.1
  104.5 12.6 %all_to_all.11.rows_ref = f32[4,32,1024]{2,1,0:T(8,128)S(1)} all-to-all(f32[4,32,1024]{2,1,0:T(8,128)S(1)} %scale.1), channel_id=1, replica_groups=mesh['z'=16,'c'=2,'y'=4,'x'=4] {'x'}, dimensions={0} | all-to-all | bytes 1048576 | tf_op jit(solution)/shard_map/all_to_all | solution.py:298
  117.1 3.7 %collective-permute-start.5 = (f32[2,32,1024]{2,1,0:T(8,128)S(1)}, f32[2,32,1024]{2,1,0:T(8,128)S(1)}, u32[]{:S(2)}, u32[]{:S(2)}) collective-permute-start(f32[2,32,1024]{2,1,0:T(8,128)S(1)} %constant_dynamic-slice_fusion), channel_id=1, source_target_pairs={{0,16},{16,0},{1,17},{17,1},{2,18},{18,2},{3,19},{19,3},{4,20},{20... | collective-permute-start | bytes 786440 | tf_op jit(solution)/shard_map/ppermute | solution.py:299
  120.8 1.1 collective-permute-done.5.swap_ref
  122.0 1.4 %place.1 = f32[2,64,1024]{2,1,0:T(8,128)} custom-call(s32[5]{0:T(128)S(1)} %stack.23.at_ref, f32[4,32,1024]{2,1,0:T(8,128)S(1)} %all_to_all.11.rows_ref, f32[2,32,1024]{2,1,0:T(8,128)S(1)} %collective-permute-done.5.swap_ref), custom_call_target="tpu_custom_call" | custom-call | tf_op jit(solution)/shard_map/place/pallas_call | solution.py:269
  (2 shorter events, 0.0 us)
Async XLA Ops:
  66.0 17.0 %collective-permute-start = (bf16[3072,128]{1,0:T(8,128)(2,1)S(1)}, bf16[3072,128]{1,0:T(8,128)(2,1)S(1)}, u32[]{:S(2)}, u32[]{:S(2)}) collective-permute-start(bf16[3072,128]{1,0:T(8,128)(2,1)S(1)} %bitcast.11), channel_id=1, source_target_pairs={{0,4},{4,0},{8,12},{12,8},{1,5},{5,1},{9,13},{13,9},{2,6},{6,2},{1... | collective-permute-start | bytes 2359304 | tf_op jit(solution)/shard_map/ppermute | solution.py:289
  69.2 18.0 %collective-permute-start.1 = (bf16[3072,128]{1,0:T(8,128)(2,1)S(1)}, bf16[3072,128]{1,0:T(8,128)(2,1)S(1)}, u32[]{:S(2)}, u32[]{:S(2)}) collective-permute-start(bf16[3072,128]{1,0:T(8,128)(2,1)S(1)} %bitcast.12), channel_id=1, source_target_pairs={{0,12},{4,8},{8,4},{12,0},{1,13},{5,9},{9,5},{13,1},{2,14},{6,10},... | collective-permute-start | bytes 2359304 | tf_op jit(solution)/shard_map/ppermute | solution.py:290
  87.9 10.8 %collective-permute-start.3 = (f32[2,136,256]{2,1,0:T(8,128)S(1)}, f32[2,136,256]{2,1,0:T(8,128)S(1)}, u32[]{:S(2)}, u32[]{:S(2)}) collective-permute-start(f32[2,136,256]{2,1,0:T(8,128)S(1)} %cross.1), channel_id=1, source_target_pairs={{0,4},{4,0},{8,12},{12,8},{1,5},{5,1},{9,13},{13,9},{2,6},{6,2},{1... | collective-permute-start | bytes 835592 | tf_op jit(solution)/shard_map/ppermute | solution.py:291
  91.7 12.6 %collective-permute-start.2 = (f32[144,768]{1,0:T(8,128)S(1)}, f32[144,768]{1,0:T(8,128)S(1)}, u32[]{:S(2)}, u32[]{:S(2)}) collective-permute-start(f32[144,768]{1,0:T(8,128)S(1)} %get-tuple-element.12), channel_id=1, source_target_pairs={{0,16},{16,0},{1,17},{17,1},{2,18},{18,2},{3,19},{19,3},{4,20},{20... | collective-permute-start | bytes 1327112 | tf_op jit(solution)/shard_map/ppermute | solution.py:293
  98.7 5.6 %collective-permute-start.4 = (f32[136,256]{1,0:T(8,128)S(1)}, f32[136,256]{1,0:T(8,128)S(1)}, u32[]{:S(2)}, u32[]{:S(2)}) collective-permute-start(f32[136,256]{1,0:T(8,128)S(1)} %slice_bitcast_fusion), channel_id=1, source_target_pairs={{0,16},{16,0},{1,17},{17,1},{2,18},{18,2},{3,19},{19,3},{4,20},{20... | collective-permute-start | bytes 417800 | tf_op jit(solution)/shard_map/ppermute | solution.py:294
  117.1 4.9 %collective-permute-start.5 = (f32[2,32,1024]{2,1,0:T(8,128)S(1)}, f32[2,32,1024]{2,1,0:T(8,128)S(1)}, u32[]{:S(2)}, u32[]{:S(2)}) collective-permute-start(f32[2,32,1024]{2,1,0:T(8,128)S(1)} %constant_dynamic-slice_fusion), channel_id=1, source_target_pairs={{0,16},{16,0},{1,17},{17,1},{2,18},{18,2},{3,19},{19,3},{4,20},{20... | collective-permute-start | bytes 786440 | tf_op jit(solution)/shard_map/ppermute | solution.py:299

commit v9 on v8

--- a/solution.py
+++ b/solution.py
@@ -165,24 +165,24 @@
         yield e, fold(even, even, odd, odd)
 
 
-def cross_kernel(core_ref, near_ref, wrap_ref, far_ref):
+def cross_kernel(core_ref, near_ref, wrap_ref, same_ref, flip_ref):
     first = core_ref[0] == 0
     near, wrap = matrix(near_ref), matrix(wrap_ref)
     for x, e, part in products(near, wrap):
         lanes = slice(e * 128, e * 128 + 128)
-        far_ref[0, x * 32:(x + 1) * 32, lanes] = jnp.where(first, part[:32], part[32:])
-        far_ref[1, x * 32:(x + 1) * 32, lanes] = jnp.where(first, part[32:], part[:32])
+        same_ref[x * 32:(x + 1) * 32, lanes] = jnp.where(first, part[:32], part[32:])
+        flip_ref[x * 32:(x + 1) * 32, lanes] = jnp.where(first, part[32:], part[:32])
     for e, part in totals(wrap):
-        for half in range(2):
-            far_ref[half, 128:, e * 128:e * 128 + 128] = part
+        same_ref[128:, e * 128:e * 128 + 128] = part
+        flip_ref[128:, e * 128:e * 128 + 128] = part
 
 
 def cross(core, near, wrap):
     return pl.pallas_call(
         cross_kernel,
-        out_shape=jax.ShapeDtypeStruct((2, 136, 256), jnp.float32),
+        out_shape=(jax.ShapeDtypeStruct((136, 256), jnp.float32),) * 2,
         in_specs=[pl.BlockSpec(memory_space=pltpu.SMEM)] + [pl.BlockSpec(memory_space=pltpu.VMEM)] * 2,
-        out_specs=pl.BlockSpec(memory_space=pltpu.VMEM),
+        out_specs=(pl.BlockSpec(memory_space=pltpu.VMEM),) * 2,
         compiler_params=pltpu.CompilerParams(vmem_limit_bytes=16 << 20),
         name="cross",
     )(core, near, wrap)
@@ -227,7 +227,7 @@
 def scale_kernel(core_ref, keep_ref, got_ref, own_ref, far_ref, far_got_ref, rows_ref):
     first = core_ref[0] == 0
     sums = own_ref[...] + got_ref[128:, :]
-    far_sums = far_ref[0, 128:, :] + far_got_ref[128:, :]
+    far_sums = far_ref[128:, :] + far_got_ref[128:, :]
     count = sums[8:9, :256]
     tall = [jnp.broadcast_to(sums[0:1, 256 + e * 128:384 + e * 128], (128, 128)).T for e in range(2)]
     tall = jnp.concatenate(tall, axis=0)
@@ -239,7 +239,7 @@
             lanes = slice(group * 256, group * 256 + 256)
             value = keep_ref[x, :, lanes] + got_ref[rows, lanes]
             rows_ref[x, :, lanes] = count * value / (mine * sums[0:1, lanes])
-        value = far_ref[0, rows, :] + far_got_ref[rows, :]
+        value = far_ref[rows, :] + far_got_ref[rows, :]
         rows_ref[x, :, 768:] = count * value / (mine * far_sums[0:1, :])
 
 
@@ -288,10 +288,11 @@
     mine = lax.all_to_all(packed, ("x", "z"), 0, 0, tiled=True).reshape(4 * DEPTH, 128)
     near = lax.ppermute(mine, "y", NEAR)
     wrap = lax.ppermute(mine, "y", WRAP)
-    far = lax.ppermute(cross(core[None], near, wrap), "y", NEAR)
+    same, flip = cross(core[None], near, wrap)
+    far_got = lax.ppermute(flip, ("c", "y"), [(4 * c + a, 4 * (1 - c) + b) for c in range(2) for a, b in NEAR])
+    far = lax.ppermute(same, "y", NEAR)
     keep, send, own = gram(core[None], mine, near, wrap)
     got = lax.ppermute(send, "c", SWAP)
-    far_got = lax.ppermute(far[1], "c", SWAP)
     at, second, rows = lax.optimization_barrier(
         (jnp.stack([core, row ^ 1, row, 3 - row, (row + 2) % 4]), 2 - 2 * core,
          scale(core[None], keep, got, own, far, far_got)))

time: 124 us -> 127 us (1.024)
  waiting for transfers between devices: 16.2 us -> 20 us
  starting transfers between devices: 24.2 us -> 22.7 us
    ppermute x2, waiting for transfers between devices: 0.87 us -> 4.69 us  [the longest x1 3.17 us: shards(): lax.ppermute(flip, ('c', 'y'), [(4 * c + a, 4 * (1 - c) + b) for c in ran...]
  transfers between devices with their start and end apart: 6 -> 6, of which waited for: 4 -> 5; matrix products, arithmetic and copies ran while one was open for 0% -> 0% of each run, Pallas kernels for 2% -> 1%
where the time goes in v9:
time: 127 us; the launch traced here: 126 us
  blocking collectives  71.9 us (57%)
  starting transfers between devices  22.7 us (18%)
  waiting for transfers between devices  20 us (16%)
  Pallas kernels  11.3 us (9%)
    all_to_all x1, blocking collectives, shards(): lax.all_to_all(packed, ('x', 'z'), 0, 0, tiled=True).reshape(4 * DEPTH, 128)  58.8 us
    all_to_all x1, blocking collectives, shards(): rows = lax.all_to_all(rows, 'x', 0, 0, tiled=True)  13 us
    ppermute x1, waiting for transfers between devices, shards(): near = lax.ppermute(mine, 'y', NEAR)  10 us
    pallas_call x1, Pallas kernels, pack(): pl.pallas_call(pack_kernel, out_shape=jax.ShapeDtypeStruct((DESTS, PART,...  7.18 us
    ppermute x1, starting transfers between devices, shards(): got = lax.ppermute(send, 'c', SWAP)  6.98 us
    ppermute x1, waiting for transfers between devices, shards(): wrap = lax.ppermute(mine, 'y', WRAP)  4.16 us
    ppermute x1, starting transfers between devices, shards(): wrap = lax.ppermute(mine, 'y', WRAP)  3.8 us
    ppermute x1, starting transfers between devices, shards(): lax.ppermute(flip, ('c', 'y'), [(4 * c + a, 4 * (1 - c) + b) for c in ran...  3.55 us
  transfers between devices with their start and end apart: 6, of which 5 were waited for; matrix products, arithmetic and copies ran while one was open for 0% of the time, Pallas kernels for 1%

profile of v9, /device:TPU:1, one launch (start us, length us, event | category | flops | bytes accessed | tf_op | source)
XLA Modules:
  0.0 126.1 jit_solution(17926801179605086268)
XLA Ops:
  0.0 7.2 %pack.1 = bf16[64,48,128]{2,1,0:T(8,128)(2,1)S(1)} custom-call(f32[16,64]{1,0:T(8,128)} %bitcast.13, s32[1,64]{1,0:T(1,128)} %bitcast.14, s32[64,128]{1,0:T(8,128)} %bitcast.12, bf16[16,8192]{1,0:T(8,128)(2,1)} %eigen_hbm.1, bf16[64,8192]{1,0:T(8,128)(2,1)} %raw_hbm.1), custom_call_target="tpu_custom_call" | custom-call | tf_op jit(solution)/shard_map/pack/pallas_call | solution.py:117
  7.2 58.8 %all_to_all.10 = bf16[64,48,128]{2,1,0:T(8,128)(2,1)S(1)} all-to-all(bf16[64,48,128]{2,1,0:T(8,128)(2,1)S(1)} %pack.1), channel_id=1, replica_groups=mesh['z'=16,'c'=2,'y'=4,'x'=4] {'x','z'}, dimensions={0} | all-to-all | bytes 1572864 | tf_op jit(solution)/shard_map/all_to_all | solution.py:288
  66.0 3.2 %collective-permute-start = (bf16[3072,128]{1,0:T(8,128)(2,1)S(1)}, bf16[3072,128]{1,0:T(8,128)(2,1)S(1)}, u32[]{:S(2)}, u32[]{:S(2)}) collective-permute-start(bf16[3072,128]{1,0:T(8,128)(2,1)S(1)} %bitcast.9), channel_id=1, source_target_pairs={{0,4},{4,0},{8,12},{12,8},{1,5},{5,1},{9,13},{13,9},{2,6},{6,2},{1... | collective-permute-start | bytes 2359304 | tf_op jit(solution)/shard_map/ppermute | solution.py:289
  69.2 3.8 %collective-permute-start.1 = (bf16[3072,128]{1,0:T(8,128)(2,1)S(1)}, bf16[3072,128]{1,0:T(8,128)(2,1)S(1)}, u32[]{:S(2)}, u32[]{:S(2)}) collective-permute-start(bf16[3072,128]{1,0:T(8,128)(2,1)S(1)} %bitcast.10), channel_id=1, source_target_pairs={{0,12},{4,8},{8,4},{12,0},{1,13},{5,9},{9,5},{13,1},{2,14},{6,10},... | collective-permute-start | bytes 2359304 | tf_op jit(solution)/shard_map/ppermute | solution.py:290
  73.0 10.0 %collective-permute-done.near_ref = bf16[3072,128]{1,0:T(8,128)(2,1)S(1)} collective-permute-done((bf16[3072,128]{1,0:T(8,128)(2,1)S(1)}, bf16[3072,128]{1,0:T(8,128)(2,1)S(1)}, u32[]{:S(2)}, u32[]{:S(2)}) %collective-permute-start) | collective-permute-done | bytes 786464 | tf_op jit(solution)/shard_map/ppermute | solution.py:289
  83.1 4.2 %collective-permute-done.1.wrap_ref = bf16[3072,128]{1,0:T(8,128)(2,1)S(1)} collective-permute-done((bf16[3072,128]{1,0:T(8,128)(2,1)S(1)}, bf16[3072,128]{1,0:T(8,128)(2,1)S(1)}, u32[]{:S(2)}, u32[]{:S(2)}) %collective-permute-start.1) | collective-permute-done | bytes 786464 | tf_op jit(solution)/shard_map/ppermute | solution.py:290
  87.2 1.9 %gram.1 = (f32[4,32,768]{2,1,0:T(8,128)S(1)}, f32[144,768]{1,0:T(8,128)S(1)}, f32[16,768]{1,0:T(8,128)S(1)}) custom-call(s32[1]{0:T(128)} %bitcast.core_ref, bf16[3072,128]{1,0:T(8,128)(2,1)S(1)} %bitcast.11, bf16[3072,128]{1,0:T(8,128)(2,1)S(1)} %collective-permute-done.near_ref, bf16[3072,128]{1,0:T(8,128)(2,1)S(1)} %collective-permute-done.1.wrap_ref), custom_call_target="tpu_custom_call" | custom-call | tf_op jit(solution)/shard_map/gram/pallas_call | solution.py:215
  89.1 7.0 %collective-permute-start.2 = (f32[144,768]{1,0:T(8,128)S(1)}, f32[144,768]{1,0:T(8,128)S(1)}, u32[]{:S(2)}, u32[]{:S(2)}) collective-permute-start(f32[144,768]{1,0:T(8,128)S(1)} %get-tuple-element.14), channel_id=1, source_target_pairs={{0,16},{16,0},{1,17},{17,1},{2,18},{18,2},{3,19},{19,3},{4,20},{20... | collective-permute-start | bytes 1327112 | tf_op jit(solution)/shard_map/ppermute | solution.py:295
  96.1 0.7 cross.1
  96.8 1.9 %collective-permute-start.3 = (f32[136,256]{1,0:T(8,128)S(1)}, f32[136,256]{1,0:T(8,128)S(1)}, u32[]{:S(2)}, u32[]{:S(2)}) collective-permute-start(f32[136,256]{1,0:T(8,128)S(1)} %get-tuple-element.16), channel_id=1, source_target_pairs={{0,4},{4,0},{8,12},{12,8},{1,5},{5,1},{9,13},{13,9},{2,6},{6,2},{1... | collective-permute-start | bytes 417800 | tf_op jit(solution)/shard_map/ppermute | solution.py:293
  98.7 3.5 %collective-permute-start.4 = (f32[136,256]{1,0:T(8,128)S(1)}, f32[136,256]{1,0:T(8,128)S(1)}, u32[]{:S(2)}, u32[]{:S(2)}) collective-permute-start(f32[136,256]{1,0:T(8,128)S(1)} %get-tuple-element.17), channel_id=1, source_target_pairs={{0,20},{4,16},{8,28},{12,24},{16,4},{20,0},{24,12},{28,8},{1,21},{... | collective-permute-start | bytes 417800 | tf_op jit(solution)/shard_map/ppermute | solution.py:292
  102.3 0.1 stack.23.at_ref
  102.4 1.5 %collective-permute-done.3.far_ref = f32[136,256]{1,0:T(8,128)S(1)} collective-permute-done((f32[136,256]{1,0:T(8,128)S(1)}, f32[136,256]{1,0:T(8,128)S(1)}, u32[]{:S(2)}, u32[]{:S(2)}) %collective-permute-start.3) | collective-permute-done | bytes 139296 | tf_op jit(solution)/shard_map/ppermute | solution.py:293
  103.9 3.2 %collective-permute-done.4.far_got_ref = f32[136,256]{1,0:T(8,128)S(1)} collective-permute-done((f32[136,256]{1,0:T(8,128)S(1)}, f32[136,256]{1,0:T(8,128)S(1)}, u32[]{:S(2)}, u32[]{:S(2)}) %collective-permute-start.4) | collective-permute-done | bytes 139296 | tf_op jit(solution)/shard_map/ppermute | solution.py:292
  107.1 0.0 collective-permute-done.2.got_ref
  107.1 0.2 scale.1
  107.2 13.0 %all_to_all.11.rows_ref = f32[4,32,1024]{2,1,0:T(8,128)S(1)} all-to-all(f32[4,32,1024]{2,1,0:T(8,128)S(1)} %scale.1), channel_id=1, replica_groups=mesh['z'=16,'c'=2,'y'=4,'x'=4] {'x'}, dimensions={0} | all-to-all | bytes 1048576 | tf_op jit(solution)/shard_map/all_to_all | solution.py:299
  120.3 3.3 %collective-permute-start.5 = (f32[2,32,1024]{2,1,0:T(8,128)S(1)}, f32[2,32,1024]{2,1,0:T(8,128)S(1)}, u32[]{:S(2)}, u32[]{:S(2)}) collective-permute-start(f32[2,32,1024]{2,1,0:T(8,128)S(1)} %constant_dynamic-slice_fusion), channel_id=1, source_target_pairs={{0,16},{16,0},{1,17},{17,1},{2,18},{18,2},{3,19},{19,3},{4,20},{20... | collective-permute-start | bytes 786440 | tf_op jit(solution)/shard_map/ppermute | solution.py:300
  123.6 1.1 collective-permute-done.5.swap_ref
  124.7 1.4 %place.1 = f32[2,64,1024]{2,1,0:T(8,128)} custom-call(s32[5]{0:T(128)S(1)} %stack.23.at_ref, f32[4,32,1024]{2,1,0:T(8,128)S(1)} %all_to_all.11.rows_ref, f32[2,32,1024]{2,1,0:T(8,128)S(1)} %collective-permute-done.5.swap_ref), custom_call_target="tpu_custom_call" | custom-call | tf_op jit(solution)/shard_map/place/pallas_call | solution.py:269
  (1 shorter events, 0.0 us)
Async XLA Ops:
  66.0 17.0 %collective-permute-start = (bf16[3072,128]{1,0:T(8,128)(2,1)S(1)}, bf16[3072,128]{1,0:T(8,128)(2,1)S(1)}, u32[]{:S(2)}, u32[]{:S(2)}) collective-permute-start(bf16[3072,128]{1,0:T(8,128)(2,1)S(1)} %bitcast.9), channel_id=1, source_target_pairs={{0,4},{4,0},{8,12},{12,8},{1,5},{5,1},{9,13},{13,9},{2,6},{6,2},{1... | collective-permute-start | bytes 2359304 | tf_op jit(solution)/shard_map/ppermute | solution.py:289
  69.2 18.0 %collective-permute-start.1 = (bf16[3072,128]{1,0:T(8,128)(2,1)S(1)}, bf16[3072,128]{1,0:T(8,128)(2,1)S(1)}, u32[]{:S(2)}, u32[]{:S(2)}) collective-permute-start(bf16[3072,128]{1,0:T(8,128)(2,1)S(1)} %bitcast.10), channel_id=1, source_target_pairs={{0,12},{4,8},{8,4},{12,0},{1,13},{5,9},{9,5},{13,1},{2,14},{6,10},... | collective-permute-start | bytes 2359304 | tf_op jit(solution)/shard_map/ppermute | solution.py:290
  89.1 18.0 %collective-permute-start.2 = (f32[144,768]{1,0:T(8,128)S(1)}, f32[144,768]{1,0:T(8,128)S(1)}, u32[]{:S(2)}, u32[]{:S(2)}) collective-permute-start(f32[144,768]{1,0:T(8,128)S(1)} %get-tuple-element.14), channel_id=1, source_target_pairs={{0,16},{16,0},{1,17},{17,1},{2,18},{18,2},{3,19},{19,3},{4,20},{20... | collective-permute-start | bytes 1327112 | tf_op jit(solution)/shard_map/ppermute | solution.py:295
  96.8 7.1 %collective-permute-start.3 = (f32[136,256]{1,0:T(8,128)S(1)}, f32[136,256]{1,0:T(8,128)S(1)}, u32[]{:S(2)}, u32[]{:S(2)}) collective-permute-start(f32[136,256]{1,0:T(8,128)S(1)} %get-tuple-element.16), channel_id=1, source_target_pairs={{0,4},{4,0},{8,12},{12,8},{1,5},{5,1},{9,13},{13,9},{2,6},{6,2},{1... | collective-permute-start | bytes 417800 | tf_op jit(solution)/shard_map/ppermute | solution.py:293
  98.7 8.3 %collective-permute-start.4 = (f32[136,256]{1,0:T(8,128)S(1)}, f32[136,256]{1,0:T(8,128)S(1)}, u32[]{:S(2)}, u32[]{:S(2)}) collective-permute-start(f32[136,256]{1,0:T(8,128)S(1)} %get-tuple-element.17), channel_id=1, source_target_pairs={{0,20},{4,16},{8,28},{12,24},{16,4},{20,0},{24,12},{28,8},{1,21},{... | collective-permute-start | bytes 417800 | tf_op jit(solution)/shard_map/ppermute | solution.py:292
  120.3 4.4 %collective-permute-start.5 = (f32[2,32,1024]{2,1,0:T(8,128)S(1)}, f32[2,32,1024]{2,1,0:T(8,128)S(1)}, u32[]{:S(2)}, u32[]{:S(2)}) collective-permute-start(f32[2,32,1024]{2,1,0:T(8,128)S(1)} %constant_dynamic-slice_fusion), channel_id=1, source_target_pairs={{0,16},{16,0},{1,17},{17,1},{2,18},{18,2},{3,19},{19,3},{4,20},{20... | collective-permute-start | bytes 786440 | tf_op jit(solution)/shard_map/ppermute | solution.py:300

commit v10 on v8

--- a/solution.py
+++ b/solution.py
@@ -149,8 +149,7 @@
         jnp.where(left, odd_top, even_low), FRAMES, 1)
 
 
-def products(a, b):
-    full = lax.dot_general(a, b, (((0,), (0,)), ((), ())), preferred_element_type=jnp.float32)
+def products(full):
     for x in range(4):
         top, low = slice(x * 128, x * 128 + 64), slice(x * 128 + 64, x * 128 + 128)
         for e in range(2):
@@ -168,7 +167,8 @@
 def cross_kernel(core_ref, near_ref, wrap_ref, far_ref):
     first = core_ref[0] == 0
     near, wrap = matrix(near_ref), matrix(wrap_ref)
-    for x, e, part in products(near, wrap):
+    full = lax.dot_general(near, wrap, (((0,), (0,)), ((), ())), preferred_element_type=jnp.float32)
+    for x, e, part in products(full):
         lanes = slice(e * 128, e * 128 + 128)
         far_ref[0, x * 32:(x + 1) * 32, lanes] = jnp.where(first, part[:32], part[32:])
         far_ref[1, x * 32:(x + 1) * 32, lanes] = jnp.where(first, part[32:], part[:32])
@@ -188,13 +188,44 @@
     )(core, near, wrap)
 
 
-def gram_kernel(core_ref, mine_ref, near_ref, wrap_ref, keep_ref, send_ref, own_ref):
+def self_kernel(core_ref, mine_ref, turned_ref, keep_ref, send_ref):
     f32, bf16 = jnp.float32, jnp.bfloat16
     first = core_ref[0] == 0
     mine = matrix(mine_ref)
-    for group, ref in enumerate((near_ref, mine_ref, wrap_ref)):
+    turned = mine.T
+    turned_ref[...] = turned
+    for x, e, part in products(jnp.dot(turned, mine, preferred_element_type=f32)):
+        lanes = slice(e * 128, e * 128 + 128)
+        keep_ref[x, :, lanes] = jnp.where(first, part[:32], part[32:])
+        send_ref[x * 32:(x + 1) * 32, lanes] = jnp.where(first, part[32:], part[:32])
+    for e, part in totals(mine):
+        send_ref[128:136, e * 128:e * 128 + 128] = part
+    hits = jnp.where(mine_ref[:DEPTH, :].astype(f32) != 0.0, 1.0, 0.0).astype(bf16)
+    hits = jnp.dot(jnp.ones((8, DEPTH), bf16), hits, preferred_element_type=f32)
+    hits = hits + pltpu.roll(hits, FRAMES, 1)
+    send_ref[136:, :] = jnp.concatenate([hits, hits], axis=1)
+
+
+def self_gram(core, mine):
+    f32 = jnp.float32
+    return pl.pallas_call(
+        self_kernel,
+        out_shape=(jax.ShapeDtypeStruct((512, DEPTH), jnp.bfloat16),
+                   jax.ShapeDtypeStruct((4, 32, 256), f32),
+                   jax.ShapeDtypeStruct((144, 256), f32)),
+        in_specs=[pl.BlockSpec(memory_space=pltpu.SMEM), pl.BlockSpec(memory_space=pltpu.VMEM)],
+        out_specs=(pl.BlockSpec(memory_space=pltpu.VMEM),) * 3,
+        compiler_params=pltpu.CompilerParams(vmem_limit_bytes=16 << 20),
+        name="self_gram",
+    )(core, mine)
+
+
+def gram_kernel(core_ref, turned_ref, near_ref, wrap_ref, self_keep_ref, self_send_ref, keep_ref, send_ref, own_ref):
+    first = core_ref[0] == 0
+    turned = turned_ref[...]
+    for group, ref in ((0, near_ref), (2, wrap_ref)):
         other = matrix(ref)
-        for x, e, part in products(mine, other):
+        for x, e, part in products(jnp.dot(turned, other, preferred_element_type=jnp.float32)):
             lanes = slice(group * 256 + e * 128, group * 256 + e * 128 + 128)
             keep_ref[x, :, lanes] = jnp.where(first, part[:32], part[32:])
             send_ref[x * 32:(x + 1) * 32, lanes] = jnp.where(first, part[32:], part[:32])
@@ -202,26 +233,27 @@
             lanes = slice(group * 256 + e * 128, group * 256 + e * 128 + 128)
             own_ref[:8, lanes] = part
             send_ref[128:136, lanes] = part
-    hits = jnp.where(mine_ref[:DEPTH, :].astype(f32) != 0.0, 1.0, 0.0).astype(bf16)
-    hits = jnp.dot(jnp.ones((8, DEPTH), bf16), hits, preferred_element_type=f32)
-    hits = hits + pltpu.roll(hits, FRAMES, 1)
-    hits = jnp.concatenate([hits] * 6, axis=1)
+    for x in range(4):
+        keep_ref[x, :, 256:512] = self_keep_ref[x]
+    send_ref[:136, 256:512] = self_send_ref[:136, :]
+    own_ref[:8, 256:512] = self_send_ref[128:136, :]
+    hits = jnp.concatenate([self_send_ref[136:, :]] * 3, axis=1)
     own_ref[8:, :] = hits
     send_ref[136:, :] = hits
 
 
-def gram(core, mine, near, wrap):
+def gram(core, turned, near, wrap, self_keep, self_send):
     f32 = jnp.float32
     return pl.pallas_call(
         gram_kernel,
         out_shape=(jax.ShapeDtypeStruct((4, 32, 768), f32),
                    jax.ShapeDtypeStruct((144, 768), f32),
                    jax.ShapeDtypeStruct((16, 768), f32)),
-        in_specs=[pl.BlockSpec(memory_space=pltpu.SMEM)] + [pl.BlockSpec(memory_space=pltpu.VMEM)] * 3,
+        in_specs=[pl.BlockSpec(memory_space=pltpu.SMEM)] + [pl.BlockSpec(memory_space=pltpu.VMEM)] * 5,
         out_specs=(pl.BlockSpec(memory_space=pltpu.VMEM),) * 3,
-        compiler_params=pltpu.CompilerParams(vmem_limit_bytes=24 << 20),
+        compiler_params=pltpu.CompilerParams(vmem_limit_bytes=16 << 20),
         name="gram",
-    )(core, mine, near, wrap)
+    )(core, turned, near, wrap, self_keep, self_send)
 
 
 def scale_kernel(core_ref, keep_ref, got_ref, own_ref, far_ref, far_got_ref, rows_ref):
@@ -288,8 +320,9 @@
     mine = lax.all_to_all(packed, ("x", "z"), 0, 0, tiled=True).reshape(4 * DEPTH, 128)
     near = lax.ppermute(mine, "y", NEAR)
     wrap = lax.ppermute(mine, "y", WRAP)
+    turned, self_keep, self_send = self_gram(core[None], mine)
     far = lax.ppermute(cross(core[None], near, wrap), "y", NEAR)
-    keep, send, own = gram(core[None], mine, near, wrap)
+    keep, send, own = gram(core[None], turned, near, wrap, self_keep, self_send)
     got = lax.ppermute(send, "c", SWAP)
     far_got = lax.ppermute(far[1], "c", SWAP)
     at, second, rows = lax.optimization_barrier(

time: 124 us -> 124 us (level)
  no operation moved by 1% of the time
where the time goes in v10:
time: 124 us; the launch traced here: 123 us
  blocking collectives  71.4 us (58%)
  starting transfers between devices  24 us (19%)
  waiting for transfers between devices  16.2 us (13%)
  Pallas kernels  11.5 us (9%)
    all_to_all x1, blocking collectives, shards(): lax.all_to_all(packed, ('x', 'z'), 0, 0, tiled=True).reshape(4 * DEPTH, 128)  58.8 us
    all_to_all x1, blocking collectives, shards(): rows = lax.all_to_all(rows, 'x', 0, 0, tiled=True)  12.6 us
    ppermute x1, waiting for transfers between devices, shards(): near = lax.ppermute(mine, 'y', NEAR)  10 us
    pallas_call x1, Pallas kernels, pack(): pl.pallas_call(pack_kernel, out_shape=jax.ShapeDtypeStruct((DESTS, PART,...  7.18 us
    ppermute x1, starting transfers between devices, shards(): got = lax.ppermute(send, 'c', SWAP)  6.98 us
    ppermute x1, starting transfers between devices, shards(): far_got = lax.ppermute(far[1], 'c', SWAP)  4.44 us
    ppermute x1, waiting for transfers between devices, shards(): wrap = lax.ppermute(mine, 'y', WRAP)  4.14 us
    ppermute x1, starting transfers between devices, shards(): wrap = lax.ppermute(mine, 'y', WRAP)  3.8 us
  transfers between devices with their start and end apart: 6, of which 4 were waited for; matrix products, arithmetic and copies ran while one was open for 0% of the time, Pallas kernels for 2%

profile of v10, /device:TPU:1, one launch (start us, length us, event | category | flops | bytes accessed | tf_op | source)
XLA Modules:
  0.0 123.4 jit_solution(4041670388738877532)
XLA Ops:
  0.0 7.2 %pack.1 = bf16[64,48,128]{2,1,0:T(8,128)(2,1)S(1)} custom-call(f32[16,64]{1,0:T(8,128)} %bitcast.15, s32[1,64]{1,0:T(1,128)} %bitcast.16, s32[64,128]{1,0:T(8,128)} %bitcast.14, bf16[16,8192]{1,0:T(8,128)(2,1)} %eigen_hbm.1, bf16[64,8192]{1,0:T(8,128)(2,1)} %raw_hbm.1), custom_call_target="tpu_custom_call" | custom-call | tf_op jit(solution)/shard_map/pack/pallas_call | solution.py:117
  7.2 58.8 %all_to_all.10 = bf16[64,48,128]{2,1,0:T(8,128)(2,1)S(1)} all-to-all(bf16[64,48,128]{2,1,0:T(8,128)(2,1)S(1)} %pack.1), channel_id=1, replica_groups=mesh['z'=16,'c'=2,'y'=4,'x'=4] {'x','z'}, dimensions={0} | all-to-all | bytes 1572864 | tf_op jit(solution)/shard_map/all_to_all | solution.py:320
  66.0 3.2 %collective-permute-start = (bf16[3072,128]{1,0:T(8,128)(2,1)S(1)}, bf16[3072,128]{1,0:T(8,128)(2,1)S(1)}, u32[]{:S(2)}, u32[]{:S(2)}) collective-permute-start(bf16[3072,128]{1,0:T(8,128)(2,1)S(1)} %bitcast.11), channel_id=1, source_target_pairs={{0,4},{4,0},{8,12},{12,8},{1,5},{5,1},{9,13},{13,9},{2,6},{6,2},{1... | collective-permute-start | bytes 2359304 | tf_op jit(solution)/shard_map/ppermute | solution.py:321
  69.2 3.8 %collective-permute-start.1 = (bf16[3072,128]{1,0:T(8,128)(2,1)S(1)}, bf16[3072,128]{1,0:T(8,128)(2,1)S(1)}, u32[]{:S(2)}, u32[]{:S(2)}) collective-permute-start(bf16[3072,128]{1,0:T(8,128)(2,1)S(1)} %bitcast.12), channel_id=1, source_target_pairs={{0,12},{4,8},{8,4},{12,0},{1,13},{5,9},{9,5},{13,1},{2,14},{6,10},... | collective-permute-start | bytes 2359304 | tf_op jit(solution)/shard_map/ppermute | solution.py:322
  73.0 10.0 %collective-permute-done.near_ref = bf16[3072,128]{1,0:T(8,128)(2,1)S(1)} collective-permute-done((bf16[3072,128]{1,0:T(8,128)(2,1)S(1)}, bf16[3072,128]{1,0:T(8,128)(2,1)S(1)}, u32[]{:S(2)}, u32[]{:S(2)}) %collective-permute-start) | collective-permute-done | bytes 786464 | tf_op jit(solution)/shard_map/ppermute | solution.py:321
  83.1 4.1 %collective-permute-done.1.wrap_ref = bf16[3072,128]{1,0:T(8,128)(2,1)S(1)} collective-permute-done((bf16[3072,128]{1,0:T(8,128)(2,1)S(1)}, bf16[3072,128]{1,0:T(8,128)(2,1)S(1)}, u32[]{:S(2)}, u32[]{:S(2)}) %collective-permute-start.1) | collective-permute-done | bytes 786464 | tf_op jit(solution)/shard_map/ppermute | solution.py:322
  87.2 0.7 cross.1
  87.9 1.9 %collective-permute-start.3 = (f32[2,136,256]{2,1,0:T(8,128)S(1)}, f32[2,136,256]{2,1,0:T(8,128)S(1)}, u32[]{:S(2)}, u32[]{:S(2)}) collective-permute-start(f32[2,136,256]{2,1,0:T(8,128)S(1)} %cross.1), channel_id=1, source_target_pairs={{0,4},{4,0},{8,12},{12,8},{1,5},{5,1},{9,13},{13,9},{2,6},{6,2},{1... | collective-permute-start | bytes 835592 | tf_op jit(solution)/shard_map/ppermute | solution.py:324
  89.9 0.8 self_gram.1
  90.6 1.3 %gram.1 = (f32[4,32,768]{2,1,0:T(8,128)S(1)}, f32[144,768]{1,0:T(8,128)S(1)}, f32[16,768]{1,0:T(8,128)S(1)}) custom-call(s32[1]{0:T(128)} %bitcast.core_ref, bf16[512,768]{1,0:T(8,128)(2,1)S(1)} %get-tuple-element.14.turned_ref, bf16[3072,128]{1,0:T(8,128)(2,1)S(1)} %collective-permute-done.near_ref, bf16[3072,128]{1,0:T(8,128)(2,1)S(1)} %collective-permute-done.1.wrap_ref, ...), custom_call_target="tpu_custom_call" | custom-call | tf_op jit(solution)/shard_map/gram/pallas_call | solution.py:247
  91.9 7.0 %collective-permute-start.2 = (f32[144,768]{1,0:T(8,128)S(1)}, f32[144,768]{1,0:T(8,128)S(1)}, u32[]{:S(2)}, u32[]{:S(2)}) collective-permute-start(f32[144,768]{1,0:T(8,128)S(1)} %get-tuple-element.18), channel_id=1, source_target_pairs={{0,16},{16,0},{1,17},{17,1},{2,18},{18,2},{3,19},{19,3},{4,20},{20... | collective-permute-start | bytes 1327112 | tf_op jit(solution)/shard_map/ppermute | solution.py:326
  98.9 0.0 collective-permute-done.3.far_ref
  98.9 4.4 %collective-permute-start.4 = (f32[136,256]{1,0:T(8,128)S(1)}, f32[136,256]{1,0:T(8,128)S(1)}, u32[]{:S(2)}, u32[]{:S(2)}) collective-permute-start(f32[136,256]{1,0:T(8,128)S(1)} %slice_bitcast_fusion), channel_id=1, source_target_pairs={{0,16},{16,0},{1,17},{17,1},{2,18},{18,2},{3,19},{19,3},{4,20},{20... | collective-permute-start | bytes 417800 | tf_op jit(solution)/shard_map/ppermute | solution.py:327
  103.4 0.1 stack.23.at_ref
  103.5 0.9 collective-permute-done.4.far_got_ref
  104.3 0.0 collective-permute-done.2.got_ref
  104.4 0.2 scale.1
  104.5 12.6 %all_to_all.11.rows_ref = f32[4,32,1024]{2,1,0:T(8,128)S(1)} all-to-all(f32[4,32,1024]{2,1,0:T(8,128)S(1)} %scale.1), channel_id=1, replica_groups=mesh['z'=16,'c'=2,'y'=4,'x'=4] {'x'}, dimensions={0} | all-to-all | bytes 1048576 | tf_op jit(solution)/shard_map/all_to_all | solution.py:331
  117.1 3.7 %collective-permute-start.5 = (f32[2,32,1024]{2,1,0:T(8,128)S(1)}, f32[2,32,1024]{2,1,0:T(8,128)S(1)}, u32[]{:S(2)}, u32[]{:S(2)}) collective-permute-start(f32[2,32,1024]{2,1,0:T(8,128)S(1)} %constant_dynamic-slice_fusion), channel_id=1, source_target_pairs={{0,16},{16,0},{1,17},{17,1},{2,18},{18,2},{3,19},{19,3},{4,20},{20... | collective-permute-start | bytes 786440 | tf_op jit(solution)/shard_map/ppermute | solution.py:332
  120.8 1.1 collective-permute-done.5.swap_ref
  122.0 1.4 %place.1 = f32[2,64,1024]{2,1,0:T(8,128)} custom-call(s32[5]{0:T(128)S(1)} %stack.23.at_ref, f32[4,32,1024]{2,1,0:T(8,128)S(1)} %all_to_all.11.rows_ref, f32[2,32,1024]{2,1,0:T(8,128)S(1)} %collective-permute-done.5.swap_ref), custom_call_target="tpu_custom_call" | custom-call | tf_op jit(solution)/shard_map/place/pallas_call | solution.py:301
  (2 shorter events, 0.0 us)
Async XLA Ops:
  66.0 17.0 %collective-permute-start = (bf16[3072,128]{1,0:T(8,128)(2,1)S(1)}, bf16[3072,128]{1,0:T(8,128)(2,1)S(1)}, u32[]{:S(2)}, u32[]{:S(2)}) collective-permute-start(bf16[3072,128]{1,0:T(8,128)(2,1)S(1)} %bitcast.11), channel_id=1, source_target_pairs={{0,4},{4,0},{8,12},{12,8},{1,5},{5,1},{9,13},{13,9},{2,6},{6,2},{1... | collective-permute-start | bytes 2359304 | tf_op jit(solution)/shard_map/ppermute | solution.py:321
  69.2 18.0 %collective-permute-start.1 = (bf16[3072,128]{1,0:T(8,128)(2,1)S(1)}, bf16[3072,128]{1,0:T(8,128)(2,1)S(1)}, u32[]{:S(2)}, u32[]{:S(2)}) collective-permute-start(bf16[3072,128]{1,0:T(8,128)(2,1)S(1)} %bitcast.12), channel_id=1, source_target_pairs={{0,12},{4,8},{8,4},{12,0},{1,13},{5,9},{9,5},{13,1},{2,14},{6,10},... | collective-permute-start | bytes 2359304 | tf_op jit(solution)/shard_map/ppermute | solution.py:322
  87.9 11.0 %collective-permute-start.3 = (f32[2,136,256]{2,1,0:T(8,128)S(1)}, f32[2,136,256]{2,1,0:T(8,128)S(1)}, u32[]{:S(2)}, u32[]{:S(2)}) collective-permute-start(f32[2,136,256]{2,1,0:T(8,128)S(1)} %cross.1), channel_id=1, source_target_pairs={{0,4},{4,0},{8,12},{12,8},{1,5},{5,1},{9,13},{13,9},{2,6},{6,2},{1... | collective-permute-start | bytes 835592 | tf_op jit(solution)/shard_map/ppermute | solution.py:324
  91.9 12.4 %collective-permute-start.2 = (f32[144,768]{1,0:T(8,128)S(1)}, f32[144,768]{1,0:T(8,128)S(1)}, u32[]{:S(2)}, u32[]{:S(2)}) collective-permute-start(f32[144,768]{1,0:T(8,128)S(1)} %get-tuple-element.18), channel_id=1, source_target_pairs={{0,16},{16,0},{1,17},{17,1},{2,18},{18,2},{3,19},{19,3},{4,20},{20... | collective-permute-start | bytes 1327112 | tf_op jit(solution)/shard_map/ppermute | solution.py:326
  98.9 5.4 %collective-permute-start.4 = (f32[136,256]{1,0:T(8,128)S(1)}, f32[136,256]{1,0:T(8,128)S(1)}, u32[]{:S(2)}, u32[]{:S(2)}) collective-permute-start(f32[136,256]{1,0:T(8,128)S(1)} %slice_bitcast_fusion), channel_id=1, source_target_pairs={{0,16},{16,0},{1,17},{17,1},{2,18},{18,2},{3,19},{19,3},{4,20},{20... | collective-permute-start | bytes 417800 | tf_op jit(solution)/shard_map/ppermute | solution.py:327
  117.1 4.9 %collective-permute-start.5 = (f32[2,32,1024]{2,1,0:T(8,128)S(1)}, f32[2,32,1024]{2,1,0:T(8,128)S(1)}, u32[]{:S(2)}, u32[]{:S(2)}) collective-permute-start(f32[2,32,1024]{2,1,0:T(8,128)S(1)} %constant_dynamic-slice_fusion), channel_id=1, source_target_pairs={{0,16},{16,0},{1,17},{17,1},{2,18},{18,2},{3,19},{19,3},{4,20},{20... | collective-permute-start | bytes 786440 | tf_op jit(solution)/shard_map/ppermute | solution.py:332

commit v11 on v8

--- a/solution.py
+++ b/solution.py
@@ -254,26 +254,39 @@
     )(core, keep, got, own, far, far_got)
 
 
-def place_kernel(at_ref, rows_ref, swap_ref, out_ref):
-    core = at_ref[0]
-    own, other = (pl.ds(pl.multiple_of(c * 32, 32), 32) for c in (core, 1 - core))
-    for group in range(4):
-        lanes = pl.ds(pl.multiple_of(at_ref[1 + group] * 256, 256), 256)
-        source = slice(group * 256, (group + 1) * 256)
-        for b in range(2):
-            out_ref[b, own, lanes] = rows_ref[2 * core + b, :, source]
-            out_ref[b, other, lanes] = swap_ref[b, :, source]
+def copy_rows(at_ref, source_ref, first, half, out_ref, sems):
+    copies = []
+    for b in range(2):
+        for group in range(4):
+            lanes = pl.ds(pl.multiple_of(at_ref[1 + group] * 256, 256), 256)
+            rows = pl.ds(pl.multiple_of(half * 32, 32), 32)
+            copies.append(pltpu.make_async_copy(
+                source_ref.at[first + b, :, group * 256:(group + 1) * 256],
+                out_ref.at[b, rows, lanes], sems.at[4 * b + group]))
+    for copy in copies:
+        copy.start()
+    for copy in copies:
+        copy.wait()
+
+
+def own_kernel(at_ref, rows_ref, out_ref, sems):
+    copy_rows(at_ref, rows_ref, 2 * at_ref[0], at_ref[0], out_ref, sems)
+
+
+def other_kernel(at_ref, swap_ref, half_ref, out_ref, sems):
+    copy_rows(at_ref, swap_ref, 0, 1 - at_ref[0], out_ref, sems)
 
 
 def place(at, rows, swap):
-    return pl.pallas_call(
-        place_kernel,
-        out_shape=jax.ShapeDtypeStruct((2, 64, 1024), jnp.float32),
-        in_specs=[pl.BlockSpec(memory_space=pltpu.SMEM)] + [pl.BlockSpec(memory_space=pltpu.VMEM)] * 2,
-        out_specs=pl.BlockSpec(memory_space=pltpu.VMEM),
-        compiler_params=pltpu.CompilerParams(vmem_limit_bytes=8 << 20),
-        name="place",
-    )(at, rows, swap)
+    smem, vmem, hbm = (pl.BlockSpec(memory_space=m) for m in (pltpu.SMEM, pltpu.VMEM, pltpu.HBM))
+    shape = jax.ShapeDtypeStruct((2, 64, 1024), jnp.float32)
+    sems = [pltpu.SemaphoreType.DMA((8,))]
+    params = pltpu.CompilerParams(vmem_limit_bytes=8 << 20)
+    half = pl.pallas_call(own_kernel, out_shape=shape, in_specs=[smem, vmem], out_specs=hbm,
+                          scratch_shapes=sems, compiler_params=params, name="own_rows")(at, rows)
+    return pl.pallas_call(other_kernel, out_shape=shape, in_specs=[smem, vmem, hbm], out_specs=hbm,
+                          scratch_shapes=sems, compiler_params=params, name="other_rows",
+                          input_output_aliases={2: 0})(at, swap, half)
 
 
 SWAP = [(0, 1), (1, 0)]

time: 124 us -> 124 us (level)
    pallas_call x1 -> x2, Pallas kernels: 1.38 us -> 2.61 us  [the longest x1 1.31 us: place(): pl.pallas_call(other_kernel, out_shape=shape, in_specs=[smem, vmem, hbm],...]
  transfers between devices with their start and end apart: 6 -> 6, of which waited for: 4 -> 3; matrix products, arithmetic and copies ran while one was open for 0% -> 0% of each run, Pallas kernels for 2% -> 3%
where the time goes in v11:
time: 124 us; the launch traced here: 123 us
  blocking collectives  71.4 us (58%)
  starting transfers between devices  24.2 us (20%)
  waiting for transfers between devices  15.1 us (12%)
  Pallas kernels  12.5 us (10%)
    all_to_all x1, blocking collectives, shards(): lax.all_to_all(packed, ('x', 'z'), 0, 0, tiled=True).reshape(4 * DEPTH, 128)  58.8 us
    all_to_all x1, blocking collectives, shards(): rows = lax.all_to_all(rows, 'x', 0, 0, tiled=True)  12.6 us
    ppermute x1, waiting for transfers between devices, shards(): near = lax.ppermute(mine, 'y', NEAR)  10 us
    pallas_call x1, Pallas kernels, pack(): pl.pallas_call(pack_kernel, out_shape=jax.ShapeDtypeStruct((DESTS, PART,...  7.18 us
    ppermute x1, starting transfers between devices, shards(): got = lax.ppermute(send, 'c', SWAP)  6.97 us
    ppermute x1, starting transfers between devices, shards(): far_got = lax.ppermute(far[1], 'c', SWAP)  4.63 us
    ppermute x1, waiting for transfers between devices, shards(): wrap = lax.ppermute(mine, 'y', WRAP)  4.15 us
    ppermute x1, starting transfers between devices, shards(): wrap = lax.ppermute(mine, 'y', WRAP)  3.8 us
  transfers between devices with their start and end apart: 6, of which 3 were waited for; matrix products, arithmetic and copies ran while one was open for 0% of the time, Pallas kernels for 3%

profile of v11, /device:TPU:1, one launch (start us, length us, event | category | flops | bytes accessed | tf_op | source)
XLA Modules:
  0.0 123.5 jit_solution(3185967166012353931)
XLA Ops:
  0.0 7.2 %pack.1 = bf16[64,48,128]{2,1,0:T(8,128)(2,1)S(1)} custom-call(f32[16,64]{1,0:T(8,128)} %bitcast.15, s32[1,64]{1,0:T(1,128)} %bitcast.16, s32[64,128]{1,0:T(8,128)} %bitcast.14, bf16[16,8192]{1,0:T(8,128)(2,1)} %eigen_hbm.1, bf16[64,8192]{1,0:T(8,128)(2,1)} %raw_hbm.1), custom_call_target="tpu_custom_call" | custom-call | tf_op jit(solution)/shard_map/pack/pallas_call | solution.py:117
  7.2 58.8 %all_to_all.10 = bf16[64,48,128]{2,1,0:T(8,128)(2,1)S(1)} all-to-all(bf16[64,48,128]{2,1,0:T(8,128)(2,1)S(1)} %pack.1), channel_id=1, replica_groups=mesh['z'=16,'c'=2,'y'=4,'x'=4] {'x','z'}, dimensions={0} | all-to-all | bytes 1572864 | tf_op jit(solution)/shard_map/all_to_all | solution.py:301
  66.0 3.2 %collective-permute-start = (bf16[3072,128]{1,0:T(8,128)(2,1)S(1)}, bf16[3072,128]{1,0:T(8,128)(2,1)S(1)}, u32[]{:S(2)}, u32[]{:S(2)}) collective-permute-start(bf16[3072,128]{1,0:T(8,128)(2,1)S(1)} %bitcast.11), channel_id=1, source_target_pairs={{0,4},{4,0},{8,12},{12,8},{1,5},{5,1},{9,13},{13,9},{2,6},{6,2},{1... | collective-permute-start | bytes 2359304 | tf_op jit(solution)/shard_map/ppermute | solution.py:302
  69.2 3.8 %collective-permute-start.1 = (bf16[3072,128]{1,0:T(8,128)(2,1)S(1)}, bf16[3072,128]{1,0:T(8,128)(2,1)S(1)}, u32[]{:S(2)}, u32[]{:S(2)}) collective-permute-start(bf16[3072,128]{1,0:T(8,128)(2,1)S(1)} %bitcast.12), channel_id=1, source_target_pairs={{0,12},{4,8},{8,4},{12,0},{1,13},{5,9},{9,5},{13,1},{2,14},{6,10},... | collective-permute-start | bytes 2359304 | tf_op jit(solution)/shard_map/ppermute | solution.py:303
  73.0 10.0 %collective-permute-done.near_ref = bf16[3072,128]{1,0:T(8,128)(2,1)S(1)} collective-permute-done((bf16[3072,128]{1,0:T(8,128)(2,1)S(1)}, bf16[3072,128]{1,0:T(8,128)(2,1)S(1)}, u32[]{:S(2)}, u32[]{:S(2)}) %collective-permute-start) | collective-permute-done | bytes 786464 | tf_op jit(solution)/shard_map/ppermute | solution.py:302
  83.1 4.1 %collective-permute-done.1.wrap_ref = bf16[3072,128]{1,0:T(8,128)(2,1)S(1)} collective-permute-done((bf16[3072,128]{1,0:T(8,128)(2,1)S(1)}, bf16[3072,128]{1,0:T(8,128)(2,1)S(1)}, u32[]{:S(2)}, u32[]{:S(2)}) %collective-permute-start.1) | collective-permute-done | bytes 786464 | tf_op jit(solution)/shard_map/ppermute | solution.py:303
  87.2 0.7 cross.1
  88.0 1.9 %collective-permute-start.3 = (f32[2,136,256]{2,1,0:T(8,128)S(1)}, f32[2,136,256]{2,1,0:T(8,128)S(1)}, u32[]{:S(2)}, u32[]{:S(2)}) collective-permute-start(f32[2,136,256]{2,1,0:T(8,128)S(1)} %cross.1), channel_id=1, source_target_pairs={{0,4},{4,0},{8,12},{12,8},{1,5},{5,1},{9,13},{13,9},{2,6},{6,2},{1... | collective-permute-start | bytes 835592 | tf_op jit(solution)/shard_map/ppermute | solution.py:304
  89.9 1.9 %gram.1 = (f32[4,32,768]{2,1,0:T(8,128)S(1)}, f32[144,768]{1,0:T(8,128)S(1)}, f32[16,768]{1,0:T(8,128)S(1)}) custom-call(s32[1]{0:T(128)} %bitcast.core_ref, bf16[3072,128]{1,0:T(8,128)(2,1)S(1)} %bitcast.13, bf16[3072,128]{1,0:T(8,128)(2,1)S(1)} %collective-permute-done.near_ref, bf16[3072,128]{1,0:T(8,128)(2,1)S(1)} %collective-permute-done.1.wrap_ref), custom_call_target="tpu_custom_call" | custom-call | tf_op jit(solution)/shard_map/gram/pallas_call | solution.py:215
  91.7 7.0 %collective-permute-start.2 = (f32[144,768]{1,0:T(8,128)S(1)}, f32[144,768]{1,0:T(8,128)S(1)}, u32[]{:S(2)}, u32[]{:S(2)}) collective-permute-start(f32[144,768]{1,0:T(8,128)S(1)} %get-tuple-element.12), channel_id=1, source_target_pairs={{0,16},{16,0},{1,17},{17,1},{2,18},{18,2},{3,19},{19,3},{4,20},{20... | collective-permute-start | bytes 1327112 | tf_op jit(solution)/shard_map/ppermute | solution.py:306
  98.7 0.0 collective-permute-done.3.far_ref
  98.8 4.6 %collective-permute-start.4 = (f32[136,256]{1,0:T(8,128)S(1)}, f32[136,256]{1,0:T(8,128)S(1)}, u32[]{:S(2)}, u32[]{:S(2)}) collective-permute-start(f32[136,256]{1,0:T(8,128)S(1)} %slice_bitcast_fusion), channel_id=1, source_target_pairs={{0,16},{16,0},{1,17},{17,1},{2,18},{18,2},{3,19},{19,3},{4,20},{20... | collective-permute-start | bytes 417800 | tf_op jit(solution)/shard_map/ppermute | solution.py:307
  103.4 0.1 stack.23.at_ref
  103.5 0.9 collective-permute-done.4.far_got_ref
  104.4 0.0 collective-permute-done.2.got_ref
  104.4 0.2 scale.1
  104.5 12.6 %all_to_all.11.rows_ref = f32[4,32,1024]{2,1,0:T(8,128)S(1)} all-to-all(f32[4,32,1024]{2,1,0:T(8,128)S(1)} %scale.1), channel_id=1, replica_groups=mesh['z'=16,'c'=2,'y'=4,'x'=4] {'x'}, dimensions={0} | all-to-all | bytes 1048576 | tf_op jit(solution)/shard_map/all_to_all | solution.py:311
  117.1 3.7 %collective-permute-start.5 = (f32[2,32,1024]{2,1,0:T(8,128)S(1)}, f32[2,32,1024]{2,1,0:T(8,128)S(1)}, u32[]{:S(2)}, u32[]{:S(2)}) collective-permute-start(f32[2,32,1024]{2,1,0:T(8,128)S(1)} %constant_dynamic-slice_fusion), channel_id=1, source_target_pairs={{0,16},{16,0},{1,17},{17,1},{2,18},{18,2},{3,19},{19,3},{4,20},{20... | collective-permute-start | bytes 786440 | tf_op jit(solution)/shard_map/ppermute | solution.py:312
  120.9 1.3 %own_rows.1.half_ref = f32[2,64,1024]{2,1,0:T(8,128)} custom-call(s32[5]{0:T(128)S(1)} %stack.23.at_ref, f32[4,32,1024]{2,1,0:T(8,128)S(1)} %all_to_all.11.rows_ref), custom_call_target="tpu_custom_call" | custom-call | tf_op jit(solution)/shard_map/own_rows/pallas_call | solution.py:285
  122.2 0.0 collective-permute-done.5.swap_ref
  122.2 1.3 %other_rows.1 = f32[2,64,1024]{2,1,0:T(8,128)} custom-call(s32[5]{0:T(128)S(1)} %stack.23.at_ref, f32[2,32,1024]{2,1,0:T(8,128)S(1)} %collective-permute-done.5.swap_ref, f32[2,64,1024]{2,1,0:T(8,128)} %own_rows.1.half_ref), custom_call_target="tpu_custom_call", output_to_operand_aliasing={{}: (2, {})} | custom-call | tf_op jit(solution)/shard_map/other_rows/pallas_call | solution.py:287
  (2 shorter events, 0.0 us)
Async XLA Ops:
  66.0 17.0 %collective-permute-start = (bf16[3072,128]{1,0:T(8,128)(2,1)S(1)}, bf16[3072,128]{1,0:T(8,128)(2,1)S(1)}, u32[]{:S(2)}, u32[]{:S(2)}) collective-permute-start(bf16[3072,128]{1,0:T(8,128)(2,1)S(1)} %bitcast.11), channel_id=1, source_target_pairs={{0,4},{4,0},{8,12},{12,8},{1,5},{5,1},{9,13},{13,9},{2,6},{6,2},{1... | collective-permute-start | bytes 2359304 | tf_op jit(solution)/shard_map/ppermute | solution.py:302
  69.2 18.0 %collective-permute-start.1 = (bf16[3072,128]{1,0:T(8,128)(2,1)S(1)}, bf16[3072,128]{1,0:T(8,128)(2,1)S(1)}, u32[]{:S(2)}, u32[]{:S(2)}) collective-permute-start(bf16[3072,128]{1,0:T(8,128)(2,1)S(1)} %bitcast.12), channel_id=1, source_target_pairs={{0,12},{4,8},{8,4},{12,0},{1,13},{5,9},{9,5},{13,1},{2,14},{6,10},... | collective-permute-start | bytes 2359304 | tf_op jit(solution)/shard_map/ppermute | solution.py:303
  88.0 10.8 %collective-permute-start.3 = (f32[2,136,256]{2,1,0:T(8,128)S(1)}, f32[2,136,256]{2,1,0:T(8,128)S(1)}, u32[]{:S(2)}, u32[]{:S(2)}) collective-permute-start(f32[2,136,256]{2,1,0:T(8,128)S(1)} %cross.1), channel_id=1, source_target_pairs={{0,4},{4,0},{8,12},{12,8},{1,5},{5,1},{9,13},{13,9},{2,6},{6,2},{1... | collective-permute-start | bytes 835592 | tf_op jit(solution)/shard_map/ppermute | solution.py:304
  91.7 12.6 %collective-permute-start.2 = (f32[144,768]{1,0:T(8,128)S(1)}, f32[144,768]{1,0:T(8,128)S(1)}, u32[]{:S(2)}, u32[]{:S(2)}) collective-permute-start(f32[144,768]{1,0:T(8,128)S(1)} %get-tuple-element.12), channel_id=1, source_target_pairs={{0,16},{16,0},{1,17},{17,1},{2,18},{18,2},{3,19},{19,3},{4,20},{20... | collective-permute-start | bytes 1327112 | tf_op jit(solution)/shard_map/ppermute | solution.py:306
  98.8 5.6 %collective-permute-start.4 = (f32[136,256]{1,0:T(8,128)S(1)}, f32[136,256]{1,0:T(8,128)S(1)}, u32[]{:S(2)}, u32[]{:S(2)}) collective-permute-start(f32[136,256]{1,0:T(8,128)S(1)} %slice_bitcast_fusion), channel_id=1, source_target_pairs={{0,16},{16,0},{1,17},{17,1},{2,18},{18,2},{3,19},{19,3},{4,20},{20... | collective-permute-start | bytes 417800 | tf_op jit(solution)/shard_map/ppermute | solution.py:307
  117.1 5.0 %collective-permute-start.5 = (f32[2,32,1024]{2,1,0:T(8,128)S(1)}, f32[2,32,1024]{2,1,0:T(8,128)S(1)}, u32[]{:S(2)}, u32[]{:S(2)}) collective-permute-start(f32[2,32,1024]{2,1,0:T(8,128)S(1)} %constant_dynamic-slice_fusion), channel_id=1, source_target_pairs={{0,16},{16,0},{1,17},{17,1},{2,18},{18,2},{3,19},{19,3},{4,20},{20... | collective-permute-start | bytes 786440 | tf_op jit(solution)/shard_map/ppermute | solution.py:312
